TPU v7x, 256 devices: a whole 4x4x8 slice. The times are simulated.
256 devices in a mesh: expert: 8 (over y, core), shard: 32 (over z, x).
Axes of the slice: x: 4, y: 4, z: 8, core: 2. Of those that a mesh axis runs over, the one named last changes fastest.
Arguments:
- activations: bfloat16 [8, 32, 96, 2048], P('expert', 'shard'), may hold values from -6 to 6
- out_grads: bfloat16 [8, 32, 96, 7168], P('expert', 'shard'), may hold values from -6 to 6
- next_inputs: bfloat16 [8, 32, 96, 2048], P('expert', 'shard'), may hold values from -6 to 6
- counts: int32 [8, 32], P('expert', 'shard'), may hold values from 1 to 96, as said below
- master: float32 [8, 32, 512, 896], P('expert', 'shard'), may hold values from -0.125 to 0.125
- moment: bfloat16 [8, 32, 512, 896], P('expert', 'shard'), may hold values from -6 to 6
- second: bfloat16 [8, 32, 512, 896], P('expert', 'shard'), may hold values from 0.099609375 to 4
Outputs:
- master_new: float32 [8, 32, 512, 896], P('expert', 'shard')
- moment_new: bfloat16 [8, 32, 512, 896], P('expert', 'shard')
- second_new: bfloat16 [8, 32, 512, 896], P('expert', 'shard')
- projected: bfloat16 [8, 32, 96, 7168], P('expert', 'shard')
Inputs may be any that keep to these rules, and one draw needn't show every extreme that they name: counts[e, s] of the 96 slots of expert e from shard s hold tokens, the leading ones; the rest are padding.
All inputs are finite; a program needn't handle non-finite values.
Results may differ from a plain program's by a relative error of at most 0.00055.
The roundings to bfloat16 on the way count: a program that leaves them out, or rounds other values in their place, can miss the bound.
Values may be sent and summed in bfloat16 or wider, within the bound.
No kernel may reach another device: no remote copies, remote signals or barrier semaphores. Data moves between devices by JAX's collectives and lax.ppermute only.
A program may use at most 192 MiB of HBM per device.

v0:
```python
import functools

import jax
import jax.numpy as jnp
from jax import lax
from jax.sharding import Mesh
from jax.sharding import PartitionSpec as P

D = 2048
FF = 7168
SHARD = ("shard_0", "shard_1")
EXPERT = ("expert_0", "expert_1")
EXPERT_SHARD = ("expert_0", "expert_1", "shard_0", "shard_1")


def sent_together(arrays, axis, split_dim, concat_dim, along):
    both = jnp.concatenate(arrays, axis=along)
    filled, at, done = (
        lax.all_to_all(both, axis, split_axis=split_dim, concat_axis=concat_dim, tiled=True),
        0,
        [],
    )
    for a in arrays:
        done.append(lax.slice_in_dim(filled, at, at + a.shape[along], axis=along))
        at += a.shape[along]
    return tuple(done)


def over_axes(shard, axes):
    return functools.reduce(lax.psum, axes, shard)


def from_everyone(shard, axis):
    size = lax.axis_size(axis)
    return lax.all_to_all(
        jnp.broadcast_to(shard[None], (size, *shard.shape)), axis, 0, 0, tiled=True
    )


def over_copies(shard, axis):
    everything = from_everyone(shard, axis)
    return jnp.sum(everything, axis=0)


def together(arrays, axis):
    ends = [0]
    for a in arrays:
        ends.append(ends[-1] + a.size)
    subtotal = over_copies(jnp.concatenate([a.ravel() for a in arrays]), axis)
    return tuple((subtotal[b:e].reshape(a.shape) for a, b, e in zip(arrays, ends, ends[1:])))


def spread_rows(matrix, grid_r, grid_c, stride):
    capacity = matrix.shape[0]
    blocks = matrix.reshape(capacity, grid_r, stride).transpose(1, 0, 2)
    blocks = jnp.broadcast_to(blocks[:, None], (grid_r, grid_c, capacity, stride))
    return blocks.reshape(grid_r * grid_c, capacity, stride)


def spread_cols(matrix, grid_r, grid_c, stride):
    capacity = matrix.shape[0]
    blocks = matrix.reshape(capacity, grid_c, stride).transpose(1, 0, 2)
    blocks = jnp.broadcast_to(blocks[None], (grid_r, grid_c, capacity, stride))
    return blocks.reshape(grid_r * grid_c, capacity, stride)


def body(activations, out_grads, next_inputs, counts, master, moment, second):
    capacity = activations.shape[2]
    d_blk = master.shape[2]
    f_blk = master.shape[3]
    grid_r = D // d_blk
    grid_c = FF // f_blk
    valid = lax.iota(jnp.int32, capacity) < counts[0, 0]
    masked = jnp.where(valid[:, None], out_grads[0, 0], jnp.zeros((), jnp.bfloat16))
    send_rows = spread_rows(activations[0, 0], grid_r, grid_c, d_blk)
    send_cols = spread_cols(masked, grid_r, grid_c, f_blk)
    got_rows, got_cols = sent_together((send_rows, send_cols), SHARD, 0, 0, 2)
    gradient = jnp.einsum("sci,scj->ij", got_rows, got_cols, preferred_element_type=jnp.float32)
    weights = master[0, 0]
    first = moment[0, 0].astype(jnp.float32)
    later = second[0, 0].astype(jnp.float32)
    experts = lax.axis_size(EXPERT) * master.shape[0]
    entries = float(experts * D * FF)
    grad_sq = jnp.sum(gradient * gradient)
    weight_local = jnp.sum(weights * weights)
    norm_total = over_axes(grad_sq, EXPERT_SHARD)
    grad_rms = jnp.sqrt(norm_total / entries + 1e-06)
    clip_factor = jnp.minimum(1.0, 1.0 / grad_rms)
    clipped = clip_factor * gradient
    first_new = 0.9 * first + 0.1 * clipped
    later_new = 0.999 * later + 0.001 * clipped * clipped
    update = (
        first_new / (1.0 - 0.9**10) / (jnp.sqrt(later_new / (1.0 - 0.999**10)) + 1e-06)
        + 0.01 * weights
    )
    update_local = jnp.sum(update * update)
    weight_sq, update_sq = together((weight_local, update_local), SHARD)
    trust_ratio = jnp.sqrt(weight_sq) / (jnp.sqrt(update_sq) + 1e-06)
    weights_new = weights - 0.08 * trust_ratio * update
    rounded = weights_new.astype(jnp.bfloat16)
    inputs_next = next_inputs[0, 0]
    empty = jnp.zeros((capacity, FF), jnp.float32)
    pieces = lax.all_gather(rounded[None], SHARD, axis=0, tiled=True)

    def add_one(tile_index, current):
        tile = lax.dynamic_index_in_dim(pieces, tile_index, 0, keepdims=False)
        row_start = tile_index // grid_c * d_blk
        col_start = tile_index % grid_c * f_blk
        columns = lax.dynamic_slice_in_dim(inputs_next, row_start, d_blk, 1)
        partial_value = jnp.dot(columns, tile, preferred_element_type=jnp.float32)
        before = lax.dynamic_slice_in_dim(current, col_start, f_blk, 1)
        return lax.dynamic_update_slice_in_dim(current, before + partial_value, col_start, 1)

    summed = lax.fori_loop(0, pieces.shape[0], add_one, empty)
    projected = summed.astype(jnp.bfloat16)
    moment_out = first_new.astype(jnp.bfloat16)
    second_out = later_new.astype(jnp.bfloat16)
    return (
        weights_new[None, None],
        moment_out[None, None],
        second_out[None, None],
        projected[None, None],
    )


def solution(mesh):
    finer = Mesh(mesh.devices.reshape(4, 2, 8, 4), ("expert_0", "expert_1", "shard_0", "shard_1"))
    placed = (
        P(EXPERT, SHARD, None, None),
        P(EXPERT, SHARD, None, None),
        P(EXPERT, SHARD, None, None),
        P(EXPERT, SHARD),
        P(EXPERT, SHARD, None, None),
        P(EXPERT, SHARD, None, None),
        P(EXPERT, SHARD, None, None),
    )
    return jax.shard_map(
        body,
        mesh=finer,
        in_specs=placed,
        out_specs=(
            P(EXPERT, SHARD, None, None),
            P(EXPERT, SHARD, None, None),
            P(EXPERT, SHARD, None, None),
            P(EXPERT, SHARD, None, None),
        ),
        check_vma=False,
    )
```

profile of v0, /device:TPU:1, one launch (start us, length us, event | category | flops | bytes accessed | tf_op | source)
XLA Modules:
  0.0 558.3 jit_solution(14726423744017282262)
XLA Ops:
  7.2 1.6 copy.21
  11.1 3.0 broadcast_in_dim.52
  14.4 6.6 %pad_maximum_fusion = bf16[32,96,1408]{2,1,0:T(8,128)(2,1)} fusion(bf16[32,96,896]{2,1,0:T(8,128)(2,1)} %bitcast.80, bf16[32,96,512]{2,1,0:T(8,128)(2,1)S(1)} %bitcast.81), kind=kLoop, calls=%fused_computation.6 | loop fusion | flops 17301504 | bytes 17301504 | tf_op jit(solution)/shard_map/concatenate | solution.py:17
  21.0 203.0 %all_to_all.11 = bf16[32,96,1408]{2,1,0:T(8,128)(2,1)S(1)} all-to-all(bf16[32,96,1408]{2,1,0:T(8,128)(2,1)} %pad_maximum_fusion), channel_id=1, replica_groups=mesh['expert_0'=4,'expert_1'=2,'shard_0'=8,'shard_1'=4] {'shard_0','shar..., dimensions={0} | all-to-all | bytes 17301504 | tf_op jit(solution)/shard_map/all_to_all | solution.py:19
  224.0 5.3 fusion.9
  229.2 9.3 %psum.28 = f32[]{:T(128)} all-reduce(f32[]{:T(128)} %get-tuple-element.135), channel_id=1, replica_groups=mesh['expert_0'=4,'expert_1'=2,'shard_0'=8,'shard_1'=4] {'expert_0'}, use_global_device_ids=true, to_apply=%region_2.3 | all-reduce | flops 1 | bytes 8 | tf_op jit(solution)/shard_map/psum | solution.py:30
  238.5 7.1 %psum.29 = f32[]{:T(128)} all-reduce(f32[]{:T(128)} %psum.28), channel_id=1, replica_groups=mesh['expert_0'=4,'expert_1'=2,'shard_0'=8,'shard_1'=4] {'expert_1'}, use_global_device_ids=true, to_apply=%region_3.4 | all-reduce | flops 1 | bytes 8 | tf_op jit(solution)/shard_map/psum | solution.py:30
  245.7 12.3 %psum.30 = f32[]{:T(128)} all-reduce(f32[]{:T(128)} %psum.29), channel_id=1, replica_groups=mesh['expert_0'=4,'expert_1'=2,'shard_0'=8,'shard_1'=4] {'shard_0'}, use_global_device_ids=true, to_apply=%region_4.5 | all-reduce | flops 1 | bytes 8 | tf_op jit(solution)/shard_map/psum | solution.py:30
  257.9 7.4 %psum.31 = f32[]{:T(128)} all-reduce(f32[]{:T(128)} %psum.30), channel_id=1, replica_groups=mesh['expert_0'=4,'expert_1'=2,'shard_0'=8,'shard_1'=4] {'shard_1'}, use_global_device_ids=true, to_apply=%region_5.6 | all-reduce | flops 1 | bytes 8 | tf_op jit(solution)/shard_map/psum | solution.py:30
  266.1 5.8 %multiply_reduce_fusion = (f32[]{:T(128)}, f32[512,896]{1,0:T(8,128)}, bf16[1,1,512,896]{3,2,1,0:T(8,128)(2,1)}, bf16[1,1,512,896]{3,2,1,0:T(8,128)(2,1)}, f32[]{:T(128)}) fusion(f32[1,1,512,896]{3,2,1,0:T(8,128)S(1)} %copy-done, bf16[1,1,512,896]{3,2,1,0:T(8,128)(2,1)S(1)} %copy-done.1, f32[512,896,1]{1,0,2:T(8,128)} %get-tuple-element.136, f32[]{:T(128)S(6)} %min.3, ...), kind=kLoop, calls=%fused_computation.21 | loop fusion | flops 10092542 | bytes 9175052 | tf_op jit(solution)/shard_map/reduce_sum | solution.py:96
  271.9 1.4 pad_maximum_fusion.1
  273.3 13.2 %all_to_all.12 = f32[32,1,2]{2,1,0:T(1,128)S(1)} all-to-all(f32[32,1,2]{2,1,0:T(1,128)S(1)} %broadcast_in_dim.53), channel_id=1, replica_groups=mesh['expert_0'=4,'expert_1'=2,'shard_0'=8,'shard_1'=4] {'shard_0','shar..., dimensions={0} | all-to-all | bytes 512 | tf_op jit(solution)/shard_map/all_to_all | solution.py:35
  288.6 3.3 fusion.14
  291.9 207.4 %all-gather.3.cloned.1.call-done = bf16[16384,896]{1,0:T(8,128)(2,1)} async-done(((bf16[512,896]{1,0:T(8,128)(2,1)}), bf16[16384,896]{1,0:T(8,128)(2,1)}) %all-gather.3.cloned.1.call-update) | async-done | bytes 29360144 | tf_op jit(solution)/shard_map/all_gather | solution.py:103
  499.5 50.7 %while.15 = (s32[]{:T(128)}, f32[96,7168]{1,0:T(8,128)S(1)}, bf16[96,2048]{1,0:T(8,128)(2,1)}, bf16[32,512,896]{2,1,0:T(8,128)(2,1)}, s32[]{:T(128)}, /*index=5*...) while((s32[]{:T(128)}, f32[96,7168]{1,0:T(8,128)S(1)}, ...), condition=%wide.region_9.10_spmd, body=%wide.region_8.9_spmd.sunk | while | flops 88166424 | bytes 1704796 | solution.py:114
  499.5 1.5 fusion.23
  501.1 1.5 fusion.23
  502.7 1.5 fusion.23
  504.3 1.5 fusion.23
  505.9 1.5 fusion.23
  507.5 1.5 fusion.23
  509.0 1.5 fusion.23
  510.6 1.5 fusion.23
  512.2 1.5 fusion.23
  513.8 1.5 fusion.23
  515.4 1.5 fusion.23
  517.0 1.5 fusion.23
  518.5 1.5 fusion.23
  520.1 1.5 fusion.23
  521.7 1.5 fusion.23
  523.3 1.5 fusion.23
  524.9 1.5 fusion.23
  526.5 1.5 fusion.23
  528.0 1.5 fusion.23
  529.6 1.5 fusion.23
  531.2 1.5 fusion.23
  532.8 1.5 fusion.23
  534.4 1.5 fusion.23
  535.9 1.5 fusion.23
  537.5 1.5 fusion.23
  539.1 1.5 fusion.23
  540.7 1.5 fusion.23
  542.3 1.5 fusion.23
  543.9 1.5 fusion.23
  545.4 1.5 fusion.23
  547.0 1.5 fusion.23
  548.6 1.5 fusion.23
  550.2 1.2 convert_bitcast_fusion
  (18 shorter events, 2.9 us)
Async XLA Ops:
  7.2 492.1 %all-gather.3.cloned.1.call-start = ((), (), s32[]{:S(2)}) async-start(), calls=%async_computation.2 | async-start | bytes 30277632 | tf_op jit(solution)/shard_map/all_gather | solution.py:103
  9.7 1.0 copy-start.2
  223.9 42.1 %copy-start = (f32[1,1,512,896]{3,2,1,0:T(8,128)S(1)}, f32[1,1,512,896]{3,2,1,0:T(8,128)}, u32[]{:S(2)}) copy-start(f32[1,1,512,896]{3,2,1,0:T(8,128)} %param.13) | copy-start | bytes 5505028
  223.9 42.1 %copy-start.1 = (bf16[1,1,512,896]{3,2,1,0:T(8,128)(2,1)S(1)}, bf16[1,1,512,896]{3,2,1,0:T(8,128)(2,1)}, u32[]{:S(2)}) copy-start(bf16[1,1,512,896]{3,2,1,0:T(8,128)(2,1)} %param.15) | copy-start | bytes 2752516
Sparse Core Ops, SparseCore 0:
  292.0 207.2 all-gather.2
where the time goes:
time: 560 us; the launch traced here: 558 us
  blocking collectives  252 us (45%)
  waiting for transfers between devices  207 us (37%)
  matrix products  54.7 us (10%)
  other arithmetic  18.6 us (3%)
  between operations  16.9 us (3%)
  local copies, waits for them, and re-layouts  7.05 us (1%)
    all_gather x1, waiting for transfers between devices, body(): pieces = lax.all_gather(rounded[None], SHARD, axis=0, tiled=True)  207 us
    all_to_all x1, blocking collectives, sent_together(): lax.all_to_all(both, axis, split_axis=split_dim, concat_axis=concat_dim,...  203 us
    dot_general x32, matrix products, add_one(): partial_value = jnp.dot(columns, tile, preferred_element_type=jnp.float32)  49.4 us
    psum x4, blocking collectives, over_axes(): return functools.reduce(lax.psum, axes, shard)  36.1 us
    all_to_all x1, blocking collectives, from_everyone(): lax.all_to_all(jnp.broadcast_to(shard[None], (size, *shard.shape)), axis,...  13.2 us
  transfers between devices with their start and end apart: 1, of which 1 were waited for; matrix products, arithmetic and copies ran while one was open for 0% of the time, Pallas kernels for 0%

commit v1 on v0

v1 whole, which is shorter than its diff:
```python
import functools

import jax
import jax.numpy as jnp
from jax import lax
from jax.experimental import pallas as pl
from jax.experimental.pallas import tpu as pltpu
from jax.sharding import Mesh
from jax.sharding import PartitionSpec as P

GRID_R = 4
GRID_C = 8
EXPERT = ("y", "k")
SHARD = ("z", "x")
EVERYONE = ("y", "k", "z", "x")


def totals(values, axes):
    size = lax.axis_size(axes)
    mine = jnp.stack(values)
    sent = jnp.broadcast_to(mine[None, None], (size, 1, len(values)))
    got = lax.all_to_all(sent, axes, 0, 0, tiled=True)
    return jnp.sum(got, axis=(0, 1))


def project(tokens, tiles):
    count, _ = tokens.shape
    grid_r, parities, d_blk, f_blk = tiles.shape

    def kernel(x_ref, w_ref, o_ref, acc_ref):
        step = pl.program_id(1)
        partial = jnp.dot(x_ref[...], w_ref[0, 0], preferred_element_type=jnp.float32)

        @pl.when(step == 0)
        def _():
            acc_ref[...] = partial

        @pl.when(step > 0)
        def _():
            acc_ref[...] += partial

        @pl.when(step == grid_r - 1)
        def _():
            o_ref[0] = acc_ref[...].astype(o_ref.dtype)

    return pl.pallas_call(
        kernel,
        grid=(parities, grid_r),
        in_specs=[
            pl.BlockSpec((count, d_blk), lambda p, r: (0, r)),
            pl.BlockSpec((1, 1, d_blk, f_blk), lambda p, r: (r, p, 0, 0)),
        ],
        out_specs=pl.BlockSpec((1, count, f_blk), lambda p, r: (p, 0, 0)),
        out_shape=jax.ShapeDtypeStruct((parities, count, f_blk), jnp.bfloat16),
        scratch_shapes=[pltpu.VMEM((count, f_blk), jnp.float32)],
        name="project",
    )(tokens, tiles)


def body(activations, out_grads, next_inputs, counts, master, moment, second):
    cap, d = activations.shape[2:]
    ff = out_grads.shape[3]
    d_blk, f_blk = master.shape[2:]
    size_z, size_x = lax.axis_size("z"), lax.axis_size("x")
    parities = GRID_C // size_x
    parity = lax.axis_index("z") % parities

    valid = lax.iota(jnp.int32, cap) < counts[0, 0]
    masked = jnp.where(valid[:, None], out_grads[0, 0], jnp.zeros((), jnp.bfloat16))
    cols = masked.reshape(cap, parities, size_x, f_blk).transpose(2, 1, 0, 3)
    cols = lax.all_to_all(cols, "x", 0, 0, tiled=True)
    cols = lax.all_gather(cols.transpose(1, 0, 2, 3), "z")
    cols = lax.dynamic_index_in_dim(cols, parity, 1, keepdims=False)

    rows = activations[0, 0].reshape(cap, GRID_R, d_blk).transpose(1, 0, 2)
    rows = jnp.repeat(rows, size_z // GRID_R, axis=0)
    rows = lax.all_to_all(rows, "z", 0, 0, tiled=True)
    rows = lax.all_gather(rows, "x")

    gradient = jnp.einsum("xzci,zxcj->ij", rows, cols, preferred_element_type=jnp.float32)

    tokens = lax.all_gather(next_inputs[0, 0], "x").reshape(size_x * cap, d)

    weights = master[0, 0]
    first = moment[0, 0].astype(jnp.float32)
    later = second[0, 0].astype(jnp.float32)
    entries = float(lax.axis_size(EXPERT) * d * ff)
    (norm_total,) = totals([jnp.sum(gradient * gradient)], EVERYONE)
    grad_rms = jnp.sqrt(norm_total / entries + 1e-06)
    clip_factor = jnp.minimum(1.0, 1.0 / grad_rms)
    clipped = clip_factor * gradient
    first_new = 0.9 * first + 0.1 * clipped
    later_new = 0.999 * later + 0.001 * clipped * clipped
    update = (
        first_new / (1.0 - 0.9**10) / (jnp.sqrt(later_new / (1.0 - 0.999**10)) + 1e-06)
        + 0.01 * weights
    )
    weight_sq, update_sq = totals([jnp.sum(weights * weights), jnp.sum(update * update)], SHARD)
    trust_ratio = jnp.sqrt(weight_sq) / (jnp.sqrt(update_sq) + 1e-06)
    weights_new = weights - 0.08 * trust_ratio * update

    tiles = lax.all_gather(weights_new.astype(jnp.bfloat16), "z")
    tiles = tiles.reshape(GRID_R, parities, d_blk, f_blk)
    found = project(tokens, tiles).reshape(parities, size_x, cap, f_blk)
    found = lax.all_to_all(found, "x", 1, 1, tiled=True)
    projected = found.transpose(2, 0, 1, 3).reshape(cap, ff)
    return (
        weights_new[None, None],
        first_new.astype(jnp.bfloat16)[None, None],
        later_new.astype(jnp.bfloat16)[None, None],
        projected[None, None],
    )


def solution(mesh):
    finer = Mesh(mesh.devices.reshape(4, 2, 8, 4), EVERYONE)
    tiled = P(EXPERT, SHARD, None, None)
    return jax.shard_map(
        body,
        mesh=finer,
        in_specs=(tiled, tiled, tiled, P(EXPERT, SHARD), tiled, tiled, tiled),
        out_specs=(tiled,) * 4,
        check_vma=False,
    )
```

time: 560 us -> 421 us (0.75)
  blocking collectives: 252 us -> 70.3 us
  matrix products: 54.7 us -> 8.38 us
  waiting for transfers between devices: 207 us -> 253 us
  local copies, waits for them, and re-layouts: 7.05 us -> 34.9 us
  starting transfers between devices: 0.04 us -> 14.4 us
  Pallas kernels: 0 us -> 10.2 us
  other arithmetic: 18.6 us -> 12.3 us
    all_to_all x2 -> x3, blocking collectives: 216 us -> 70.3 us  [the longest x1 30.7 us: body(): rows = lax.all_to_all(rows, 'z', 0, 0, tiled=True)]
    dot_general x33 -> x1, matrix products: 54.7 us -> 8.38 us  [body(): jnp.einsum('xzci,zxcj->ij', rows, cols, preferred_element_type=jnp.float32)]
    psum x4 -> x0, blocking collectives: 36.1 us -> none  [over_axes(): return functools.reduce(lax.psum, axes, shard)]
    all_gather x1 -> x4, waiting for transfers between devices: 207 us -> 234 us  [the longest x1 117 us: body(): cols = lax.all_gather(cols.transpose(1, 0, 2, 3), 'z')]
    all_to_all x0 -> x2, waiting for transfers between devices: none -> 18.8 us  [the longest x1 11.7 us: body(): found = lax.all_to_all(found, 'x', 1, 1, tiled=True)]
    all_to_all x0 -> x2, starting transfers between devices: none -> 14 us  [the longest x1 10.5 us: totals(): got = lax.all_to_all(sent, axes, 0, 0, tiled=True)]
    all_gather x0 -> x1, local copies, waits for them, and re-layouts: none -> 10.8 us  [body(): tiles = lax.all_gather(weights_new.astype(jnp.bfloat16), 'z')]
    pallas_call x0 -> x1, Pallas kernels: none -> 10.2 us  [project(): pl.pallas_call(kernel, grid=(parities, grid_r), in_specs=[pl.BlockSpec((c...]
  transfers between devices with their start and end apart: 1 -> 6, of which waited for: 1 -> 6; matrix products, arithmetic and copies ran while one was open for 0% -> 6% of each run, Pallas kernels for 0% -> 0%
where the time goes in v1:
time: 421 us; the launch traced here: 420 us
  waiting for transfers between devices  253 us (60%)
  blocking collectives  70.3 us (17%)
  local copies, waits for them, and re-layouts  34.9 us (8%)
  between operations  16.7 us (4%)
  starting transfers between devices  14.4 us (3%)
  other arithmetic  12.3 us (3%)
  Pallas kernels  10.2 us (2%)
  matrix products  8.38 us (2%)
    all_gather x1, waiting for transfers between devices, body(): cols = lax.all_gather(cols.transpose(1, 0, 2, 3), 'z')  117 us
    all_gather x1, waiting for transfers between devices, body(): tiles = lax.all_gather(weights_new.astype(jnp.bfloat16), 'z')  79.3 us
    all_to_all x1, blocking collectives, body(): rows = lax.all_to_all(rows, 'z', 0, 0, tiled=True)  30.7 us
    all_to_all x1, blocking collectives, body(): cols = lax.all_to_all(cols, 'x', 0, 0, tiled=True)  27.7 us
    all_gather x1, waiting for transfers between devices, body(): rows = lax.all_gather(rows, 'x')  19.3 us
    all_gather x1, waiting for transfers between devices, body(): tokens = lax.all_gather(next_inputs[0, 0], 'x').reshape(size_x * cap, d)  18.6 us
    all_to_all x1, blocking collectives, totals(): got = lax.all_to_all(sent, axes, 0, 0, tiled=True)  11.9 us
    unnamed x10, local copies, waits for them, and re-layouts  11.7 us
  transfers between devices with their start and end apart: 6, of which 6 were waited for; matrix products, arithmetic and copies ran while one was open for 6% of the time, Pallas kernels for 0%

profile of v1, /device:TPU:1, one launch (start us, length us, event | category | flops | bytes accessed | tf_op | source)
XLA Modules:
  0.0 420.1 jit_solution(7835737069408960485)
XLA Ops:
  7.2 0.0 all-gather.11.cloned.1.call-start
  7.2 1.3 reshape_squeeze.3
  8.5 0.1 copy.97
  8.6 0.0 copy-start.1
  8.6 0.1 broadcast_in_dim.38
  8.7 30.7 %all_to_all.25 = bf16[8,96,512]{2,1,0:T(8,128)(2,1)} all-to-all(bf16[8,96,512]{2,1,0:T(8,128)(2,1)S(1)} %bitcast.106), channel_id=1, replica_groups=mesh['y'=4,'k'=2,'z'=8,'x'=4] {'z'}, dimensions={0} | all-to-all | bytes 1572864 | tf_op jit(solution)/shard_map/all_to_all | solution.py:77
  39.3 0.0 all-gather.11.cloned.1.call-update
  39.3 0.0 all-gather.9.cloned.1.call-start
  39.4 1.1 squeeze.17
  41.1 0.7 select_bitcast_fusion
  41.8 1.1 copy.94
  42.9 27.7 %all_to_all.26 = bf16[4,2,96,896]{3,1,2,0:T(2,128)(2,1)S(1)} all-to-all(bf16[4,2,96,896]{3,1,2,0:T(2,128)(2,1)S(1)} %copy.94), channel_id=1, replica_groups=mesh['y'=4,'k'=2,'z'=8,'x'=4] {'x'}, dimensions={0} | all-to-all | bytes 2752512 | tf_op jit(solution)/shard_map/all_to_all | solution.py:71
  70.6 1.2 copy.95
  71.8 0.0 all-gather.9.cloned.1.call-update
  71.9 19.3 %all-gather.11.cloned.1.call-done = bf16[32,96,512]{2,1,0:T(8,128)(2,1)} async-done(((bf16[8,96,512]{2,1,0:T(8,128)(2,1)}), bf16[32,96,512]{2,1,0:T(8,128)(2,1)}) %all-gather.11.cloned.1.call-update) | async-done | bytes 3145744 | tf_op jit(solution)/shard_map/all_gather | solution.py:78
  91.2 116.7 %all-gather.9.cloned.1.call-done = bf16[16,4,96,896]{3,2,1,0:T(8,128)(2,1)} async-done(((bf16[2,4,96,896]{3,2,1,0:T(8,128)(2,1)}), bf16[16,4,96,896]{3,2,1,0:T(8,128)(2,1)}) %all-gather.9.cloned.1.call-update) | async-done | bytes 11010064 | tf_op jit(solution)/shard_map/all_gather | solution.py:72
  207.9 8.4 %fusion.4 = (f32[]{:T(128)}, f32[896,512,1,1]{1,0,3,2:T(8,128)}) fusion(bf16[4,8,96,512]{3,2,1,0:T(8,128)(2,1)} %bitcast.110, bf16[8,2,4,96,896]{4,3,2,1,0:T(8,128)(2,1)} %bitcast.109, s32[]{:T(128)S(6)} %select_n.18), kind=kOutput, calls=%fused_computation.7 | convolution fusion | flops 2819489792 | bytes 10485768 | tf_op jit(solution)/shard_map/xzci,zxcj->ij/dot_general | solution.py:80
  216.3 1.4 broadcast_in_dim.39
  217.6 10.5 %all-to-all-start.2 = ((f32[256,1,1]{2,1,0:T(1,128)}), f32[256,1,1]{2,1,0:T(1,128)S(1)}, u32[]{:S(2)}, u32[]{:S(2)}) async-start(f32[256,1,1]{2,1,0:T(1,128)} %broadcast_in_dim.39), calls=%async_computation.2 | async-start | bytes 262144 | tf_op jit(solution)/shard_map/all_to_all | solution.py:22
  228.1 0.0 all-gather.15.cloned.1.call-start
  228.2 1.8 copy.92
  230.0 1.5 copy.93
  231.5 2.2 copy.99
  233.7 7.0 %all-to-all-done.2 = f32[256,1,1]{2,1,0:T(1,128)S(1)} async-done(((f32[256,1,1]{2,1,0:T(1,128)}), f32[256,1,1]{2,1,0:T(1,128)S(1)}, u32[]{:S(2)}, u32[]{:S(2)}) %all-to-all-start.2) | async-done | bytes 1056 | tf_op jit(solution)/shard_map/all_to_all | solution.py:22
  240.7 0.9 reduce_sum.47
  242.3 5.9 %multiply_reduce_fusion = (f32[]{:T(128)}, f32[512,896]{0,1:T(8,128)}, bf16[1,1,512,896]{2,3,1,0:T(8,128)(2,1)}, bf16[1,1,512,896]{2,3,1,0:T(8,128)(2,1)}, f32[]{:T(128)}) fusion(f32[1,1,512,896]{2,3,1,0:T(8,128)S(1)} %copy.92, bf16[1,1,512,896]{2,3,1,0:T(8,128)(2,1)} %copy.99, f32[896,512,1,1]{1,0,3,2:T(8,128)} %get-tuple-element.46, f32[]{:T(128)S(6)} %min.3, ...), kind=kLoop, calls=%fused_computation.15 | loop fusion | flops 10092542 | bytes 9175052 | tf_op jit(solution)/shard_map/reduce_sum | solution.py:98
  248.1 1.4 pad_maximum_fusion
  249.5 11.9 %all_to_all.27 = f32[32,1,2]{2,1,0:T(1,128)S(1)} all-to-all(f32[32,1,2]{2,1,0:T(1,128)S(1)} %broadcast_in_dim.40), channel_id=1, replica_groups=mesh['y'=4,'k'=2,'z'=8,'x'=4] {'z','x'}, dimensions={0} | all-to-all | bytes 512 | tf_op jit(solution)/shard_map/all_to_all | solution.py:22
  261.4 0.1 reduce_sum.49
  261.5 0.6 fusion.13
  263.5 3.5 fusion.10
  267.0 0.0 all-gather.15.cloned.1.call-update
  267.0 0.2 all-gather.13.cloned.1.call-start
  267.2 0.3 all-gather.13.cloned.1.call-update
  267.6 79.3 %all-gather.15.cloned.1.call-done = bf16[4096,896]{0,1:T(8,128)(2,1)} async-done(((bf16[512,896]{0,1:T(8,128)(2,1)}), bf16[4096,896]{0,1:T(8,128)(2,1)}) %all-gather.15.cloned.1.call-update) | async-done | bytes 7340048 | tf_op jit(solution)/shard_map/all_gather | solution.py:102
  346.9 10.8 %copy.101 = bf16[4096,896]{1,0:T(8,128)(2,1)} copy(bf16[4096,896]{0,1:T(8,128)(2,1)} %all-gather.15.cloned.1.call-done) | data formatting | bytes 14680064 | tf_op jit(solution)/shard_map/all_gather | solution.py:102
  357.7 18.6 %all-gather.13.cloned.1.call-done = bf16[4,1,96,2048]{3,2,1,0:T(8,128)(2,1)} async-done(((bf16[1,1,96,2048]{3,2,1,0:T(8,128)(2,1)}), bf16[4,1,96,2048]{3,2,1,0:T(8,128)(2,1)}) %all-gather.13.cloned.1.call-update) | async-done | bytes 1572880 | tf_op jit(solution)/shard_map/all_gather | solution.py:82
  376.3 10.2 %project.1 = bf16[2,384,896]{2,1,0:T(8,128)(2,1)} custom-call(bf16[384,2048]{1,0:T(8,128)(2,1)} %bitcast.107, bf16[4,2,512,896]{3,2,1,0:T(8,128)(2,1)} %bitcast.102), custom_call_target="tpu_custom_call" | custom-call | tf_op jit(solution)/shard_map/project/pallas_call | solution.py:46
  386.5 2.6 copy.102
  389.0 3.5 all-to-all-start.4
  392.6 0.0 copy-start
  392.6 2.3 copy.105
  394.9 2.2 copy.106
  397.1 0.0 copy-done
  397.1 1.7 copy.104
  398.8 11.7 %all-to-all-done.4 = bf16[2,4,96,896]{3,2,0,1:T(8,128)(2,1)S(1)} async-done(((bf16[2,4,96,896]{3,2,0,1:T(8,128)(2,1)}), bf16[2,4,96,896]{3,2,0,1:T(8,128)(2,1)S(1)}, u32[]{:S(2)}, u32[]{:S(2)}) %all-to-all-start.4) | async-done | bytes 1376288 | tf_op jit(solution)/shard_map/all_to_all | solution.py:105
  410.5 1.1 copy.103
  411.6 1.9 broadcast_in_dim_reshape.3
  (3 shorter events, 0.0 us)
Async XLA Ops:
  7.2 84.0 %all-gather.11.cloned.1.call-start = ((), (), s32[]{:S(2)}) async-start(), calls=%async_computation.6 | async-start | bytes 3932160 | tf_op jit(solution)/shard_map/all_gather | solution.py:78
  8.6 30.8 %copy-start.1 = (bf16[1,1,96,7168]{3,2,1,0:T(8,128)(2,1)S(1)}, bf16[1,1,96,7168]{3,2,1,0:T(8,128)(2,1)}, u32[]{:S(2)}) copy-start(bf16[1,1,96,7168]{3,2,1,0:T(8,128)(2,1)} %param.8) | copy-start | bytes 4128772
  39.3 168.5 %all-gather.9.cloned.1.call-start = ((), (), s32[]{:S(2)}) async-start(), calls=%async_computation.5 | async-start | bytes 12386304 | tf_op jit(solution)/shard_map/all_gather | solution.py:72
  217.6 23.1 %all-to-all-start.2 = ((f32[256,1,1]{2,1,0:T(1,128)}), f32[256,1,1]{2,1,0:T(1,128)S(1)}, u32[]{:S(2)}, u32[]{:S(2)}) async-start(f32[256,1,1]{2,1,0:T(1,128)} %broadcast_in_dim.39), calls=%async_computation.2 | async-start | bytes 262144 | tf_op jit(solution)/shard_map/all_to_all | solution.py:22
  228.1 118.7 %all-gather.15.cloned.1.call-start = ((), (), s32[]{:S(2)}) async-start(), calls=%async_computation.8 | async-start | bytes 8257536 | tf_op jit(solution)/shard_map/all_gather | solution.py:102
  267.0 109.3 %all-gather.13.cloned.1.call-start = ((), (), s32[]{:S(2)}) async-start(), calls=%async_computation.7 | async-start | bytes 1966080 | tf_op jit(solution)/shard_map/all_gather | solution.py:82
  389.0 21.5 %all-to-all-start.4 = ((bf16[2,4,96,896]{3,2,0,1:T(8,128)(2,1)}), bf16[2,4,96,896]{3,2,0,1:T(8,128)(2,1)S(1)}, u32[]{:S(2)}, u32[]{:S(2)}) async-start(bf16[2,4,96,896]{3,2,0,1:T(8,128)(2,1)} %copy.102), calls=%async_computation.4 | async-start | bytes 2752512 | tf_op jit(solution)/shard_map/all_to_all | solution.py:105
  392.6 4.6 %copy-start = (f32[1,1,512,896]{2,3,1,0:T(8,128)S(1)}, f32[1,1,512,896]{2,3,1,0:T(8,128)}, u32[]{:S(2)}) copy-start(f32[1,1,512,896]{2,3,1,0:T(8,128)} %get-tuple-element.39) | copy-start | bytes 5505028
Sparse Core Ops, SparseCore 0:
  39.5 51.6 all-gather.10
  93.5 114.3 all-gather.8
  267.1 79.7 all-gather.14
  348.5 27.6 all-gather.12

commit v2 on v1

v2 whole, which is shorter than its diff:
```python
import functools

import jax
import jax.numpy as jnp
from jax import lax
from jax.experimental import pallas as pl
from jax.experimental.pallas import tpu as pltpu
from jax.sharding import Mesh
from jax.sharding import PartitionSpec as P

GRID_R = 4
GRID_C = 8
EXPERT = ("y", "k")
SHARD = ("z", "x")
EVERYONE = ("y", "k", "z", "x")


def shift(value, axis, by):
    size = lax.axis_size(axis)
    return lax.ppermute(value, axis, [(i, (i + by) % size) for i in range(size)])


VMEM_LIMIT = 20 << 20
ANYWHERE = pl.BlockSpec(memory_space=pl.ANY)
IN_VMEM = pl.BlockSpec(memory_space=pltpu.VMEM)
IN_SMEM = pl.BlockSpec(memory_space=pltpu.SMEM)


def split(counts, activations, out_grads, d_blk, f_blk):
    cap = activations.shape[0]
    size_x = out_grads.shape[1] // (2 * f_blk)

    def kernel(count_ref, rows_ref, cols_ref, own_ref, other_ref, *row_refs):
        z = lax.axis_index("z")
        q = lax.rem(z, 2)
        valid = lax.broadcasted_iota(jnp.int32, (cap, f_blk), 0) < count_ref[0, 0]
        for i, by in enumerate((0, 1, 3, 2)):
            start = pl.multiple_of(lax.rem(z // 2 + by, GRID_R) * d_blk, 128)
            row_refs[i][...] = rows_ref[:, pl.ds(start, d_blk)]
        for ref, parity in ((own_ref, q), (other_ref, 1 - q)):
            for to_x in range(size_x):
                start = pl.multiple_of((parity * size_x + to_x) * f_blk, 128)
                block = cols_ref[:, pl.ds(start, f_blk)].astype(jnp.float32)
                ref[to_x] = jnp.where(valid, block, 0.0).astype(jnp.bfloat16)

    cols = jax.ShapeDtypeStruct((size_x, cap, f_blk), jnp.bfloat16)
    row = jax.ShapeDtypeStruct((cap, d_blk), jnp.bfloat16)
    return pl.pallas_call(
        kernel,
        in_specs=[IN_SMEM, IN_VMEM, IN_VMEM],
        out_specs=[IN_VMEM] * 6,
        out_shape=[cols] * 2 + [row] * 4,
        compiler_params=pltpu.CompilerParams(vmem_limit_bytes=VMEM_LIMIT),
        name="split",
    )(counts, activations, out_grads)


def fetch(copies, sems):
    started = [pltpu.make_async_copy(src, dst, sems.at[i]) for i, (src, dst) in enumerate(copies)]
    for copy in started:
        copy.start()
    for copy in started:
        copy.wait()


def by_lane(values):
    values = jnp.sum(values, axis=0, keepdims=True)
    return sum(values[:, i : i + 128] for i in range(0, values.shape[1], 128))


def across(values):
    return jnp.sum(jnp.sum(values, axis=0, keepdims=True), axis=1, keepdims=True)


def exchanged(values, axes):
    return lax.all_to_all(values, axes, 0, 0, tiled=True)


def update_of(squares, gradient, master, moment, second, entries):
    d_blk, f_blk = gradient.shape
    steps = 4
    rows = d_blk // steps
    peers = lax.axis_size(SHARD)

    def kernel(n_ref, g_ref, w_ref, m_ref, v_ref, u_ref, m_out, v_out, sums_ref, clip_ref, acc_ref):
        step = pl.program_id(0)

        @pl.when(step == 0)
        def _():
            grad_rms = jnp.sqrt(across(n_ref[:, 0, :]) / entries + 1e-06)
            clip_ref[...] = jnp.broadcast_to(jnp.minimum(1.0, 1.0 / grad_rms), clip_ref.shape)
            acc_ref[...] = jnp.zeros_like(acc_ref)

        weights = w_ref[...]
        clipped = clip_ref[0:1, 0:1] * g_ref[...]
        first_new = 0.9 * m_ref[...].astype(jnp.float32) + 0.1 * clipped
        later_new = 0.999 * v_ref[...].astype(jnp.float32) + 0.001 * clipped * clipped
        update = (
            first_new / (1.0 - 0.9**10) / (jnp.sqrt(later_new / (1.0 - 0.999**10)) + 1e-06)
            + 0.01 * weights
        )
        u_ref[...] = update
        m_out[...] = first_new.astype(jnp.bfloat16)
        v_out[...] = later_new.astype(jnp.bfloat16)
        acc_ref[0:1, :] += by_lane(weights * weights)
        acc_ref[1:2, :] += by_lane(update * update)

        @pl.when(step == steps - 1)
        def _():
            sums_ref[...] = jnp.broadcast_to(acc_ref[0:2, :][None], sums_ref.shape)

    block = pl.BlockSpec((rows, f_blk), lambda i: (i, 0))
    return pl.pallas_call(
        kernel,
        grid=(steps,),
        in_specs=[pl.BlockSpec(squares.shape, lambda i: (0, 0, 0))] + [block] * 4,
        out_specs=[block] * 3 + [pl.BlockSpec((peers, 2, 128), lambda i: (0, 0, 0))],
        out_shape=[
            jax.ShapeDtypeStruct((d_blk, f_blk), jnp.float32),
            jax.ShapeDtypeStruct((d_blk, f_blk), jnp.bfloat16),
            jax.ShapeDtypeStruct((d_blk, f_blk), jnp.bfloat16),
            jax.ShapeDtypeStruct((peers, 2, 128), jnp.float32),
        ],
        scratch_shapes=[pltpu.VMEM((8, 128), jnp.float32), pltpu.VMEM((8, 128), jnp.float32)],
        compiler_params=pltpu.CompilerParams(vmem_limit_bytes=VMEM_LIMIT),
        name="update_of",
    )(squares, gradient, master, moment, second)


def weights_of(sums, update, master):
    d_blk, f_blk = update.shape
    steps = 4
    rows = d_blk // steps

    def kernel(sums_ref, u_ref, w_ref, out_ref, upper_ref, lower_ref, rate_ref):
        step = pl.program_id(0)

        @pl.when(step == 0)
        def _():
            weight_sq = across(sums_ref[:, 0, :])
            update_sq = across(sums_ref[:, 1, :])
            trust_ratio = jnp.sqrt(weight_sq) / (jnp.sqrt(update_sq) + 1e-06)
            rate_ref[...] = jnp.broadcast_to(0.08 * trust_ratio, rate_ref.shape)

        new = w_ref[...] - rate_ref[0:1, 0:1] * u_ref[...]
        out_ref[...] = new

        @pl.when(step < steps // 2)
        def _():
            upper_ref[...] = new.astype(jnp.bfloat16)

        @pl.when(step >= steps // 2)
        def _():
            lower_ref[...] = new.astype(jnp.bfloat16)

    block = pl.BlockSpec((rows, f_blk), lambda i: (i, 0))
    half = jax.ShapeDtypeStruct((d_blk // 2, f_blk), jnp.bfloat16)
    return pl.pallas_call(
        kernel,
        grid=(steps,),
        in_specs=[pl.BlockSpec(sums.shape, lambda i: (0, 0, 0)), block, block],
        out_specs=[
            block,
            pl.BlockSpec((rows, f_blk), lambda i: (jnp.minimum(i, steps // 2 - 1), 0)),
            pl.BlockSpec((rows, f_blk), lambda i: (jnp.maximum(i - steps // 2, 0), 0)),
        ],
        out_shape=[jax.ShapeDtypeStruct((d_blk, f_blk), jnp.float32), half, half],
        scratch_shapes=[pltpu.VMEM((8, 128), jnp.float32)],
        compiler_params=pltpu.CompilerParams(vmem_limit_bytes=VMEM_LIMIT),
        name="weights_of",
    )(sums, update, master)


def outer_sum(rows, places, pieces, before=None, last=False):
    size_x, _, cap, d_blk = rows.shape
    f_blk = pieces[0][0].shape[-1]
    flat = [part for piece in pieces for part in piece]
    depth = size_x * cap
    n = len(pieces)

    def kernel(*refs):
        refs = list(refs)
        rows_ref = refs.pop(0)
        flat_refs = [refs.pop(0) for _ in flat]
        before_ref = refs.pop(0) if before is not None else None
        total_ref = refs.pop(0)
        square_ref = refs.pop(0) if last else None
        left, right, sems = refs
        q = lax.rem(lax.axis_index("z"), 2)
        copies = []
        at = 0
        for i, piece in enumerate(pieces):
            start = 0
            for part in piece:
                size = part.shape[0]
                copies.append((flat_refs[at], right.at[i, pl.ds(start, size)]))
                start += size
                at += 1
            copies.append((rows_ref.at[:, places[i](q)], left.at[i]))
        fetch(copies, sems)
        if before is None:
            total_ref[...] = jnp.zeros_like(total_ref)
        else:
            total_ref[...] = before_ref[...]

        def add(i, carry):
            total_ref[...] += lax.dot_general(
                left[i].reshape(depth, d_blk),
                right[i].reshape(depth, f_blk),
                (((0,), (0,)), ((), ())),
                preferred_element_type=jnp.float32,
            )
            return carry

        lax.fori_loop(0, n, add, 0)
        if last:
            value = total_ref[...]
            square_ref[...] = jnp.broadcast_to(by_lane(value * value)[None], square_ref.shape)

    operands = [rows, *flat]
    in_specs = [ANYWHERE] * len(operands)
    aliases = {}
    if before is not None:
        aliases = {len(operands): 0}
        operands.append(before)
        in_specs.append(IN_VMEM)
    out_shape = [jax.ShapeDtypeStruct((d_blk, f_blk), jnp.float32)]
    if last:
        out_shape.append(jax.ShapeDtypeStruct((lax.axis_size(EVERYONE), 1, 128), jnp.float32))
    return pl.pallas_call(
        kernel,
        in_specs=in_specs,
        out_specs=[IN_VMEM] * len(out_shape),
        out_shape=out_shape,
        scratch_shapes=[
            pltpu.VMEM((n, size_x, cap, d_blk), jnp.bfloat16),
            pltpu.VMEM((n, size_x, cap, f_blk), jnp.bfloat16),
            pltpu.SemaphoreType.DMA((len(flat) + n,)),
        ],
        input_output_aliases=aliases,
        cost_estimate=pl.CostEstimate(
            flops=2 * n * depth * d_blk * f_blk,
            bytes_accessed=n * depth * (d_blk + f_blk) * 2 + 4 * d_blk * f_blk,
            transcendentals=0,
        ),
        compiler_params=pltpu.CompilerParams(vmem_limit_bytes=VMEM_LIMIT),
        name="outer_last" if last else "outer_first",
    )(*operands)


def project(tokens, tiles, before=None):
    size_x, cap, d = tokens.shape
    d_blk = d // GRID_R
    f_blk = tiles[0][1][0].shape[-1]
    flat = [part for _, piece in tiles for part in piece]
    evens = [i for i, (away, _) in enumerate(tiles) if away % 2 == 0]
    odds = [i for i, (away, _) in enumerate(tiles) if away % 2]
    assert evens + odds == list(range(len(tiles)))
    count = size_x * cap
    n = len(tiles)

    def kernel(*refs):
        refs = list(refs)
        tokens_ref = refs.pop(0)
        flat_refs = [refs.pop(0) for _ in flat]
        before_ref = None if before is None else refs.pop(0)
        out_ref, left, right, total, sems = refs
        z = lax.axis_index("z")
        copies = []
        at = 0
        for i, (away, piece) in enumerate(tiles):
            start = 0
            for part in piece:
                size = part.shape[0]
                copies.append((flat_refs[at], right.at[i, pl.ds(start, size)]))
                start += size
                at += 1
            block = lax.rem(z + away + 8, 8) // 2
            columns = pl.ds(pl.multiple_of(block * d_blk, 128), d_blk)
            copies.append((tokens_ref.at[:, :, columns], left.at[i]))
        fetch(copies, sems)

        def add(i, carry):
            total[...] += jnp.dot(
                left[i].reshape(count, d_blk), right[i], preferred_element_type=jnp.float32
            )
            return carry

        for i, steps in enumerate(((0, len(evens)), (len(evens), n))):
            total[...] = jnp.zeros_like(total) if before is None else before_ref[i]
            lax.fori_loop(*steps, add, 0)
            if before is None:
                out_ref[i] = total[...]
            else:
                out_ref[:, i] = total[...].astype(jnp.bfloat16).reshape(size_x, cap, f_blk)

    if before is None:
        out_shape = jax.ShapeDtypeStruct((2, count, f_blk), jnp.float32)
    else:
        out_shape = jax.ShapeDtypeStruct((size_x, 2, cap, f_blk), jnp.bfloat16)
    operands = [tokens, *flat] + ([] if before is None else [before])
    return pl.pallas_call(
        kernel,
        in_specs=[ANYWHERE] * (1 + len(flat)) + [IN_VMEM] * (len(operands) - 1 - len(flat)),
        out_specs=IN_VMEM,
        out_shape=out_shape,
        scratch_shapes=[
            pltpu.VMEM((n, size_x, cap, d_blk), jnp.bfloat16),
            pltpu.VMEM((n, d_blk, f_blk), jnp.bfloat16),
            pltpu.VMEM((count, f_blk), jnp.float32),
            pltpu.SemaphoreType.DMA((len(flat) + n,)),
        ],
        cost_estimate=pl.CostEstimate(
            flops=2 * n * count * d_blk * f_blk,
            bytes_accessed=n * d_blk * (count + f_blk) * 2,
            transcendentals=0,
        ),
        compiler_params=pltpu.CompilerParams(vmem_limit_bytes=VMEM_LIMIT),
        name="project_first" if before is None else "project_last",
    )(*operands)


def assemble(found):
    size_x, _, cap, f_blk = found.shape

    def kernel(found_ref, out_ref):
        q = lax.rem(lax.axis_index("z"), 2)
        for i in range(2):
            parity = q if i == 0 else 1 - q
            for j in range(size_x):
                start = pl.multiple_of((parity * size_x + j) * f_blk, 128)
                out_ref[:, pl.ds(start, f_blk)] = found_ref[j, i]

    return pl.pallas_call(
        kernel,
        in_specs=[IN_VMEM],
        out_specs=IN_VMEM,
        out_shape=jax.ShapeDtypeStruct((cap, 2 * size_x * f_blk), found.dtype),
        compiler_params=pltpu.CompilerParams(vmem_limit_bytes=VMEM_LIMIT),
        name="assemble",
    )(found)


def body(activations, out_grads, next_inputs, counts, master, moment, second):
    cap, d = activations.shape[2:]
    ff = out_grads.shape[3]
    d_blk, f_blk = master.shape[2:]
    size_x = lax.axis_size("x")

    own, other, row0, row_p1, row_m1, row_2 = split(
        counts, activations[0, 0], out_grads[0, 0], d_blk, f_blk
    )

    rows = [row0, shift(row_p1, "z", 2), shift(row_m1, "z", -2), shift(row_2, "z", 4)]
    other = exchanged(other, "x")
    rows = jnp.stack(rows)
    place_of = {
        0: lambda q: 0,
        -2: lambda q: 1,
        2: lambda q: 2,
        4: lambda q: 3,
        1: lambda q: 4 + 2 * q,
        -1: lambda q: 5 - q,
        3: lambda q: 6 + q,
        -3: lambda q: 7 - 2 * q,
    }

    other_m1, other_p1 = shift(other, "z", 1), shift(other, "z", -1)
    own, rows, other_m1, other_p1 = lax.optimization_barrier((own, rows, other_m1, other_p1))
    beside = lax.ppermute(rows, "z", [(i, i ^ 1) for i in range(lax.axis_size("z"))])
    rows = lax.all_gather(jnp.concatenate([rows, beside]), "x")
    own = exchanged(own, "x")
    other_m3, other_p3 = shift(other_m1, "z", 2), shift(other_p1, "z", -2)
    own, other_m3, other_p3 = lax.optimization_barrier((own, other_m3, other_p3))
    own_m2, own_p2 = shift(own, "z", 2), shift(own, "z", -2)
    pieces = {0: [own], -1: [other_m1], 1: [other_p1], -3: [other_m3], 3: [other_p3]}
    pieces |= {-2: [own_m2], 2: [own_p2]}
    first_away = (0, -1, 1, -3, 3)
    last_away = (-2, 2, 4)
    (gradient,) = outer_sum(
        rows, [place_of[a] for a in first_away], [pieces[a] for a in first_away]
    )
    half = size_x // 2
    up, down = own_m2[:half], own_p2[half:]
    pieces[4] = [shift(up, "z", 2), shift(down, "z", -2)]
    late_inputs, gradient = lax.optimization_barrier((next_inputs[0, 0], gradient))
    tokens = lax.all_gather(late_inputs, "x")
    gradient, squares = outer_sum(
        rows,
        [place_of[a] for a in last_away],
        [pieces[a] for a in last_away],
        before=gradient,
        last=True,
    )

    entries = float(lax.axis_size(EXPERT) * d * ff)
    update, first_new, later_new, sums = update_of(
        exchanged(squares, EVERYONE), gradient, master[0, 0], moment[0, 0], second[0, 0], entries
    )
    weights_new, upper, lower = weights_of(exchanged(sums, SHARD), update, master[0, 0])

    up = [[upper], [lower]]
    down = [[upper], [lower]]
    for step in range(1, 4):
        for c in range(2):
            up[c].append(shift(up[c][-1], "z", 1))
            down[c].append(shift(down[c][-1], "z", -1))
    tiles = [(0, [upper, lower])]
    for away in (2, 1):
        tiles.append((-away, [up[0][away], up[1][away]]))
        tiles.append((away, [down[0][away], down[1][away]]))
    part = project(tokens, tiles)
    part, last_up, last_down = lax.optimization_barrier((part, up[0][3], down[1][3]))
    tiles = [(4, [shift(last_up, "z", 1), shift(last_down, "z", -1)])]
    tiles.append((-3, [up[0][3], up[1][3]]))
    tiles.append((3, [down[0][3], down[1][3]]))
    found = project(tokens, tiles, before=part)
    projected = assemble(exchanged(found, "x"))
    return (
        weights_new[None, None],
        first_new[None, None],
        later_new[None, None],
        projected[None, None],
    )


def solution(mesh):
    finer = Mesh(mesh.devices.reshape(4, 2, 8, 4), EVERYONE)
    tiled = P(EXPERT, SHARD, None, None)
    return jax.shard_map(
        body,
        mesh=finer,
        in_specs=(tiled, tiled, tiled, P(EXPERT, SHARD), tiled, tiled, tiled),
        out_specs=(tiled,) * 4,
        check_vma=False,
    )
```

time: 421 us -> 298 us (0.71)
  waiting for transfers between devices: 253 us -> 114 us
  starting transfers between devices: 14.4 us -> 44.3 us
  local copies, waits for them, and re-layouts: 34.9 us -> 14.7 us
  Pallas kernels: 10.2 us -> 26.9 us
  other arithmetic: 12.3 us -> 1 us
  blocking collectives: 70.3 us -> 79.3 us
  matrix products: 8.38 us -> 0 us
    all_gather x4 -> x2, waiting for transfers between devices: 234 us -> 20.6 us  [the longest x1 20.6 us: body(): rows = lax.all_gather(jnp.concatenate([rows, beside]), 'x')]
    ppermute x0 -> x26, waiting for transfers between devices: none -> 93.7 us  [the longest x25 87.8 us: shift(): lax.ppermute(value, axis, [(i, (i + by) % size) for i in range(size)])]
    ppermute x0 -> x26, starting transfers between devices: none -> 44.2 us  [the longest x25 43.4 us: shift(): lax.ppermute(value, axis, [(i, (i + by) % size) for i in range(size)])]
    all_to_all x2 -> x0, waiting for transfers between devices: 18.8 us -> none  [the longest x1 11.7 us: body(): found = lax.all_to_all(found, 'x', 1, 1, tiled=True)]
    pallas_call x1 -> x8, Pallas kernels: 10.2 us -> 26.9 us  [the longest x2 9.62 us: outer_sum(): pl.pallas_call(kernel, in_specs=in_specs, out_specs=[IN_VMEM] * len(out_s...]
    all_to_all x2 -> x0, starting transfers between devices: 14 us -> none  [the longest x1 10.5 us: totals(): got = lax.all_to_all(sent, axes, 0, 0, tiled=True)]
    all_gather x1 -> x0, local copies, waits for them, and re-layouts: 10.8 us -> none  [body(): tiles = lax.all_gather(weights_new.astype(jnp.bfloat16), 'z')]
    all_to_all x3 -> x5, blocking collectives: 70.3 us -> 79.3 us  [exchanged(): return lax.all_to_all(values, axes, 0, 0, tiled=True)]
  transfers between devices with their start and end apart: 6 -> 28, of which waited for: 6 -> 15; matrix products, arithmetic and copies ran while one was open for 6% -> 0% of each run, Pallas kernels for 0% -> 7%
where the time goes in v2:
time: 298 us; the launch traced here: 295 us
  waiting for transfers between devices  114 us (38%)
  blocking collectives  79.3 us (27%)
  starting transfers between devices  44.3 us (15%)
  Pallas kernels  26.9 us (9%)
  between operations  14.8 us (5%)
  local copies, waits for them, and re-layouts  14.7 us (5%)
    ppermute x25, waiting for transfers between devices, shift(): lax.ppermute(value, axis, [(i, (i + by) % size) for i in range(size)])  87.8 us
    all_to_all x5, blocking collectives, exchanged(): return lax.all_to_all(values, axes, 0, 0, tiled=True)  79.3 us
    ppermute x25, starting transfers between devices, shift(): lax.ppermute(value, axis, [(i, (i + by) % size) for i in range(size)])  43.4 us
    all_gather x1, waiting for transfers between devices, body(): rows = lax.all_gather(jnp.concatenate([rows, beside]), 'x')  20.6 us
    unnamed x32, local copies, waits for them, and re-layouts  13.7 us
    pallas_call x2, Pallas kernels, outer_sum(): pl.pallas_call(kernel, in_specs=in_specs, out_specs=[IN_VMEM] * len(out_s...  9.62 us
    pallas_call x2, Pallas kernels, project(): pl.pallas_call(kernel, in_specs=[ANYWHERE] * (1 + len(flat)) + [IN_VMEM]...  9.38 us
  transfers between devices with their start and end apart: 28, of which 15 were waited for; matrix products, arithmetic and copies ran while one was open for 0% of the time, Pallas kernels for 7%

profile of v2, /device:TPU:1, one launch (start us, length us, event | category | flops | bytes accessed | tf_op | source)
XLA Modules:
  0.0 295.4 jit_solution(13973104734512646821)
XLA Ops:
  7.9 1.3 copy-done.4
  10.4 14.8 %all_to_all.25 = bf16[4,96,896]{2,1,0:T(8,128)(2,1)S(1)} all-to-all(bf16[4,96,896]{2,1,0:T(8,128)(2,1)S(1)} %get-tuple-element.36), channel_id=1, replica_groups=mesh['y'=4,'k'=2,'z'=8,'x'=4] {'x'}, dimensions={0} | all-to-all | bytes 1376256 | tf_op jit(solution)/shard_map/all_to_all | solution.py:76
  25.2 1.6 collective-permute-start.3
  26.8 3.9 %collective-permute-start.4 = (bf16[4,96,896]{2,1,0:T(8,128)(2,1)S(1)}, bf16[4,96,896]{2,1,0:T(8,128)(2,1)S(1)}, u32[]{:S(2)}, u32[]{:S(2)}) collective-permute-start(bf16[4,96,896]{2,1,0:T(8,128)(2,1)S(1)} %all_to_all.25), channel_id=1, source_target_pairs={{0,28},{4,0},{8,4},{12,8},{16,12},{20,16},{24,20},{28,24},{1,29},{... | collective-permute-start | bytes 2064392 | tf_op jit(solution)/shard_map/ppermute | solution.py:20
  30.8 4.0 %collective-permute-start.2 = (bf16[96,512]{1,0:T(8,128)(2,1)S(1)}, bf16[96,512]{1,0:T(8,128)(2,1)S(1)}, u32[]{:S(2)}, u32[]{:S(2)}) collective-permute-start(bf16[96,512]{1,0:T(8,128)(2,1)S(1)} %get-tuple-element.35), channel_id=1, source_target_pairs={{0,16},{4,20},{8,24},{12,28},{16,0},{20,4},{24,8},{28,12},{1,17},{... | collective-permute-start | bytes 294920 | tf_op jit(solution)/shard_map/ppermute | solution.py:20
  34.8 2.4 collective-permute-start
  37.1 11.3 %collective-permute-done.2 = bf16[96,512]{1,0:T(8,128)(2,1)S(1)} collective-permute-done((bf16[96,512]{1,0:T(8,128)(2,1)S(1)}, bf16[96,512]{1,0:T(8,128)(2,1)S(1)}, u32[]{:S(2)}, u32[]{:S(2)}) %collective-permute-start.2) | collective-permute-done | bytes 98336 | tf_op jit(solution)/shard_map/ppermute | solution.py:20
  49.1 2.2 collective-permute-done
  52.2 5.9 %collective-permute-done.5 = bf16[4,96,512]{2,1,0:T(8,128)(2,1)S(1)} collective-permute-done((bf16[4,96,512]{2,1,0:T(8,128)(2,1)S(1)}, bf16[4,96,512]{2,1,0:T(8,128)(2,1)S(1)}, u32[]{:S(2)}, u32[]{:S(2)}) %collective-permute-start.5) | collective-permute-done | bytes 393248 | tf_op jit(solution)/shard_map/ppermute | solution.py:370
  59.2 2.9 collective-permute-start.6
  63.0 11.6 %all_to_all.26.refs_1_ = bf16[4,96,896]{2,1,0:T(8,128)(2,1)S(1)} all-to-all(bf16[4,96,896]{2,1,0:T(8,128)(2,1)S(1)} %get-tuple-element.38), channel_id=1, replica_groups=mesh['y'=4,'k'=2,'z'=8,'x'=4] {'x'}, dimensions={0} | all-to-all | bytes 1376256 | tf_op jit(solution)/shard_map/all_to_all | solution.py:76
  74.6 11.7 %collective-permute-done.6.refs_4_ = bf16[4,96,896]{2,1,0:T(8,128)(2,1)S(1)} collective-permute-done((bf16[4,96,896]{2,1,0:T(8,128)(2,1)S(1)}, bf16[4,96,896]{2,1,0:T(8,128)(2,1)S(1)}, u32[]{:S(2)}, u32[]{:S(2)}) %collective-permute-start.6) | collective-permute-done | bytes 688160 | tf_op jit(solution)/shard_map/ppermute | solution.py:20
  88.0 4.7 %collective-permute-start.9 = (bf16[4,96,896]{2,1,0:T(8,128)(2,1)S(1)}, bf16[4,96,896]{2,1,0:T(8,128)(2,1)}, u32[]{:S(2)}, u32[]{:S(2)}) collective-permute-start(bf16[4,96,896]{2,1,0:T(8,128)(2,1)S(1)} %all_to_all.26.refs_1_), channel_id=1, source_target_pairs={{0,24},{4,28},{8,0},{12,4},{16,8},{20,12},{24,16},{28,20},{1,25},{... | collective-permute-start | bytes 2064392 | tf_op jit(solution)/shard_map/ppermute | solution.py:20
  92.7 20.6 %all-gather.5.cloned.1.call-done = bf16[32,96,512]{2,1,0:T(8,128)(2,1)} async-done(((bf16[8,96,512]{2,1,0:T(8,128)(2,1)}), bf16[32,96,512]{2,1,0:T(8,128)(2,1)}) %all-gather.5.cloned.1.call-update) | async-done | bytes 3145744 | tf_op jit(solution)/shard_map/all_gather | solution.py:371
  113.3 1.9 copy-done
  115.2 1.1 copy-done.8
  116.3 1.1 copy-done.10
  117.4 1.1 copy-done.12
  118.5 1.1 copy-done.14
  119.6 5.4 %outer_first.1.refs_5_ = f32[512,896]{1,0:T(8,128)S(1)} custom-call(bf16[4,8,96,512]{3,2,1,0:T(8,128)(2,1)S(1)} %bitcast.16, bf16[4,96,896]{2,1,0:T(8,128)(2,1)S(1)} %all_to_all.26.refs_1_, bf16[4,96,896]{2,1,0:T(8,128)(2,1)S(1)} %copy-done.8, bf16[4,96,896]{2,1,0:T(8,128)(2,1)S(1)} %copy-done.10, bf16[4,96,896]{2,1,0:T(8,128)(2,1)S(1)} %copy-done.12, ...), custom_call_target="tpu_custom_call" | custom-call | flops 1761607680 | bytes 7241728 | tf_op jit(solution)/shard_map/outer_first/pallas_call | solution.py:230
  125.0 2.3 collective-permute-start.10
  128.4 1.9 collective-permute-start.11
  130.2 10.5 %collective-permute-done.10.refs_3_ = bf16[2,96,896]{2,1,0:T(8,128)(2,1)S(1)} collective-permute-done((bf16[2,96,896]{2,1,0:T(8,128)(2,1)S(1)}, bf16[2,96,896]{2,1,0:T(8,128)(2,1)S(1)}, u32[]{:S(2)}, u32[]{:S(2)}) %collective-permute-start.10) | collective-permute-done | bytes 344096 | tf_op jit(solution)/shard_map/ppermute | solution.py:20
  140.8 7.0 %collective-permute-done.11.refs_4_ = bf16[2,96,896]{2,1,0:T(8,128)(2,1)S(1)} collective-permute-done((bf16[2,96,896]{2,1,0:T(8,128)(2,1)S(1)}, bf16[2,96,896]{2,1,0:T(8,128)(2,1)S(1)}, u32[]{:S(2)}, u32[]{:S(2)}) %collective-permute-start.11) | collective-permute-done | bytes 344096 | tf_op jit(solution)/shard_map/ppermute | solution.py:20
  147.7 1.9 copy-done.1
  149.7 4.2 %outer_last.1 = (f32[512,896]{1,0:T(8,128)S(1)}, f32[256,1,128]{2,1,0:T(1,128)S(1)}) custom-call(bf16[4,8,96,512]{3,2,1,0:T(8,128)(2,1)S(1)} %bitcast.17, bf16[4,96,896]{2,1,0:T(8,128)(2,1)S(1)} %collective-permute-done.8.refs_1_, bf16[4,96,896]{2,1,0:T(8,128)(2,1)} %collective-permute-done.9.refs_2_, ...), custom_call_target="tpu_custom_call", output_to_operand_aliasing={{0}: (5, {})} | custom-call | flops 1056964608 | bytes 5079040 | tf_op jit(solution)/shard_map/outer_last/pallas_call | solution.py:230
  153.9 23.3 %all_to_all.27.n_ref = f32[256,1,128]{2,1,0:T(1,128)S(1)} all-to-all(f32[256,1,128]{2,1,0:T(1,128)S(1)} %get-tuple-element.45), channel_id=1, replica_groups=mesh['y'=4,'k'=2,'z'=8,'x'=4] {'y','k','z','x'}, dimensions={0} | all-to-all | bytes 262144 | tf_op jit(solution)/shard_map/all_to_all | solution.py:76
  177.2 4.3 %update_of.1 = (f32[512,896]{1,0:T(8,128)S(1)}, bf16[512,896]{1,0:T(8,128)(2,1)}, bf16[512,896]{1,0:T(8,128)(2,1)}, f32[32,2,128]{2,1,0:T(2,128)S(1)}) custom-call(f32[256,1,128]{2,1,0:T(1,128)S(1)} %all_to_all.27.n_ref, f32[512,896]{1,0:T(8,128)S(1)} %get-tuple-element.46.g_ref, f32[512,896]{1,0:T(8,128)S(1)} %bitcast.18, bf16[512,896]{1,0:T(8,128)(2,1)S(1)} %bitcast.23, ...), custom_call_target="tpu_custom_call" | custom-call | tf_op jit(solution)/shard_map/update_of/pallas_call | solution.py:113
  181.6 12.0 %all_to_all.28.sums_ref = f32[32,2,128]{2,1,0:T(2,128)S(1)} all-to-all(f32[32,2,128]{2,1,0:T(2,128)S(1)} %get-tuple-element.47), channel_id=1, replica_groups=mesh['y'=4,'k'=2,'z'=8,'x'=4] {'z','x'}, dimensions={0} | all-to-all | bytes 65536 | tf_op jit(solution)/shard_map/all_to_all | solution.py:76
  193.6 2.1 weights_of.1
  196.0 2.3 collective-permute-start.18
  198.3 2.7 collective-permute-start.16
  201.0 5.6 %collective-permute-done.12.refs_7_ = bf16[256,896]{1,0:T(8,128)(2,1)S(1)} collective-permute-done((bf16[256,896]{1,0:T(8,128)(2,1)S(1)}, bf16[256,896]{1,0:T(8,128)(2,1)S(1)}, u32[]{:S(2)}, u32[]{:S(2)}) %collective-permute-start.12) | collective-permute-done | bytes 458784 | tf_op jit(solution)/shard_map/ppermute | solution.py:20
  206.6 2.7 collective-permute-start.19
  209.3 7.1 %collective-permute-done.14.refs_8_ = bf16[256,896]{1,0:T(8,128)(2,1)S(1)} collective-permute-done((bf16[256,896]{1,0:T(8,128)(2,1)S(1)}, bf16[256,896]{1,0:T(8,128)(2,1)S(1)}, u32[]{:S(2)}, u32[]{:S(2)}) %collective-permute-start.14) | collective-permute-done | bytes 458784 | tf_op jit(solution)/shard_map/ppermute | solution.py:20
  216.5 2.7 collective-permute-start.17
  219.1 7.3 %collective-permute-done.13.refs_3_ = bf16[256,896]{1,0:T(8,128)(2,1)} collective-permute-done((bf16[256,896]{1,0:T(8,128)(2,1)S(1)}, bf16[256,896]{1,0:T(8,128)(2,1)}, u32[]{:S(2)}, u32[]{:S(2)}) %collective-permute-start.13) | collective-permute-done | bytes 458784 | tf_op jit(solution)/shard_map/ppermute | solution.py:20
  226.4 2.7 collective-permute-start.21
  229.1 7.1 %collective-permute-done.15.refs_4_ = bf16[256,896]{1,0:T(8,128)(2,1)} collective-permute-done((bf16[256,896]{1,0:T(8,128)(2,1)S(1)}, bf16[256,896]{1,0:T(8,128)(2,1)}, u32[]{:S(2)}, u32[]{:S(2)}) %collective-permute-start.15) | collective-permute-done | bytes 458784 | tf_op jit(solution)/shard_map/ppermute | solution.py:20
  236.2 2.7 collective-permute-start.25
  238.9 1.4 copy-done.3
  240.3 5.4 %project_first.1.refs_7_ = f32[2,384,896]{2,1,0:T(8,128)S(1)} custom-call(bf16[4,96,2048]{2,1,0:T(8,128)(2,1)S(1)} %bitcast.20, bf16[256,896]{1,0:T(8,128)(2,1)S(1)} %get-tuple-element.53.refs_1_, bf16[256,896]{1,0:T(8,128)(2,1)S(1)} %get-tuple-element.54.refs_2_, bf16[256,896]{1,0:T(8,128)(2,1)} %collective-permute-done.13.refs_3_, ...), custom_call_target="tpu_custom_call" | custom-call | flops 1761607680 | bytes 6553600 | tf_op jit(solution)/shard_map/project_first/pallas_call | solution.py:302
  246.0 2.7 collective-permute-start.23
  248.6 7.3 %collective-permute-done.24.refs_4_ = bf16[256,896]{1,0:T(8,128)(2,1)} collective-permute-done((bf16[256,896]{1,0:T(8,128)(2,1)}, bf16[256,896]{1,0:T(8,128)(2,1)}, u32[]{:S(2)}, u32[]{:S(2)}) %collective-permute-start.24) | collective-permute-done | bytes 458784 | tf_op jit(solution)/shard_map/ppermute | solution.py:20
  255.9 9.7 %collective-permute-done.22.refs_1_ = bf16[256,896]{1,0:T(8,128)(2,1)S(1)} collective-permute-done((bf16[256,896]{1,0:T(8,128)(2,1)S(1)}, bf16[256,896]{1,0:T(8,128)(2,1)S(1)}, u32[]{:S(2)}, u32[]{:S(2)}) %collective-permute-start.22) | collective-permute-done | bytes 458784 | tf_op jit(solution)/shard_map/ppermute | solution.py:20
  265.6 4.0 %project_last.1 = bf16[4,2,96,896]{3,2,1,0:T(8,128)(2,1)S(1)} custom-call(bf16[4,96,2048]{2,1,0:T(8,128)(2,1)S(1)} %bitcast.21, bf16[256,896]{1,0:T(8,128)(2,1)S(1)} %collective-permute-done.22.refs_1_, bf16[256,896]{1,0:T(8,128)(2,1)S(1)} %collective-permute-done.23.refs_2_, bf16[256,896]{1,0:T(8,128)(2,1)S(1)} %collective-permute-done.20.refs_3_, ...), custom_call_target="tpu_custom_call" | custom-call | flops 1056964608 | bytes 3932160 | tf_op jit(solution)/shard_map/project_last/pallas_call | solution.py:302
  269.6 17.7 %all_to_all.29.found_ref = bf16[4,2,96,896]{3,2,1,0:T(8,128)(2,1)S(1)} all-to-all(bf16[4,2,96,896]{3,2,1,0:T(8,128)(2,1)S(1)} %project_last.1), channel_id=1, replica_groups=mesh['y'=4,'k'=2,'z'=8,'x'=4] {'x'}, dimensions={0} | all-to-all | bytes 2752512 | tf_op jit(solution)/shard_map/all_to_all | solution.py:76
  287.3 1.2 assemble.1
  (59 shorter events, 8.2 us)
Async XLA Ops:
  7.2 106.1 %all-gather.5.cloned.1.call-start = ((), (), s32[]{:S(2)}) async-start(), calls=%async_computation.5 | async-start | bytes 3932160 | tf_op jit(solution)/shard_map/all_gather | solution.py:371
  7.9 1.3 copy-start.4
  9.2 1.0 copy-start.15
  25.2 26.2 %collective-permute-start.3 = (bf16[4,96,896]{2,1,0:T(8,128)(2,1)S(1)}, bf16[4,96,896]{2,1,0:T(8,128)(2,1)S(1)}, u32[]{:S(2)}, u32[]{:S(2)}) collective-permute-start(bf16[4,96,896]{2,1,0:T(8,128)(2,1)S(1)} %all_to_all.25), channel_id=1, source_target_pairs={{0,4},{4,8},{8,12},{12,16},{16,20},{20,24},{24,28},{28,0},{1,5},{5... | collective-permute-start | bytes 2064392 | tf_op jit(solution)/shard_map/ppermute | solution.py:20
  26.8 24.6 %collective-permute-start.4 = (bf16[4,96,896]{2,1,0:T(8,128)(2,1)S(1)}, bf16[4,96,896]{2,1,0:T(8,128)(2,1)S(1)}, u32[]{:S(2)}, u32[]{:S(2)}) collective-permute-start(bf16[4,96,896]{2,1,0:T(8,128)(2,1)S(1)} %all_to_all.25), channel_id=1, source_target_pairs={{0,28},{4,0},{8,4},{12,8},{16,12},{20,16},{24,20},{28,24},{1,29},{... | collective-permute-start | bytes 2064392 | tf_op jit(solution)/shard_map/ppermute | solution.py:20
  30.8 17.7 %collective-permute-start.2 = (bf16[96,512]{1,0:T(8,128)(2,1)S(1)}, bf16[96,512]{1,0:T(8,128)(2,1)S(1)}, u32[]{:S(2)}, u32[]{:S(2)}) collective-permute-start(bf16[96,512]{1,0:T(8,128)(2,1)S(1)} %get-tuple-element.35), channel_id=1, source_target_pairs={{0,16},{4,20},{8,24},{12,28},{16,0},{20,4},{24,8},{28,12},{1,17},{... | collective-permute-start | bytes 294920 | tf_op jit(solution)/shard_map/ppermute | solution.py:20
  34.8 14.4 %collective-permute-start.1 = (bf16[96,512]{1,0:T(8,128)(2,1)S(1)}, bf16[96,512]{1,0:T(8,128)(2,1)S(1)}, u32[]{:S(2)}, u32[]{:S(2)}) collective-permute-start(bf16[96,512]{1,0:T(8,128)(2,1)S(1)} %get-tuple-element.34), channel_id=1, source_target_pairs={{0,24},{4,28},{8,0},{12,4},{16,8},{20,12},{24,16},{28,20},{1,25},{... | collective-permute-start | bytes 294920 | tf_op jit(solution)/shard_map/ppermute | solution.py:20
  34.8 16.6 %collective-permute-start = (bf16[96,512]{1,0:T(8,128)(2,1)S(1)}, bf16[96,512]{1,0:T(8,128)(2,1)S(1)}, u32[]{:S(2)}, u32[]{:S(2)}) collective-permute-start(bf16[96,512]{1,0:T(8,128)(2,1)S(1)} %get-tuple-element.33), channel_id=1, source_target_pairs={{0,8},{4,12},{8,16},{12,20},{16,24},{20,28},{24,0},{28,4},{1,9},{5... | collective-permute-start | bytes 294920 | tf_op jit(solution)/shard_map/ppermute | solution.py:20
  51.4 23.2 %copy-start.7 = (bf16[4,96,896]{2,1,0:T(8,128)(2,1)}, bf16[4,96,896]{2,1,0:T(8,128)(2,1)S(1)}, u32[]{:S(2)}) copy-start(bf16[4,96,896]{2,1,0:T(8,128)(2,1)S(1)} %collective-permute-done.3.refs_2_) | copy-start | bytes 2064388
  51.4 23.2 %copy-start.9 = (bf16[4,96,896]{2,1,0:T(8,128)(2,1)}, bf16[4,96,896]{2,1,0:T(8,128)(2,1)S(1)}, u32[]{:S(2)}) copy-start(bf16[4,96,896]{2,1,0:T(8,128)(2,1)S(1)} %collective-permute-done.4.refs_3_) | copy-start | bytes 2064388
  51.4 6.7 %collective-permute-start.5 = (bf16[4,96,512]{2,1,0:T(8,128)(2,1)S(1)}, bf16[4,96,512]{2,1,0:T(8,128)(2,1)S(1)}, u32[]{:S(2)}, u32[]{:S(2)}) collective-permute-start(bf16[4,96,512]{2,1,0:T(8,128)(2,1)S(1)} %pad_maximum_fusion.1), channel_id=1, source_target_pairs={{0,4},{4,0},{8,12},{12,8},{16,20},{20,16},{24,28},{28,24},{1,5},{5... | collective-permute-start | bytes 1179656 | tf_op jit(solution)/shard_map/ppermute | solution.py:370
  59.1 179.8 %all-gather.7.cloned.1.call-start = ((), (), s32[]{:S(2)}) async-start(), calls=%async_computation.6 | async-start | bytes 1966080 | tf_op jit(solution)/shard_map/all_gather | solution.py:387
  59.2 27.1 %collective-permute-start.6 = (bf16[4,96,896]{2,1,0:T(8,128)(2,1)S(1)}, bf16[4,96,896]{2,1,0:T(8,128)(2,1)S(1)}, u32[]{:S(2)}, u32[]{:S(2)}) collective-permute-start(bf16[4,96,896]{2,1,0:T(8,128)(2,1)S(1)} %collective-permute-done.3.refs_2_), channel_id=1, source_target_pairs={{0,8},{4,12},{8,16},{12,20},{16,24},{20,28},{24,0},{28,4},{1,9},{5... | collective-permute-start | bytes 2064392 | tf_op jit(solution)/shard_map/ppermute | solution.py:20
  62.1 25.1 %collective-permute-start.7 = (bf16[4,96,896]{2,1,0:T(8,128)(2,1)S(1)}, bf16[4,96,896]{2,1,0:T(8,128)(2,1)S(1)}, u32[]{:S(2)}, u32[]{:S(2)}) collective-permute-start(bf16[4,96,896]{2,1,0:T(8,128)(2,1)S(1)} %collective-permute-done.4.refs_3_), channel_id=1, source_target_pairs={{0,24},{4,28},{8,0},{12,4},{16,8},{20,12},{24,16},{28,20},{1,25},{... | collective-permute-start | bytes 2064392 | tf_op jit(solution)/shard_map/ppermute | solution.py:20
  86.3 0.8 copy-start.11
  87.2 0.8 copy-start.13
  88.0 37.0 %collective-permute-start.8 = (bf16[4,96,896]{2,1,0:T(8,128)(2,1)S(1)}, bf16[4,96,896]{2,1,0:T(8,128)(2,1)S(1)}, u32[]{:S(2)}, u32[]{:S(2)}) collective-permute-start(bf16[4,96,896]{2,1,0:T(8,128)(2,1)S(1)} %all_to_all.26.refs_1_), channel_id=1, source_target_pairs={{0,8},{4,12},{8,16},{12,20},{16,24},{20,28},{24,0},{28,4},{1,9},{5... | collective-permute-start | bytes 2064392 | tf_op jit(solution)/shard_map/ppermute | solution.py:20
  88.0 39.4 %collective-permute-start.9 = (bf16[4,96,896]{2,1,0:T(8,128)(2,1)S(1)}, bf16[4,96,896]{2,1,0:T(8,128)(2,1)}, u32[]{:S(2)}, u32[]{:S(2)}) collective-permute-start(bf16[4,96,896]{2,1,0:T(8,128)(2,1)S(1)} %all_to_all.26.refs_1_), channel_id=1, source_target_pairs={{0,24},{4,28},{8,0},{12,4},{16,8},{20,12},{24,16},{28,20},{1,25},{... | collective-permute-start | bytes 2064392 | tf_op jit(solution)/shard_map/ppermute | solution.py:20
  113.3 1.9 copy-start
  115.2 1.1 copy-start.8
  116.3 1.1 copy-start.10
  117.4 1.1 copy-start.12
  118.5 1.1 copy-start.14
  125.0 15.7 %collective-permute-start.10 = (bf16[2,96,896]{2,1,0:T(8,128)(2,1)S(1)}, bf16[2,96,896]{2,1,0:T(8,128)(2,1)S(1)}, u32[]{:S(2)}, u32[]{:S(2)}) collective-permute-start(bf16[2,96,896]{2,1,0:T(8,128)(2,1)S(1)} %slice.8), channel_id=1, source_target_pairs={{0,8},{4,12},{8,16},{12,20},{16,24},{20,28},{24,0},{28,4},{1,9},{5... | collective-permute-start | bytes 1032200 | tf_op jit(solution)/shard_map/ppermute | solution.py:20
  128.4 19.4 %collective-permute-start.11 = (bf16[2,96,896]{2,1,0:T(8,128)(2,1)S(1)}, bf16[2,96,896]{2,1,0:T(8,128)(2,1)S(1)}, u32[]{:S(2)}, u32[]{:S(2)}) collective-permute-start(bf16[2,96,896]{2,1,0:T(8,128)(2,1)S(1)} %slice.9), channel_id=1, source_target_pairs={{0,24},{4,28},{8,0},{12,4},{16,8},{20,12},{24,16},{28,20},{1,25},{... | collective-permute-start | bytes 1032200 | tf_op jit(solution)/shard_map/ppermute | solution.py:20
  147.7 1.9 copy-start.1
  149.7 27.6 %copy-start.2 = (f32[1,1,512,896]{3,2,1,0:T(8,128)S(1)}, f32[1,1,512,896]{3,2,1,0:T(8,128)}, u32[]{:S(2)}) copy-start(f32[1,1,512,896]{3,2,1,0:T(8,128)} %param.11) | copy-start | bytes 5505028
  149.7 27.6 %copy-start.5 = (bf16[1,1,512,896]{3,2,1,0:T(8,128)(2,1)S(1)}, bf16[1,1,512,896]{3,2,1,0:T(8,128)(2,1)}, u32[]{:S(2)}) copy-start(bf16[1,1,512,896]{3,2,1,0:T(8,128)(2,1)} %param.12) | copy-start | bytes 2752516
  149.7 27.6 %copy-start.6 = (bf16[1,1,512,896]{3,2,1,0:T(8,128)(2,1)S(1)}, bf16[1,1,512,896]{3,2,1,0:T(8,128)(2,1)}, u32[]{:S(2)}) copy-start(bf16[1,1,512,896]{3,2,1,0:T(8,128)(2,1)} %param.13) | copy-start | bytes 2752516
  195.7 11.0 %collective-permute-start.12 = (bf16[256,896]{1,0:T(8,128)(2,1)S(1)}, bf16[256,896]{1,0:T(8,128)(2,1)S(1)}, u32[]{:S(2)}, u32[]{:S(2)}) collective-permute-start(bf16[256,896]{1,0:T(8,128)(2,1)S(1)} %get-tuple-element.53.refs_1_), channel_id=1, source_target_pairs={{0,4},{4,8},{8,12},{12,16},{16,20},{20,24},{24,28},{28,0},{1,5},{5... | collective-permute-start | bytes 1376264 | tf_op jit(solution)/shard_map/ppermute | solution.py:20
  196.0 10.6 %collective-permute-start.18 = (bf16[256,896]{1,0:T(8,128)(2,1)S(1)}, bf16[256,896]{1,0:T(8,128)(2,1)S(1)}, u32[]{:S(2)}, u32[]{:S(2)}) collective-permute-start(bf16[256,896]{1,0:T(8,128)(2,1)S(1)} %get-tuple-element.54.refs_2_), channel_id=1, source_target_pairs={{0,28},{4,0},{8,4},{12,8},{16,12},{20,16},{24,20},{28,24},{1,29},{... | collective-permute-start | bytes 1376264 | tf_op jit(solution)/shard_map/ppermute | solution.py:20
  198.3 18.1 %collective-permute-start.14 = (bf16[256,896]{1,0:T(8,128)(2,1)S(1)}, bf16[256,896]{1,0:T(8,128)(2,1)S(1)}, u32[]{:S(2)}, u32[]{:S(2)}) collective-permute-start(bf16[256,896]{1,0:T(8,128)(2,1)S(1)} %get-tuple-element.54.refs_2_), channel_id=1, source_target_pairs={{0,4},{4,8},{8,12},{12,16},{16,20},{20,24},{24,28},{28,0},{1,5},{5... | collective-permute-start | bytes 1376264 | tf_op jit(solution)/shard_map/ppermute | solution.py:20
  198.3 18.1 %collective-permute-start.16 = (bf16[256,896]{1,0:T(8,128)(2,1)S(1)}, bf16[256,896]{1,0:T(8,128)(2,1)S(1)}, u32[]{:S(2)}, u32[]{:S(2)}) collective-permute-start(bf16[256,896]{1,0:T(8,128)(2,1)S(1)} %get-tuple-element.53.refs_1_), channel_id=1, source_target_pairs={{0,28},{4,0},{8,4},{12,8},{16,12},{20,16},{24,20},{28,24},{1,29},{... | collective-permute-start | bytes 1376264 | tf_op jit(solution)/shard_map/ppermute | solution.py:20
  206.6 19.8 %collective-permute-start.13 = (bf16[256,896]{1,0:T(8,128)(2,1)S(1)}, bf16[256,896]{1,0:T(8,128)(2,1)}, u32[]{:S(2)}, u32[]{:S(2)}) collective-permute-start(bf16[256,896]{1,0:T(8,128)(2,1)S(1)} %collective-permute-done.12.refs_7_), channel_id=1, source_target_pairs={{0,4},{4,8},{8,12},{12,16},{16,20},{20,24},{24,28},{28,0},{1,5},{5... | collective-permute-start | bytes 1376264 | tf_op jit(solution)/shard_map/ppermute | solution.py:20
  206.6 19.8 %collective-permute-start.19 = (bf16[256,896]{1,0:T(8,128)(2,1)S(1)}, bf16[256,896]{1,0:T(8,128)(2,1)}, u32[]{:S(2)}, u32[]{:S(2)}) collective-permute-start(bf16[256,896]{1,0:T(8,128)(2,1)S(1)} %collective-permute-done.18.refs_10_), channel_id=1, source_target_pairs={{0,28},{4,0},{8,4},{12,8},{16,12},{20,16},{24,20},{28,24},{1,29},{... | collective-permute-start | bytes 1376264 | tf_op jit(solution)/shard_map/ppermute | solution.py:20
  216.5 19.8 %collective-permute-start.15 = (bf16[256,896]{1,0:T(8,128)(2,1)S(1)}, bf16[256,896]{1,0:T(8,128)(2,1)}, u32[]{:S(2)}, u32[]{:S(2)}) collective-permute-start(bf16[256,896]{1,0:T(8,128)(2,1)S(1)} %collective-permute-done.14.refs_8_), channel_id=1, source_target_pairs={{0,4},{4,8},{8,12},{12,16},{16,20},{20,24},{24,28},{28,0},{1,5},{5... | collective-permute-start | bytes 1376264 | tf_op jit(solution)/shard_map/ppermute | solution.py:20
  216.5 19.8 %collective-permute-start.17 = (bf16[256,896]{1,0:T(8,128)(2,1)S(1)}, bf16[256,896]{1,0:T(8,128)(2,1)}, u32[]{:S(2)}, u32[]{:S(2)}) collective-permute-start(bf16[256,896]{1,0:T(8,128)(2,1)S(1)} %collective-permute-done.16.refs_9_), channel_id=1, source_target_pairs={{0,28},{4,0},{8,4},{12,8},{16,12},{20,16},{24,20},{28,24},{1,29},{... | collective-permute-start | bytes 1376264 | tf_op jit(solution)/shard_map/ppermute | solution.py:20
  226.4 19.6 %collective-permute-start.20 = (bf16[256,896]{1,0:T(8,128)(2,1)}, bf16[256,896]{1,0:T(8,128)(2,1)S(1)}, u32[]{:S(2)}, u32[]{:S(2)}) collective-permute-start(bf16[256,896]{1,0:T(8,128)(2,1)} %collective-permute-done.13.refs_3_), channel_id=1, source_target_pairs={{0,4},{4,8},{8,12},{12,16},{16,20},{20,24},{24,28},{28,0},{1,5},{5... | collective-permute-start | bytes 1376264 | tf_op jit(solution)/shard_map/ppermute | solution.py:20
  226.4 19.6 %collective-permute-start.21 = (bf16[256,896]{1,0:T(8,128)(2,1)}, bf16[256,896]{1,0:T(8,128)(2,1)}, u32[]{:S(2)}, u32[]{:S(2)}) collective-permute-start(bf16[256,896]{1,0:T(8,128)(2,1)} %collective-permute-done.19.refs_6_), channel_id=1, source_target_pairs={{0,28},{4,0},{8,4},{12,8},{16,12},{20,16},{24,20},{28,24},{1,29},{... | collective-permute-start | bytes 1376264 | tf_op jit(solution)/shard_map/ppermute | solution.py:20
  236.2 19.7 %collective-permute-start.24 = (bf16[256,896]{1,0:T(8,128)(2,1)}, bf16[256,896]{1,0:T(8,128)(2,1)}, u32[]{:S(2)}, u32[]{:S(2)}) collective-permute-start(bf16[256,896]{1,0:T(8,128)(2,1)} %collective-permute-done.15.refs_4_), channel_id=1, source_target_pairs={{0,4},{4,8},{8,12},{12,16},{16,20},{20,24},{24,28},{28,0},{1,5},{5... | collective-permute-start | bytes 1376264 | tf_op jit(solution)/shard_map/ppermute | solution.py:20
  236.2 19.7 %collective-permute-start.25 = (bf16[256,896]{1,0:T(8,128)(2,1)}, bf16[256,896]{1,0:T(8,128)(2,1)}, u32[]{:S(2)}, u32[]{:S(2)}) collective-permute-start(bf16[256,896]{1,0:T(8,128)(2,1)} %collective-permute-done.17.refs_5_), channel_id=1, source_target_pairs={{0,28},{4,0},{8,4},{12,8},{16,12},{20,16},{24,20},{28,24},{1,29},{... | collective-permute-start | bytes 1376264 | tf_op jit(solution)/shard_map/ppermute | solution.py:20
  238.9 1.4 copy-start.3
  245.9 19.7 %collective-permute-start.22 = (bf16[256,896]{1,0:T(8,128)(2,1)S(1)}, bf16[256,896]{1,0:T(8,128)(2,1)S(1)}, u32[]{:S(2)}, u32[]{:S(2)}) collective-permute-start(bf16[256,896]{1,0:T(8,128)(2,1)S(1)} %collective-permute-done.20.refs_3_), channel_id=1, source_target_pairs={{0,4},{4,8},{8,12},{12,16},{16,20},{20,24},{24,28},{28,0},{1,5},{5... | collective-permute-start | bytes 1376264 | tf_op jit(solution)/shard_map/ppermute | solution.py:20
  246.0 19.7 %collective-permute-start.23 = (bf16[256,896]{1,0:T(8,128)(2,1)}, bf16[256,896]{1,0:T(8,128)(2,1)S(1)}, u32[]{:S(2)}, u32[]{:S(2)}) collective-permute-start(bf16[256,896]{1,0:T(8,128)(2,1)} %collective-permute-done.21.refs_6_), channel_id=1, source_target_pairs={{0,28},{4,0},{8,4},{12,8},{16,12},{20,16},{24,20},{28,24},{1,29},{... | collective-permute-start | bytes 1376264 | tf_op jit(solution)/shard_map/ppermute | solution.py:20
Sparse Core Ops, SparseCore 0:
  59.3 53.9 all-gather.4
  125.1 29.2 all-gather.6

commit v3 on v2

--- a/solution.py
+++ b/solution.py
@@ -203,22 +203,25 @@
         else:
             total_ref[...] = before_ref[...]
 
-        def add(i, carry):
-            total_ref[...] += lax.dot_general(
-                left[i].reshape(depth, d_blk),
+        def add(step, carry):
+            i, at = step // 2, pl.multiple_of(lax.rem(step, 2) * (d_blk // 2), 128)
+            here = pl.ds(at, d_blk // 2)
+            total_ref[here, :] += lax.dot_general(
+                left[i, :, :, here].reshape(depth, d_blk // 2),
                 right[i].reshape(depth, f_blk),
                 (((0,), (0,)), ((), ())),
                 preferred_element_type=jnp.float32,
             )
             return carry
 
-        lax.fori_loop(0, n, add, 0)
+        lax.fori_loop(0, 2 * n, add, 0)
         if last:
             value = total_ref[...]
             square_ref[...] = jnp.broadcast_to(by_lane(value * value)[None], square_ref.shape)
 
     operands = [rows, *flat]
-    in_specs = [ANYWHERE] * len(operands)
+    in_specs = [ANYWHERE] * (1 + len(flat))
+    operands[0] = pltpu.with_memory_space_constraint(rows, pltpu.HBM)
     aliases = {}
     if before is not None:
         aliases = {len(operands): 0}
@@ -244,11 +247,11 @@
             transcendentals=0,
         ),
         compiler_params=pltpu.CompilerParams(vmem_limit_bytes=VMEM_LIMIT),
-        name="outer_last" if last else "outer_first",
+        name="outer_last" if last else "outer_first" if before is None else "outer_next",
     )(*operands)
 
 
-def project(tokens, tiles, before=None):
+def project(tokens, tiles, before=None, last=False):
     size_x, cap, d = tokens.shape
     d_blk = d // GRID_R
     f_blk = tiles[0][1][0].shape[-1]
@@ -288,17 +291,18 @@
 
         for i, steps in enumerate(((0, len(evens)), (len(evens), n))):
             total[...] = jnp.zeros_like(total) if before is None else before_ref[i]
-            lax.fori_loop(*steps, add, 0)
-            if before is None:
+            if steps[0] < steps[1]:
+                lax.fori_loop(*steps, add, 0)
+            if last:
+                out_ref[:, i] = total[...].astype(jnp.bfloat16).reshape(size_x, cap, f_blk)
+            else:
                 out_ref[i] = total[...]
-            else:
-                out_ref[:, i] = total[...].astype(jnp.bfloat16).reshape(size_x, cap, f_blk)
-
-    if before is None:
+
+    if last:
+        out_shape = jax.ShapeDtypeStruct((size_x, 2, cap, f_blk), jnp.bfloat16)
+    else:
         out_shape = jax.ShapeDtypeStruct((2, count, f_blk), jnp.float32)
-    else:
-        out_shape = jax.ShapeDtypeStruct((size_x, 2, cap, f_blk), jnp.bfloat16)
-    operands = [tokens, *flat] + ([] if before is None else [before])
+    operands = [pltpu.with_memory_space_constraint(tokens, pltpu.HBM), *flat] + ([] if before is None else [before])
     return pl.pallas_call(
         kernel,
         in_specs=[ANYWHERE] * (1 + len(flat)) + [IN_VMEM] * (len(operands) - 1 - len(flat)),
@@ -316,7 +320,7 @@
             transcendentals=0,
         ),
         compiler_params=pltpu.CompilerParams(vmem_limit_bytes=VMEM_LIMIT),
-        name="project_first" if before is None else "project_last",
+        name="project_last" if last else "project_first" if before is None else "project_next",
     )(*operands)
 
 
@@ -353,7 +357,8 @@
 
     rows = [row0, shift(row_p1, "z", 2), shift(row_m1, "z", -2), shift(row_2, "z", 4)]
     other = exchanged(other, "x")
-    rows = jnp.stack(rows)
+    other, rows = lax.optimization_barrier((other, jnp.stack(rows)))
+    beside = lax.ppermute(rows, "z", [(i, i ^ 1) for i in range(lax.axis_size("z"))])
     place_of = {
         0: lambda q: 0,
         -2: lambda q: 1,
@@ -366,8 +371,7 @@
     }
 
     other_m1, other_p1 = shift(other, "z", 1), shift(other, "z", -1)
-    own, rows, other_m1, other_p1 = lax.optimization_barrier((own, rows, other_m1, other_p1))
-    beside = lax.ppermute(rows, "z", [(i, i ^ 1) for i in range(lax.axis_size("z"))])
+    own, beside, other_m1, other_p1 = lax.optimization_barrier((own, beside, other_m1, other_p1))
     rows = lax.all_gather(jnp.concatenate([rows, beside]), "x")
     own = exchanged(own, "x")
     other_m3, other_p3 = shift(other_m1, "z", 2), shift(other_p1, "z", -2)
@@ -376,7 +380,8 @@
     pieces = {0: [own], -1: [other_m1], 1: [other_p1], -3: [other_m3], 3: [other_p3]}
     pieces |= {-2: [own_m2], 2: [own_p2]}
     first_away = (0, -1, 1, -3, 3)
-    last_away = (-2, 2, 4)
+    next_away = (-2, 2)
+    last_away = (4,)
     (gradient,) = outer_sum(
         rows, [place_of[a] for a in first_away], [pieces[a] for a in first_away]
     )
@@ -385,6 +390,12 @@
     pieces[4] = [shift(up, "z", 2), shift(down, "z", -2)]
     late_inputs, gradient = lax.optimization_barrier((next_inputs[0, 0], gradient))
     tokens = lax.all_gather(late_inputs, "x")
+    (gradient,) = outer_sum(
+        rows,
+        [place_of[a] for a in next_away],
+        [pieces[a] for a in next_away],
+        before=gradient,
+    )
     gradient, squares = outer_sum(
         rows,
         [place_of[a] for a in last_away],
@@ -411,10 +422,10 @@
         tiles.append((away, [down[0][away], down[1][away]]))
     part = project(tokens, tiles)
     part, last_up, last_down = lax.optimization_barrier((part, up[0][3], down[1][3]))
-    tiles = [(4, [shift(last_up, "z", 1), shift(last_down, "z", -1)])]
-    tiles.append((-3, [up[0][3], up[1][3]]))
-    tiles.append((3, [down[0][3], down[1][3]]))
-    found = project(tokens, tiles, before=part)
+    last_tile = [shift(last_up, "z", 1), shift(last_down, "z", -1)]
+    tiles = [(-3, [up[0][3], up[1][3]]), (3, [down[0][3], down[1][3]])]
+    part = project(tokens, tiles, before=part)
+    found = project(tokens, [(4, last_tile)], before=part, last=True)
     projected = assemble(exchanged(found, "x"))
     return (
         weights_new[None, None],

time: 298 us -> 288 us (0.966)
  blocking collectives: 79.3 us -> 62.7 us
  Pallas kernels: 26.9 us -> 33.5 us
  local copies, waits for them, and re-layouts: 14.7 us -> 9.47 us
  starting transfers between devices: 44.3 us -> 48.2 us
    all_to_all x5 -> x4, blocking collectives: 79.3 us -> 62.7 us  [exchanged(): return lax.all_to_all(values, axes, 0, 0, tiled=True)]
    ppermute x1, waiting for transfers between devices: 5.91 us -> 22.3 us  [body(): lax.ppermute(rows, 'z', [(i, i ^ 1) for i in range(lax.axis_size('z'))])]
    all_gather x1, waiting for transfers between devices: 20.6 us -> 6.84 us  [body(): rows = lax.all_gather(jnp.concatenate([rows, beside]), 'x')]
    unnamed x32 -> x26, local copies, waits for them, and re-layouts: 13.7 us -> 8.43 us
    all_to_all x0 -> x1, starting transfers between devices: none -> 4.84 us  [exchanged(): return lax.all_to_all(values, axes, 0, 0, tiled=True)]
    pallas_call x2 -> x3, Pallas kernels: 9.62 us -> 13.2 us  [outer_sum(): pl.pallas_call(kernel, in_specs=in_specs, out_specs=[IN_VMEM] * len(out_s...]
    pallas_call x2 -> x3, Pallas kernels: 9.38 us -> 11.7 us  [project(): pl.pallas_call(kernel, in_specs=[ANYWHERE] * (1 + len(flat)) + [IN_VMEM]...]
  transfers between devices with their start and end apart: 28 -> 29, of which waited for: 15 -> 17; matrix products, arithmetic and copies ran while one was open for 0% -> 0% of each run, Pallas kernels for 7% -> 10%
where the time goes in v3:
time: 288 us; the launch traced here: 286 us
  waiting for transfers between devices  116 us (40%)
  blocking collectives  62.7 us (22%)
  starting transfers between devices  48.2 us (17%)
  Pallas kernels  33.5 us (12%)
  between operations  14.8 us (5%)
  local copies, waits for them, and re-layouts  9.47 us (3%)
    ppermute x25, waiting for transfers between devices, shift(): lax.ppermute(value, axis, [(i, (i + by) % size) for i in range(size)])  86.7 us
    all_to_all x4, blocking collectives, exchanged(): return lax.all_to_all(values, axes, 0, 0, tiled=True)  62.7 us
    ppermute x25, starting transfers between devices, shift(): lax.ppermute(value, axis, [(i, (i + by) % size) for i in range(size)])  41.9 us
    ppermute x1, waiting for transfers between devices, body(): lax.ppermute(rows, 'z', [(i, i ^ 1) for i in range(lax.axis_size('z'))])  22.3 us
    pallas_call x3, Pallas kernels, outer_sum(): pl.pallas_call(kernel, in_specs=in_specs, out_specs=[IN_VMEM] * len(out_s...  13.2 us
    pallas_call x3, Pallas kernels, project(): pl.pallas_call(kernel, in_specs=[ANYWHERE] * (1 + len(flat)) + [IN_VMEM]...  11.7 us
    unnamed x26, local copies, waits for them, and re-layouts  8.43 us
    all_gather x1, waiting for transfers between devices, body(): rows = lax.all_gather(jnp.concatenate([rows, beside]), 'x')  6.84 us
  transfers between devices with their start and end apart: 29, of which 17 were waited for; matrix products, arithmetic and copies ran while one was open for 0% of the time, Pallas kernels for 10%

profile of v3, /device:TPU:1, one launch (start us, length us, event | category | flops | bytes accessed | tf_op | source)
XLA Modules:
  0.0 285.8 jit_solution(18253589296593633863)
XLA Ops:
  7.8 1.3 copy-done.1
  11.2 4.8 %all-to-all-start = ((bf16[4,96,896]{2,1,0:T(8,128)(2,1)}), bf16[4,96,896]{2,1,0:T(8,128)(2,1)S(1)}, u32[]{:S(2)}, u32[]{:S(2)}) async-start(bf16[4,96,896]{2,1,0:T(8,128)(2,1)} %get-tuple-element.33), calls=%async_computation | async-start | bytes 1376256 | tf_op jit(solution)/shard_map/all_to_all | solution.py:76
  16.0 3.0 %collective-permute-start = (bf16[96,512]{1,0:T(8,128)(2,1)S(1)}, bf16[96,512]{1,0:T(8,128)(2,1)S(1)}, u32[]{:S(2)}, u32[]{:S(2)}) collective-permute-start(bf16[96,512]{1,0:T(8,128)(2,1)S(1)} %get-tuple-element.35), channel_id=1, source_target_pairs={{0,8},{4,12},{8,16},{12,20},{16,24},{20,28},{24,0},{28,4},{1,9},{5... | collective-permute-start | bytes 294920 | tf_op jit(solution)/shard_map/ppermute | solution.py:20
  19.0 3.1 %collective-permute-start.1 = (bf16[96,512]{1,0:T(8,128)(2,1)S(1)}, bf16[96,512]{1,0:T(8,128)(2,1)S(1)}, u32[]{:S(2)}, u32[]{:S(2)}) collective-permute-start(bf16[96,512]{1,0:T(8,128)(2,1)S(1)} %get-tuple-element.36), channel_id=1, source_target_pairs={{0,24},{4,28},{8,0},{12,4},{16,8},{20,12},{24,16},{28,20},{1,25},{... | collective-permute-start | bytes 294920 | tf_op jit(solution)/shard_map/ppermute | solution.py:20
  22.1 4.4 %collective-permute-start.2 = (bf16[96,512]{1,0:T(8,128)(2,1)S(1)}, bf16[96,512]{1,0:T(8,128)(2,1)S(1)}, u32[]{:S(2)}, u32[]{:S(2)}) collective-permute-start(bf16[96,512]{1,0:T(8,128)(2,1)S(1)} %get-tuple-element.37), channel_id=1, source_target_pairs={{0,16},{4,20},{8,24},{12,28},{16,0},{20,4},{24,8},{28,12},{1,17},{... | collective-permute-start | bytes 294920 | tf_op jit(solution)/shard_map/ppermute | solution.py:20
  26.5 1.5 collective-permute-done.1
  28.0 4.5 %collective-permute-done.2 = bf16[96,512]{1,0:T(8,128)(2,1)S(1)} collective-permute-done((bf16[96,512]{1,0:T(8,128)(2,1)S(1)}, bf16[96,512]{1,0:T(8,128)(2,1)S(1)}, u32[]{:S(2)}, u32[]{:S(2)}) %collective-permute-start.2) | collective-permute-done | bytes 98336 | tf_op jit(solution)/shard_map/ppermute | solution.py:20
  32.6 3.0 %collective-permute-start.4 = (bf16[4,96,896]{2,1,0:T(8,128)(2,1)S(1)}, bf16[4,96,896]{2,1,0:T(8,128)(2,1)S(1)}, u32[]{:S(2)}, u32[]{:S(2)}) collective-permute-start(bf16[4,96,896]{2,1,0:T(8,128)(2,1)S(1)} %all-to-all-done), channel_id=1, source_target_pairs={{0,4},{4,8},{8,12},{12,16},{16,20},{20,24},{24,28},{28,0},{1,5},{5... | collective-permute-start | bytes 2064392 | tf_op jit(solution)/shard_map/ppermute | solution.py:20
  35.6 1.5 collective-permute-start.3
  37.1 22.3 %collective-permute-done.3 = bf16[4,96,512]{2,1,0:T(8,128)(2,1)S(1)} collective-permute-done((bf16[4,96,512]{2,1,0:T(8,128)(2,1)S(1)}, bf16[4,96,512]{2,1,0:T(8,128)(2,1)S(1)}, u32[]{:S(2)}, u32[]{:S(2)}) %collective-permute-start.3) | collective-permute-done | bytes 393248 | tf_op jit(solution)/shard_map/ppermute | solution.py:361
  60.6 3.6 %collective-permute-start.7 = (bf16[4,96,896]{2,1,0:T(8,128)(2,1)S(1)}, bf16[4,96,896]{2,1,0:T(8,128)(2,1)S(1)}, u32[]{:S(2)}, u32[]{:S(2)}) collective-permute-start(bf16[4,96,896]{2,1,0:T(8,128)(2,1)S(1)} %collective-permute-done.5.refs_3_), channel_id=1, source_target_pairs={{0,24},{4,28},{8,0},{12,4},{16,8},{20,12},{24,16},{28,20},{1,25},{... | collective-permute-start | bytes 2064392 | tf_op jit(solution)/shard_map/ppermute | solution.py:20
  64.2 11.8 %all_to_all.25.refs_1_ = bf16[4,96,896]{2,1,0:T(8,128)(2,1)S(1)} all-to-all(bf16[4,96,896]{2,1,0:T(8,128)(2,1)S(1)} %get-tuple-element.42), channel_id=1, replica_groups=mesh['y'=4,'k'=2,'z'=8,'x'=4] {'x'}, dimensions={0} | all-to-all | bytes 1376256 | tf_op jit(solution)/shard_map/all_to_all | solution.py:76
  76.0 10.9 %collective-permute-done.6.refs_4_ = bf16[4,96,896]{2,1,0:T(8,128)(2,1)S(1)} collective-permute-done((bf16[4,96,896]{2,1,0:T(8,128)(2,1)S(1)}, bf16[4,96,896]{2,1,0:T(8,128)(2,1)S(1)}, u32[]{:S(2)}, u32[]{:S(2)}) %collective-permute-start.6) | collective-permute-done | bytes 688160 | tf_op jit(solution)/shard_map/ppermute | solution.py:20
  87.7 6.6 %collective-permute-done.7.refs_5_ = bf16[4,96,896]{2,1,0:T(8,128)(2,1)S(1)} collective-permute-done((bf16[4,96,896]{2,1,0:T(8,128)(2,1)S(1)}, bf16[4,96,896]{2,1,0:T(8,128)(2,1)S(1)}, u32[]{:S(2)}, u32[]{:S(2)}) %collective-permute-start.7) | collective-permute-done | bytes 688160 | tf_op jit(solution)/shard_map/ppermute | solution.py:20
  95.1 3.3 %collective-permute-start.10 = (bf16[4,96,896]{2,1,0:T(8,128)(2,1)S(1)}, bf16[4,96,896]{2,1,0:T(8,128)(2,1)S(1)}, u32[]{:S(2)}, u32[]{:S(2)}) collective-permute-start(bf16[4,96,896]{2,1,0:T(8,128)(2,1)S(1)} %all_to_all.25.refs_1_), channel_id=1, source_target_pairs={{0,24},{4,28},{8,0},{12,4},{16,8},{20,12},{24,16},{28,20},{1,25},{... | collective-permute-start | bytes 2064392 | tf_op jit(solution)/shard_map/ppermute | solution.py:20
  98.5 6.8 %all-gather.5.cloned.1.call-done = bf16[32,96,512]{2,1,0:T(8,128)(2,1)} async-done(((bf16[8,96,512]{2,1,0:T(8,128)(2,1)}), bf16[32,96,512]{2,1,0:T(8,128)(2,1)}) %all-gather.5.cloned.1.call-update) | async-done | bytes 3145744 | tf_op jit(solution)/shard_map/all_gather | solution.py:375
  105.3 1.1 copy-done.5
  106.4 1.1 copy-done.7
  107.5 1.1 copy-done.9
  109.7 7.1 %outer_first.1.refs_3_ = f32[512,896]{1,0:T(8,128)S(1)} custom-call(bf16[4,8,96,512]{3,2,1,0:T(8,128)(2,1)} %bitcast.23, bf16[4,96,896]{2,1,0:T(8,128)(2,1)S(1)} %all_to_all.25.refs_1_, bf16[4,96,896]{2,1,0:T(8,128)(2,1)S(1)} %copy-done.5, bf16[4,96,896]{2,1,0:T(8,128)(2,1)S(1)} %copy-done.7, bf16[4,96,896]{2,1,0:T(8,128)(2,1)S(1)} %copy-done.9, ...), custom_call_target="tpu_custom_call" | custom-call | flops 1761607680 | bytes 7241728 | tf_op jit(solution)/shard_map/outer_first/pallas_call | solution.py:233
  116.8 11.1 %collective-permute-done.10.refs_2_ = bf16[4,96,896]{2,1,0:T(8,128)(2,1)S(1)} collective-permute-done((bf16[4,96,896]{2,1,0:T(8,128)(2,1)S(1)}, bf16[4,96,896]{2,1,0:T(8,128)(2,1)S(1)}, u32[]{:S(2)}, u32[]{:S(2)}) %collective-permute-start.10) | collective-permute-done | bytes 688160 | tf_op jit(solution)/shard_map/ppermute | solution.py:20
  128.0 1.7 collective-permute-start.11
  132.0 3.5 %outer_next.1.refs_3_ = f32[512,896]{1,0:T(8,128)S(1)} custom-call(bf16[4,8,96,512]{3,2,1,0:T(8,128)(2,1)} %bitcast.24, bf16[4,96,896]{2,1,0:T(8,128)(2,1)} %collective-permute-done.8.refs_1_, bf16[4,96,896]{2,1,0:T(8,128)(2,1)S(1)} %collective-permute-done.10.refs_2_, f32[512,896]{1,0:T(8,128)S(1)} %outer_first.1.refs_3_), custom_call_target="tpu_custom_call", output_to_operand_aliasing={{}: (3, {})} | custom-call | flops 704643072 | bytes 3997696 | tf_op jit(solution)/shard_map/outer_next/pallas_call | solution.py:233
  135.5 7.9 %collective-permute-done.11.refs_2_ = bf16[2,96,896]{2,1,0:T(8,128)(2,1)S(1)} collective-permute-done((bf16[2,96,896]{2,1,0:T(8,128)(2,1)S(1)}, bf16[2,96,896]{2,1,0:T(8,128)(2,1)S(1)}, u32[]{:S(2)}, u32[]{:S(2)}) %collective-permute-start.11) | collective-permute-done | bytes 344096 | tf_op jit(solution)/shard_map/ppermute | solution.py:20
  143.4 2.3 collective-permute-done.9.refs_1_
  145.7 2.6 outer_last.1
  148.3 21.2 %all_to_all.26.n_ref = f32[256,1,128]{2,1,0:T(1,128)S(1)} all-to-all(f32[256,1,128]{2,1,0:T(1,128)S(1)} %get-tuple-element.49), channel_id=1, replica_groups=mesh['y'=4,'k'=2,'z'=8,'x'=4] {'y','k','z','x'}, dimensions={0} | all-to-all | bytes 262144 | tf_op jit(solution)/shard_map/all_to_all | solution.py:76
  169.5 4.3 %update_of.1 = (f32[512,896]{1,0:T(8,128)S(1)}, bf16[512,896]{1,0:T(8,128)(2,1)}, bf16[512,896]{1,0:T(8,128)(2,1)}, f32[32,2,128]{2,1,0:T(2,128)S(1)}) custom-call(f32[256,1,128]{2,1,0:T(1,128)S(1)} %all_to_all.26.n_ref, f32[512,896]{1,0:T(8,128)S(1)} %get-tuple-element.50.g_ref, f32[512,896]{1,0:T(8,128)S(1)} %bitcast.16, bf16[512,896]{1,0:T(8,128)(2,1)S(1)} %bitcast.19, ...), custom_call_target="tpu_custom_call" | custom-call | tf_op jit(solution)/shard_map/update_of/pallas_call | solution.py:113
  173.8 12.0 %all_to_all.27.sums_ref = f32[32,2,128]{2,1,0:T(2,128)S(1)} all-to-all(f32[32,2,128]{2,1,0:T(2,128)S(1)} %get-tuple-element.51), channel_id=1, replica_groups=mesh['y'=4,'k'=2,'z'=8,'x'=4] {'z','x'}, dimensions={0} | all-to-all | bytes 65536 | tf_op jit(solution)/shard_map/all_to_all | solution.py:76
  185.8 2.1 weights_of.1
  188.3 2.3 collective-permute-start.18
  190.6 2.7 collective-permute-start.16
  193.3 5.6 %collective-permute-done.12.refs_7_ = bf16[256,896]{1,0:T(8,128)(2,1)S(1)} collective-permute-done((bf16[256,896]{1,0:T(8,128)(2,1)S(1)}, bf16[256,896]{1,0:T(8,128)(2,1)S(1)}, u32[]{:S(2)}, u32[]{:S(2)}) %collective-permute-start.12) | collective-permute-done | bytes 458784 | tf_op jit(solution)/shard_map/ppermute | solution.py:20
  198.9 2.7 collective-permute-start.19
  201.6 7.1 %collective-permute-done.14.refs_8_ = bf16[256,896]{1,0:T(8,128)(2,1)S(1)} collective-permute-done((bf16[256,896]{1,0:T(8,128)(2,1)S(1)}, bf16[256,896]{1,0:T(8,128)(2,1)S(1)}, u32[]{:S(2)}, u32[]{:S(2)}) %collective-permute-start.14) | collective-permute-done | bytes 458784 | tf_op jit(solution)/shard_map/ppermute | solution.py:20
  208.7 2.7 collective-permute-start.17
  211.4 7.3 %collective-permute-done.13.refs_3_ = bf16[256,896]{1,0:T(8,128)(2,1)} collective-permute-done((bf16[256,896]{1,0:T(8,128)(2,1)S(1)}, bf16[256,896]{1,0:T(8,128)(2,1)}, u32[]{:S(2)}, u32[]{:S(2)}) %collective-permute-start.13) | collective-permute-done | bytes 458784 | tf_op jit(solution)/shard_map/ppermute | solution.py:20
  218.7 2.7 collective-permute-start.21
  221.3 7.0 %collective-permute-done.15.refs_4_ = bf16[256,896]{1,0:T(8,128)(2,1)S(1)} collective-permute-done((bf16[256,896]{1,0:T(8,128)(2,1)S(1)}, bf16[256,896]{1,0:T(8,128)(2,1)S(1)}, u32[]{:S(2)}, u32[]{:S(2)}) %collective-permute-start.15) | collective-permute-done | bytes 458784 | tf_op jit(solution)/shard_map/ppermute | solution.py:20
  228.4 2.7 collective-permute-start.25
  231.1 6.4 %project_first.1.refs_5_ = f32[2,384,896]{2,1,0:T(8,128)S(1)} custom-call(bf16[4,96,2048]{2,1,0:T(8,128)(2,1)} %bitcast.26, bf16[256,896]{1,0:T(8,128)(2,1)S(1)} %get-tuple-element.57.refs_1_, bf16[256,896]{1,0:T(8,128)(2,1)S(1)} %get-tuple-element.58.refs_2_, bf16[256,896]{1,0:T(8,128)(2,1)} %collective-permute-done.13.refs_3_, ...), custom_call_target="tpu_custom_call" | custom-call | flops 1761607680 | bytes 6553600 | tf_op jit(solution)/shard_map/project_first/pallas_call | solution.py:306
  238.3 2.7 collective-permute-start.23
  241.0 7.1 %collective-permute-done.24.refs_2_ = bf16[256,896]{1,0:T(8,128)(2,1)} collective-permute-done((bf16[256,896]{1,0:T(8,128)(2,1)S(1)}, bf16[256,896]{1,0:T(8,128)(2,1)}, u32[]{:S(2)}, u32[]{:S(2)}) %collective-permute-start.24) | collective-permute-done | bytes 458784 | tf_op jit(solution)/shard_map/ppermute | solution.py:20
  248.1 3.1 %project_next.1.refs_3_ = f32[2,384,896]{2,1,0:T(8,128)S(1)} custom-call(bf16[4,96,2048]{2,1,0:T(8,128)(2,1)} %bitcast.27, bf16[256,896]{1,0:T(8,128)(2,1)} %collective-permute-done.20.refs_1_, bf16[256,896]{1,0:T(8,128)(2,1)} %collective-permute-done.24.refs_2_, bf16[256,896]{1,0:T(8,128)(2,1)} %collective-permute-done.25.refs_3_, ...), custom_call_target="tpu_custom_call" | custom-call | flops 704643072 | bytes 2621440 | tf_op jit(solution)/shard_map/project_next/pallas_call | solution.py:306
  251.3 6.6 %collective-permute-done.22.refs_1_ = bf16[256,896]{1,0:T(8,128)(2,1)S(1)} collective-permute-done((bf16[256,896]{1,0:T(8,128)(2,1)}, bf16[256,896]{1,0:T(8,128)(2,1)S(1)}, u32[]{:S(2)}, u32[]{:S(2)}) %collective-permute-start.22) | collective-permute-done | bytes 458784 | tf_op jit(solution)/shard_map/ppermute | solution.py:20
  257.9 2.2 project_last.1
  260.1 17.7 %all_to_all.28.found_ref = bf16[4,2,96,896]{3,2,1,0:T(8,128)(2,1)S(1)} all-to-all(bf16[4,2,96,896]{3,2,1,0:T(8,128)(2,1)S(1)} %project_last.1), channel_id=1, replica_groups=mesh['y'=4,'k'=2,'z'=8,'x'=4] {'x'}, dimensions={0} | all-to-all | bytes 2752512 | tf_op jit(solution)/shard_map/all_to_all | solution.py:76
  277.8 1.2 assemble.1
  (56 shorter events, 9.6 us)
Async XLA Ops:
  7.8 1.3 copy-start.1
  9.2 1.0 copy-start.12
  11.2 21.4 %all-to-all-start = ((bf16[4,96,896]{2,1,0:T(8,128)(2,1)}), bf16[4,96,896]{2,1,0:T(8,128)(2,1)S(1)}, u32[]{:S(2)}, u32[]{:S(2)}) async-start(bf16[4,96,896]{2,1,0:T(8,128)(2,1)} %get-tuple-element.33), calls=%async_computation | async-start | bytes 1376256 | tf_op jit(solution)/shard_map/all_to_all | solution.py:76
  16.0 89.3 %all-gather.5.cloned.1.call-start = ((), (), s32[]{:S(2)}) async-start(), calls=%async_computation.5 | async-start | bytes 3932160 | tf_op jit(solution)/shard_map/all_gather | solution.py:375
  16.0 10.5 %collective-permute-start = (bf16[96,512]{1,0:T(8,128)(2,1)S(1)}, bf16[96,512]{1,0:T(8,128)(2,1)S(1)}, u32[]{:S(2)}, u32[]{:S(2)}) collective-permute-start(bf16[96,512]{1,0:T(8,128)(2,1)S(1)} %get-tuple-element.35), channel_id=1, source_target_pairs={{0,8},{4,12},{8,16},{12,20},{16,24},{20,28},{24,0},{28,4},{1,9},{5... | collective-permute-start | bytes 294920 | tf_op jit(solution)/shard_map/ppermute | solution.py:20
  19.0 9.0 %collective-permute-start.1 = (bf16[96,512]{1,0:T(8,128)(2,1)S(1)}, bf16[96,512]{1,0:T(8,128)(2,1)S(1)}, u32[]{:S(2)}, u32[]{:S(2)}) collective-permute-start(bf16[96,512]{1,0:T(8,128)(2,1)S(1)} %get-tuple-element.36), channel_id=1, source_target_pairs={{0,24},{4,28},{8,0},{12,4},{16,8},{20,12},{24,16},{28,20},{1,25},{... | collective-permute-start | bytes 294920 | tf_op jit(solution)/shard_map/ppermute | solution.py:20
  22.1 10.4 %collective-permute-start.2 = (bf16[96,512]{1,0:T(8,128)(2,1)S(1)}, bf16[96,512]{1,0:T(8,128)(2,1)S(1)}, u32[]{:S(2)}, u32[]{:S(2)}) collective-permute-start(bf16[96,512]{1,0:T(8,128)(2,1)S(1)} %get-tuple-element.37), channel_id=1, source_target_pairs={{0,16},{4,20},{8,24},{12,28},{16,0},{20,4},{24,8},{28,12},{1,17},{... | collective-permute-start | bytes 294920 | tf_op jit(solution)/shard_map/ppermute | solution.py:20
  32.6 26.8 %collective-permute-start.4 = (bf16[4,96,896]{2,1,0:T(8,128)(2,1)S(1)}, bf16[4,96,896]{2,1,0:T(8,128)(2,1)S(1)}, u32[]{:S(2)}, u32[]{:S(2)}) collective-permute-start(bf16[4,96,896]{2,1,0:T(8,128)(2,1)S(1)} %all-to-all-done), channel_id=1, source_target_pairs={{0,4},{4,8},{8,12},{12,16},{16,20},{20,24},{24,28},{28,0},{1,5},{5... | collective-permute-start | bytes 2064392 | tf_op jit(solution)/shard_map/ppermute | solution.py:20
  35.6 23.8 %collective-permute-start.5 = (bf16[4,96,896]{2,1,0:T(8,128)(2,1)S(1)}, bf16[4,96,896]{2,1,0:T(8,128)(2,1)S(1)}, u32[]{:S(2)}, u32[]{:S(2)}) collective-permute-start(bf16[4,96,896]{2,1,0:T(8,128)(2,1)S(1)} %all-to-all-done), channel_id=1, source_target_pairs={{0,28},{4,0},{8,4},{12,8},{16,12},{20,16},{24,20},{28,24},{1,29},{... | collective-permute-start | bytes 2064392 | tf_op jit(solution)/shard_map/ppermute | solution.py:20
  35.6 23.8 %collective-permute-start.3 = (bf16[4,96,512]{2,1,0:T(8,128)(2,1)S(1)}, bf16[4,96,512]{2,1,0:T(8,128)(2,1)S(1)}, u32[]{:S(2)}, u32[]{:S(2)}) collective-permute-start(bf16[4,96,512]{2,1,0:T(8,128)(2,1)S(1)} %pad_maximum_fusion.1), channel_id=1, source_target_pairs={{0,4},{4,0},{8,12},{12,8},{16,20},{20,16},{24,28},{28,24},{1,5},{5... | collective-permute-start | bytes 1179656 | tf_op jit(solution)/shard_map/ppermute | solution.py:361
  59.4 16.6 %copy-start.4 = (bf16[4,96,896]{2,1,0:T(8,128)(2,1)}, bf16[4,96,896]{2,1,0:T(8,128)(2,1)S(1)}, u32[]{:S(2)}) copy-start(bf16[4,96,896]{2,1,0:T(8,128)(2,1)S(1)} %collective-permute-done.4.refs_2_) | copy-start | bytes 2064388
  59.4 16.6 %copy-start.6 = (bf16[4,96,896]{2,1,0:T(8,128)(2,1)}, bf16[4,96,896]{2,1,0:T(8,128)(2,1)S(1)}, u32[]{:S(2)}) copy-start(bf16[4,96,896]{2,1,0:T(8,128)(2,1)S(1)} %collective-permute-done.5.refs_3_) | copy-start | bytes 2064388
  60.5 170.6 %all-gather.7.cloned.1.call-start = ((), (), s32[]{:S(2)}) async-start(), calls=%async_computation.6 | async-start | bytes 1966080 | tf_op jit(solution)/shard_map/all_gather | solution.py:392
  60.5 26.3 %collective-permute-start.6 = (bf16[4,96,896]{2,1,0:T(8,128)(2,1)S(1)}, bf16[4,96,896]{2,1,0:T(8,128)(2,1)S(1)}, u32[]{:S(2)}, u32[]{:S(2)}) collective-permute-start(bf16[4,96,896]{2,1,0:T(8,128)(2,1)S(1)} %collective-permute-done.4.refs_2_), channel_id=1, source_target_pairs={{0,8},{4,12},{8,16},{12,20},{16,24},{20,28},{24,0},{28,4},{1,9},{5... | collective-permute-start | bytes 2064392 | tf_op jit(solution)/shard_map/ppermute | solution.py:20
  60.6 33.7 %collective-permute-start.7 = (bf16[4,96,896]{2,1,0:T(8,128)(2,1)S(1)}, bf16[4,96,896]{2,1,0:T(8,128)(2,1)S(1)}, u32[]{:S(2)}, u32[]{:S(2)}) collective-permute-start(bf16[4,96,896]{2,1,0:T(8,128)(2,1)S(1)} %collective-permute-done.5.refs_3_), channel_id=1, source_target_pairs={{0,24},{4,28},{8,0},{12,4},{16,8},{20,12},{24,16},{28,20},{1,25},{... | collective-permute-start | bytes 2064392 | tf_op jit(solution)/shard_map/ppermute | solution.py:20
  86.9 0.8 copy-start.8
  94.3 0.8 copy-start.10
  95.1 32.8 %collective-permute-start.10 = (bf16[4,96,896]{2,1,0:T(8,128)(2,1)S(1)}, bf16[4,96,896]{2,1,0:T(8,128)(2,1)S(1)}, u32[]{:S(2)}, u32[]{:S(2)}) collective-permute-start(bf16[4,96,896]{2,1,0:T(8,128)(2,1)S(1)} %all_to_all.25.refs_1_), channel_id=1, source_target_pairs={{0,24},{4,28},{8,0},{12,4},{16,8},{20,12},{24,16},{28,20},{1,25},{... | collective-permute-start | bytes 2064392 | tf_op jit(solution)/shard_map/ppermute | solution.py:20
  98.5 31.5 %collective-permute-start.8 = (bf16[4,96,896]{2,1,0:T(8,128)(2,1)S(1)}, bf16[4,96,896]{2,1,0:T(8,128)(2,1)}, u32[]{:S(2)}, u32[]{:S(2)}) collective-permute-start(bf16[4,96,896]{2,1,0:T(8,128)(2,1)S(1)} %all_to_all.25.refs_1_), channel_id=1, source_target_pairs={{0,8},{4,12},{8,16},{12,20},{16,24},{20,28},{24,0},{28,4},{1,9},{5... | collective-permute-start | bytes 2064392 | tf_op jit(solution)/shard_map/ppermute | solution.py:20
  105.3 1.1 copy-start.5
  106.4 1.1 copy-start.7
  107.5 1.1 copy-start.9
  108.6 1.1 copy-start.11
  128.0 15.4 %collective-permute-start.11 = (bf16[2,96,896]{2,1,0:T(8,128)(2,1)S(1)}, bf16[2,96,896]{2,1,0:T(8,128)(2,1)S(1)}, u32[]{:S(2)}, u32[]{:S(2)}) collective-permute-start(bf16[2,96,896]{2,1,0:T(8,128)(2,1)S(1)} %slice.9), channel_id=1, source_target_pairs={{0,24},{4,28},{8,0},{12,4},{16,8},{20,12},{24,16},{28,20},{1,25},{... | collective-permute-start | bytes 1032200 | tf_op jit(solution)/shard_map/ppermute | solution.py:20
  131.0 14.7 %collective-permute-start.9 = (bf16[2,96,896]{2,1,0:T(8,128)(2,1)S(1)}, bf16[2,96,896]{2,1,0:T(8,128)(2,1)S(1)}, u32[]{:S(2)}, u32[]{:S(2)}) collective-permute-start(bf16[2,96,896]{2,1,0:T(8,128)(2,1)S(1)} %slice.8), channel_id=1, source_target_pairs={{0,8},{4,12},{8,16},{12,20},{16,24},{20,28},{24,0},{28,4},{1,9},{5... | collective-permute-start | bytes 1032200 | tf_op jit(solution)/shard_map/ppermute | solution.py:20
  135.4 34.1 %copy-start = (f32[1,1,512,896]{3,2,1,0:T(8,128)S(1)}, f32[1,1,512,896]{3,2,1,0:T(8,128)}, u32[]{:S(2)}) copy-start(f32[1,1,512,896]{3,2,1,0:T(8,128)} %param.11) | copy-start | bytes 5505028
  135.5 34.0 %copy-start.2 = (bf16[1,1,512,896]{3,2,1,0:T(8,128)(2,1)S(1)}, bf16[1,1,512,896]{3,2,1,0:T(8,128)(2,1)}, u32[]{:S(2)}) copy-start(bf16[1,1,512,896]{3,2,1,0:T(8,128)(2,1)} %param.12) | copy-start | bytes 2752516
  135.5 34.0 %copy-start.3 = (bf16[1,1,512,896]{3,2,1,0:T(8,128)(2,1)S(1)}, bf16[1,1,512,896]{3,2,1,0:T(8,128)(2,1)}, u32[]{:S(2)}) copy-start(bf16[1,1,512,896]{3,2,1,0:T(8,128)(2,1)} %param.13) | copy-start | bytes 2752516
  187.9 11.0 %collective-permute-start.12 = (bf16[256,896]{1,0:T(8,128)(2,1)S(1)}, bf16[256,896]{1,0:T(8,128)(2,1)S(1)}, u32[]{:S(2)}, u32[]{:S(2)}) collective-permute-start(bf16[256,896]{1,0:T(8,128)(2,1)S(1)} %get-tuple-element.57.refs_1_), channel_id=1, source_target_pairs={{0,4},{4,8},{8,12},{12,16},{16,20},{20,24},{24,28},{28,0},{1,5},{5... | collective-permute-start | bytes 1376264 | tf_op jit(solution)/shard_map/ppermute | solution.py:20
  188.3 10.6 %collective-permute-start.18 = (bf16[256,896]{1,0:T(8,128)(2,1)S(1)}, bf16[256,896]{1,0:T(8,128)(2,1)S(1)}, u32[]{:S(2)}, u32[]{:S(2)}) collective-permute-start(bf16[256,896]{1,0:T(8,128)(2,1)S(1)} %get-tuple-element.58.refs_2_), channel_id=1, source_target_pairs={{0,28},{4,0},{8,4},{12,8},{16,12},{20,16},{24,20},{28,24},{1,29},{... | collective-permute-start | bytes 1376264 | tf_op jit(solution)/shard_map/ppermute | solution.py:20
  190.6 18.1 %collective-permute-start.14 = (bf16[256,896]{1,0:T(8,128)(2,1)S(1)}, bf16[256,896]{1,0:T(8,128)(2,1)S(1)}, u32[]{:S(2)}, u32[]{:S(2)}) collective-permute-start(bf16[256,896]{1,0:T(8,128)(2,1)S(1)} %get-tuple-element.58.refs_2_), channel_id=1, source_target_pairs={{0,4},{4,8},{8,12},{12,16},{16,20},{20,24},{24,28},{28,0},{1,5},{5... | collective-permute-start | bytes 1376264 | tf_op jit(solution)/shard_map/ppermute | solution.py:20
  190.6 18.1 %collective-permute-start.16 = (bf16[256,896]{1,0:T(8,128)(2,1)S(1)}, bf16[256,896]{1,0:T(8,128)(2,1)S(1)}, u32[]{:S(2)}, u32[]{:S(2)}) collective-permute-start(bf16[256,896]{1,0:T(8,128)(2,1)S(1)} %get-tuple-element.57.refs_1_), channel_id=1, source_target_pairs={{0,28},{4,0},{8,4},{12,8},{16,12},{20,16},{24,20},{28,24},{1,29},{... | collective-permute-start | bytes 1376264 | tf_op jit(solution)/shard_map/ppermute | solution.py:20
  198.9 19.8 %collective-permute-start.13 = (bf16[256,896]{1,0:T(8,128)(2,1)S(1)}, bf16[256,896]{1,0:T(8,128)(2,1)}, u32[]{:S(2)}, u32[]{:S(2)}) collective-permute-start(bf16[256,896]{1,0:T(8,128)(2,1)S(1)} %collective-permute-done.12.refs_7_), channel_id=1, source_target_pairs={{0,4},{4,8},{8,12},{12,16},{16,20},{20,24},{24,28},{28,0},{1,5},{5... | collective-permute-start | bytes 1376264 | tf_op jit(solution)/shard_map/ppermute | solution.py:20
  198.9 19.8 %collective-permute-start.19 = (bf16[256,896]{1,0:T(8,128)(2,1)S(1)}, bf16[256,896]{1,0:T(8,128)(2,1)}, u32[]{:S(2)}, u32[]{:S(2)}) collective-permute-start(bf16[256,896]{1,0:T(8,128)(2,1)S(1)} %collective-permute-done.18.refs_10_), channel_id=1, source_target_pairs={{0,28},{4,0},{8,4},{12,8},{16,12},{20,16},{24,20},{28,24},{1,29},{... | collective-permute-start | bytes 1376264 | tf_op jit(solution)/shard_map/ppermute | solution.py:20
  208.7 19.7 %collective-permute-start.15 = (bf16[256,896]{1,0:T(8,128)(2,1)S(1)}, bf16[256,896]{1,0:T(8,128)(2,1)S(1)}, u32[]{:S(2)}, u32[]{:S(2)}) collective-permute-start(bf16[256,896]{1,0:T(8,128)(2,1)S(1)} %collective-permute-done.14.refs_8_), channel_id=1, source_target_pairs={{0,4},{4,8},{8,12},{12,16},{16,20},{20,24},{24,28},{28,0},{1,5},{5... | collective-permute-start | bytes 1376264 | tf_op jit(solution)/shard_map/ppermute | solution.py:20
  208.7 19.7 %collective-permute-start.17 = (bf16[256,896]{1,0:T(8,128)(2,1)S(1)}, bf16[256,896]{1,0:T(8,128)(2,1)}, u32[]{:S(2)}, u32[]{:S(2)}) collective-permute-start(bf16[256,896]{1,0:T(8,128)(2,1)S(1)} %collective-permute-done.16.refs_9_), channel_id=1, source_target_pairs={{0,28},{4,0},{8,4},{12,8},{16,12},{20,16},{24,20},{28,24},{1,29},{... | collective-permute-start | bytes 1376264 | tf_op jit(solution)/shard_map/ppermute | solution.py:20
  218.6 19.7 %collective-permute-start.20 = (bf16[256,896]{1,0:T(8,128)(2,1)}, bf16[256,896]{1,0:T(8,128)(2,1)}, u32[]{:S(2)}, u32[]{:S(2)}) collective-permute-start(bf16[256,896]{1,0:T(8,128)(2,1)} %collective-permute-done.13.refs_3_), channel_id=1, source_target_pairs={{0,4},{4,8},{8,12},{12,16},{16,20},{20,24},{24,28},{28,0},{1,5},{5... | collective-permute-start | bytes 1376264 | tf_op jit(solution)/shard_map/ppermute | solution.py:20
  218.7 19.7 %collective-permute-start.21 = (bf16[256,896]{1,0:T(8,128)(2,1)}, bf16[256,896]{1,0:T(8,128)(2,1)}, u32[]{:S(2)}, u32[]{:S(2)}) collective-permute-start(bf16[256,896]{1,0:T(8,128)(2,1)} %collective-permute-done.19.refs_6_), channel_id=1, source_target_pairs={{0,28},{4,0},{8,4},{12,8},{16,12},{20,16},{24,20},{28,24},{1,29},{... | collective-permute-start | bytes 1376264 | tf_op jit(solution)/shard_map/ppermute | solution.py:20
  228.4 19.8 %collective-permute-start.24 = (bf16[256,896]{1,0:T(8,128)(2,1)S(1)}, bf16[256,896]{1,0:T(8,128)(2,1)}, u32[]{:S(2)}, u32[]{:S(2)}) collective-permute-start(bf16[256,896]{1,0:T(8,128)(2,1)S(1)} %collective-permute-done.15.refs_4_), channel_id=1, source_target_pairs={{0,4},{4,8},{8,12},{12,16},{16,20},{20,24},{24,28},{28,0},{1,5},{5... | collective-permute-start | bytes 1376264 | tf_op jit(solution)/shard_map/ppermute | solution.py:20
  228.4 19.8 %collective-permute-start.25 = (bf16[256,896]{1,0:T(8,128)(2,1)}, bf16[256,896]{1,0:T(8,128)(2,1)}, u32[]{:S(2)}, u32[]{:S(2)}) collective-permute-start(bf16[256,896]{1,0:T(8,128)(2,1)} %collective-permute-done.17.refs_5_), channel_id=1, source_target_pairs={{0,28},{4,0},{8,4},{12,8},{16,12},{20,16},{24,20},{28,24},{1,29},{... | collective-permute-start | bytes 1376264 | tf_op jit(solution)/shard_map/ppermute | solution.py:20
  238.3 19.6 %collective-permute-start.22 = (bf16[256,896]{1,0:T(8,128)(2,1)}, bf16[256,896]{1,0:T(8,128)(2,1)S(1)}, u32[]{:S(2)}, u32[]{:S(2)}) collective-permute-start(bf16[256,896]{1,0:T(8,128)(2,1)} %collective-permute-done.20.refs_1_), channel_id=1, source_target_pairs={{0,4},{4,8},{8,12},{12,16},{16,20},{20,24},{24,28},{28,0},{1,5},{5... | collective-permute-start | bytes 1376264 | tf_op jit(solution)/shard_map/ppermute | solution.py:20
  238.3 19.6 %collective-permute-start.23 = (bf16[256,896]{1,0:T(8,128)(2,1)}, bf16[256,896]{1,0:T(8,128)(2,1)S(1)}, u32[]{:S(2)}, u32[]{:S(2)}) collective-permute-start(bf16[256,896]{1,0:T(8,128)(2,1)} %collective-permute-done.21.refs_4_), channel_id=1, source_target_pairs={{0,28},{4,0},{8,4},{12,8},{16,12},{20,16},{24,20},{28,24},{1,29},{... | collective-permute-start | bytes 1376264 | tf_op jit(solution)/shard_map/ppermute | solution.py:20
Sparse Core Ops, SparseCore 0:
  60.6 44.6 all-gather.4
  116.9 25.9 all-gather.6

commit v4 on v3

--- a/solution.py
+++ b/solution.py
@@ -11,13 +11,14 @@
 GRID_R = 4
 GRID_C = 8
 EXPERT = ("y", "k")
-SHARD = ("z", "x")
-EVERYONE = ("y", "k", "z", "x")
-
-
-def shift(value, axis, by):
-    size = lax.axis_size(axis)
-    return lax.ppermute(value, axis, [(i, (i + by) % size) for i in range(size)])
+SHARD = ("r", "q", "x")
+EVERYONE = ("y", "k", "r", "q", "x")
+Z = ("r", "q")
+
+
+def shift(value, by):
+    size = lax.axis_size(Z)
+    return lax.ppermute(value, Z, [(i, (i + by) % size) for i in range(size)])
 
 
 VMEM_LIMIT = 20 << 20
@@ -31,11 +32,10 @@
     size_x = out_grads.shape[1] // (2 * f_blk)
 
     def kernel(count_ref, rows_ref, cols_ref, own_ref, other_ref, *row_refs):
-        z = lax.axis_index("z")
-        q = lax.rem(z, 2)
+        q = lax.axis_index("q")
         valid = lax.broadcasted_iota(jnp.int32, (cap, f_blk), 0) < count_ref[0, 0]
         for i, by in enumerate((0, 1, 3, 2)):
-            start = pl.multiple_of(lax.rem(z // 2 + by, GRID_R) * d_blk, 128)
+            start = pl.multiple_of(lax.rem(lax.axis_index("r") + by, GRID_R) * d_blk, 128)
             row_refs[i][...] = rows_ref[:, pl.ds(start, d_blk)]
         for ref, parity in ((own_ref, q), (other_ref, 1 - q)):
             for to_x in range(size_x):
@@ -186,7 +186,7 @@
         total_ref = refs.pop(0)
         square_ref = refs.pop(0) if last else None
         left, right, sems = refs
-        q = lax.rem(lax.axis_index("z"), 2)
+        q = lax.axis_index("q")
         copies = []
         at = 0
         for i, piece in enumerate(pieces):
@@ -252,14 +252,11 @@
 
 
 def project(tokens, tiles, before=None, last=False):
-    size_x, cap, d = tokens.shape
+    shards, cap, d = tokens.shape
     d_blk = d // GRID_R
     f_blk = tiles[0][1][0].shape[-1]
     flat = [part for _, piece in tiles for part in piece]
-    evens = [i for i, (away, _) in enumerate(tiles) if away % 2 == 0]
-    odds = [i for i, (away, _) in enumerate(tiles) if away % 2]
-    assert evens + odds == list(range(len(tiles)))
-    count = size_x * cap
+    count = shards * cap
     n = len(tiles)
 
     def kernel(*refs):
@@ -268,7 +265,6 @@
         flat_refs = [refs.pop(0) for _ in flat]
         before_ref = None if before is None else refs.pop(0)
         out_ref, left, right, total, sems = refs
-        z = lax.axis_index("z")
         copies = []
         at = 0
         for i, (away, piece) in enumerate(tiles):
@@ -278,38 +274,42 @@
                 copies.append((flat_refs[at], right.at[i, pl.ds(start, size)]))
                 start += size
                 at += 1
-            block = lax.rem(z + away + 8, 8) // 2
+            block = lax.rem(lax.axis_index("r") + away, GRID_R)
             columns = pl.ds(pl.multiple_of(block * d_blk, 128), d_blk)
             copies.append((tokens_ref.at[:, :, columns], left.at[i]))
         fetch(copies, sems)
-
-        def add(i, carry):
-            total[...] += jnp.dot(
-                left[i].reshape(count, d_blk), right[i], preferred_element_type=jnp.float32
+        total[...] = jnp.zeros_like(total) if before is None else before_ref[...]
+        half = shards // 2
+
+        def add(step, carry):
+            i, here = step // 2, lax.rem(step, 2)
+            rows = pl.ds(pl.multiple_of(here * half * cap, 8), half * cap)
+            total[rows, :] += jnp.dot(
+                left[i, pl.ds(here * half, half)].reshape(half * cap, d_blk),
+                right[i],
+                preferred_element_type=jnp.float32,
             )
             return carry
 
-        for i, steps in enumerate(((0, len(evens)), (len(evens), n))):
-            total[...] = jnp.zeros_like(total) if before is None else before_ref[i]
-            if steps[0] < steps[1]:
-                lax.fori_loop(*steps, add, 0)
-            if last:
-                out_ref[:, i] = total[...].astype(jnp.bfloat16).reshape(size_x, cap, f_blk)
-            else:
-                out_ref[i] = total[...]
+        lax.fori_loop(0, 2 * n, add, 0)
+        if last:
+            out_ref[...] = total[...].astype(jnp.bfloat16).reshape(shards, cap, f_blk)
+        else:
+            out_ref[...] = total[...]
 
     if last:
-        out_shape = jax.ShapeDtypeStruct((size_x, 2, cap, f_blk), jnp.bfloat16)
+        out_shape = jax.ShapeDtypeStruct((shards, cap, f_blk), jnp.bfloat16)
     else:
-        out_shape = jax.ShapeDtypeStruct((2, count, f_blk), jnp.float32)
-    operands = [pltpu.with_memory_space_constraint(tokens, pltpu.HBM), *flat] + ([] if before is None else [before])
+        out_shape = jax.ShapeDtypeStruct((count, f_blk), jnp.float32)
+    operands = [pltpu.with_memory_space_constraint(tokens, pltpu.HBM), *flat]
+    operands += [] if before is None else [before]
     return pl.pallas_call(
         kernel,
         in_specs=[ANYWHERE] * (1 + len(flat)) + [IN_VMEM] * (len(operands) - 1 - len(flat)),
         out_specs=IN_VMEM,
         out_shape=out_shape,
         scratch_shapes=[
-            pltpu.VMEM((n, size_x, cap, d_blk), jnp.bfloat16),
+            pltpu.VMEM((n, shards, cap, d_blk), jnp.bfloat16),
             pltpu.VMEM((n, d_blk, f_blk), jnp.bfloat16),
             pltpu.VMEM((count, f_blk), jnp.float32),
             pltpu.SemaphoreType.DMA((len(flat) + n,)),
@@ -325,21 +325,17 @@
 
 
 def assemble(found):
-    size_x, _, cap, f_blk = found.shape
+    blocks, cap, f_blk = found.shape
 
     def kernel(found_ref, out_ref):
-        q = lax.rem(lax.axis_index("z"), 2)
-        for i in range(2):
-            parity = q if i == 0 else 1 - q
-            for j in range(size_x):
-                start = pl.multiple_of((parity * size_x + j) * f_blk, 128)
-                out_ref[:, pl.ds(start, f_blk)] = found_ref[j, i]
+        for i in range(blocks):
+            out_ref[:, i * f_blk : (i + 1) * f_blk] = found_ref[i]
 
     return pl.pallas_call(
         kernel,
         in_specs=[IN_VMEM],
         out_specs=IN_VMEM,
-        out_shape=jax.ShapeDtypeStruct((cap, 2 * size_x * f_blk), found.dtype),
+        out_shape=jax.ShapeDtypeStruct((cap, blocks * f_blk), found.dtype),
         compiler_params=pltpu.CompilerParams(vmem_limit_bytes=VMEM_LIMIT),
         name="assemble",
     )(found)
@@ -355,10 +351,10 @@
         counts, activations[0, 0], out_grads[0, 0], d_blk, f_blk
     )
 
-    rows = [row0, shift(row_p1, "z", 2), shift(row_m1, "z", -2), shift(row_2, "z", 4)]
+    rows = [row0, shift(row_p1, 2), shift(row_m1, -2), shift(row_2, 4)]
     other = exchanged(other, "x")
     other, rows = lax.optimization_barrier((other, jnp.stack(rows)))
-    beside = lax.ppermute(rows, "z", [(i, i ^ 1) for i in range(lax.axis_size("z"))])
+    beside = lax.ppermute(rows, "q", [(0, 1), (1, 0)])
     place_of = {
         0: lambda q: 0,
         -2: lambda q: 1,
@@ -370,13 +366,15 @@
         -3: lambda q: 7 - 2 * q,
     }
 
-    other_m1, other_p1 = shift(other, "z", 1), shift(other, "z", -1)
+    other_m1, other_p1 = shift(other, 1), shift(other, -1)
     own, beside, other_m1, other_p1 = lax.optimization_barrier((own, beside, other_m1, other_p1))
     rows = lax.all_gather(jnp.concatenate([rows, beside]), "x")
     own = exchanged(own, "x")
-    other_m3, other_p3 = shift(other_m1, "z", 2), shift(other_p1, "z", -2)
+    other_m3, other_p3 = shift(other_m1, 2), shift(other_p1, -2)
     own, other_m3, other_p3 = lax.optimization_barrier((own, other_m3, other_p3))
-    own_m2, own_p2 = shift(own, "z", 2), shift(own, "z", -2)
+    own_m2, own_p2 = shift(own, 2), shift(own, -2)
+    late_inputs, own_m2, own_p2 = lax.optimization_barrier((next_inputs[0, 0], own_m2, own_p2))
+    tokens = lax.all_gather(late_inputs, ("q", "x"))
     pieces = {0: [own], -1: [other_m1], 1: [other_p1], -3: [other_m3], 3: [other_p3]}
     pieces |= {-2: [own_m2], 2: [own_p2]}
     first_away = (0, -1, 1, -3, 3)
@@ -387,9 +385,7 @@
     )
     half = size_x // 2
     up, down = own_m2[:half], own_p2[half:]
-    pieces[4] = [shift(up, "z", 2), shift(down, "z", -2)]
-    late_inputs, gradient = lax.optimization_barrier((next_inputs[0, 0], gradient))
-    tokens = lax.all_gather(late_inputs, "x")
+    pieces[4] = [shift(up, 2), shift(down, -2)]
     (gradient,) = outer_sum(
         rows,
         [place_of[a] for a in next_away],
@@ -410,23 +406,13 @@
     )
     weights_new, upper, lower = weights_of(exchanged(sums, SHARD), update, master[0, 0])
 
-    up = [[upper], [lower]]
-    down = [[upper], [lower]]
-    for step in range(1, 4):
-        for c in range(2):
-            up[c].append(shift(up[c][-1], "z", 1))
-            down[c].append(shift(down[c][-1], "z", -1))
-    tiles = [(0, [upper, lower])]
-    for away in (2, 1):
-        tiles.append((-away, [up[0][away], up[1][away]]))
-        tiles.append((away, [down[0][away], down[1][away]]))
-    part = project(tokens, tiles)
-    part, last_up, last_down = lax.optimization_barrier((part, up[0][3], down[1][3]))
-    last_tile = [shift(last_up, "z", 1), shift(last_down, "z", -1)]
-    tiles = [(-3, [up[0][3], up[1][3]]), (3, [down[0][3], down[1][3]])]
-    part = project(tokens, tiles, before=part)
-    found = project(tokens, [(4, last_tile)], before=part, last=True)
-    projected = assemble(exchanged(found, "x"))
+    upper_m, upper_p = shift(upper, 2), shift(upper, -2)
+    lower_m, lower_p = shift(lower, 2), shift(lower, -2)
+    opposite = [shift(upper_m, 2), shift(lower_p, -2)]
+    part = project(tokens, [(0, [upper, lower])])
+    part = project(tokens, [(3, [upper_m, lower_m]), (1, [upper_p, lower_p])], before=part)
+    found = project(tokens, [(2, opposite)], before=part, last=True)
+    projected = assemble(exchanged(found, ("q", "x")))
     return (
         weights_new[None, None],
         first_new[None, None],
@@ -436,7 +422,7 @@
 
 
 def solution(mesh):
-    finer = Mesh(mesh.devices.reshape(4, 2, 8, 4), EVERYONE)
+    finer = Mesh(mesh.devices.reshape(4, 2, 4, 2, 4), EVERYONE)
     tiled = P(EXPERT, SHARD, None, None)
     return jax.shard_map(
         body,

time: 288 us -> 294 us (1.021)
  blocking collectives: 62.7 us -> 85.9 us
  waiting for transfers between devices: 116 us -> 109 us
  starting transfers between devices: 48.2 us -> 41.6 us
    all_to_all x4, blocking collectives: 62.7 us -> 85.9 us  [exchanged(): return lax.all_to_all(values, axes, 0, 0, tiled=True)]
    all_gather x1, waiting for transfers between devices: 6.84 us -> 0.01 us  [body(): rows = lax.all_gather(jnp.concatenate([rows, beside]), 'x')]
    ppermute x26 -> x18, starting transfers between devices: 43.4 us -> 36.7 us  [the longest x17 35.3 us: shift(): return lax.ppermute(value, Z, [(i, (i + by) % size) for i in range(size)])]
    unnamed x26 -> x18, local copies, waits for them, and re-layouts: 8.43 us -> 6.24 us
    ppermute x26 -> x18, waiting for transfers between devices: 109 us -> 109 us  [the longest x17 86.3 us: shift(): return lax.ppermute(value, Z, [(i, (i + by) % size) for i in range(size)])]
  transfers between devices with their start and end apart: 29 -> 21, of which waited for: 17 -> 12; matrix products, arithmetic and copies ran while one was open for 0% -> 1% of each run, Pallas kernels for 10% -> 10%
where the time goes in v4:
time: 294 us; the launch traced here: 293 us
  waiting for transfers between devices  109 us (37%)
  blocking collectives  85.9 us (29%)
  starting transfers between devices  41.6 us (14%)
  Pallas kernels  33.3 us (11%)
  between operations  14.8 us (5%)
  local copies, waits for them, and re-layouts  7.74 us (3%)
    ppermute x17, waiting for transfers between devices, shift(): return lax.ppermute(value, Z, [(i, (i + by) % size) for i in range(size)])  86.3 us
    all_to_all x4, blocking collectives, exchanged(): return lax.all_to_all(values, axes, 0, 0, tiled=True)  85.9 us
    ppermute x17, starting transfers between devices, shift(): return lax.ppermute(value, Z, [(i, (i + by) % size) for i in range(size)])  35.3 us
    ppermute x1, waiting for transfers between devices, body(): beside = lax.ppermute(rows, 'q', [(0, 1), (1, 0)])  22.3 us
    pallas_call x3, Pallas kernels, outer_sum(): pl.pallas_call(kernel, in_specs=in_specs, out_specs=[IN_VMEM] * len(out_s...  13.5 us
    pallas_call x3, Pallas kernels, project(): pl.pallas_call(kernel, in_specs=[ANYWHERE] * (1 + len(flat)) + [IN_VMEM]...  11.2 us
    unnamed x18, local copies, waits for them, and re-layouts  6.24 us
  transfers between devices with their start and end apart: 21, of which 12 were waited for; matrix products, arithmetic and copies ran while one was open for 1% of the time, Pallas kernels for 10%

profile of v4, /device:TPU:1, one launch (start us, length us, event | category | flops | bytes accessed | tf_op | source)
XLA Modules:
  0.0 293.1 jit_solution(7564963146429037352)
XLA Ops:
  7.8 1.3 copy-done.1
  9.2 1.0 copy-done.8
  10.1 1.0 split.1
  11.2 4.8 %all-to-all-start = ((bf16[4,96,896]{2,1,0:T(8,128)(2,1)}), bf16[4,96,896]{2,1,0:T(8,128)(2,1)S(1)}, u32[]{:S(2)}, u32[]{:S(2)}) async-start(bf16[4,96,896]{2,1,0:T(8,128)(2,1)} %get-tuple-element.31), calls=%async_computation | async-start | bytes 1376256 | tf_op jit(solution)/shard_map/all_to_all | solution.py:76
  16.0 3.0 %collective-permute-start = (bf16[96,512]{1,0:T(8,128)(2,1)S(1)}, bf16[96,512]{1,0:T(8,128)(2,1)S(1)}, u32[]{:S(2)}, u32[]{:S(2)}) collective-permute-start(bf16[96,512]{1,0:T(8,128)(2,1)S(1)} %get-tuple-element.33), channel_id=1, source_target_pairs={{0,8},{4,12},{8,16},{12,20},{16,24},{20,28},{24,0},{28,4},{1,9},{5... | collective-permute-start | bytes 294920 | tf_op jit(solution)/shard_map/ppermute | solution.py:21
  19.0 3.1 %collective-permute-start.1 = (bf16[96,512]{1,0:T(8,128)(2,1)S(1)}, bf16[96,512]{1,0:T(8,128)(2,1)S(1)}, u32[]{:S(2)}, u32[]{:S(2)}) collective-permute-start(bf16[96,512]{1,0:T(8,128)(2,1)S(1)} %get-tuple-element.34), channel_id=1, source_target_pairs={{0,24},{4,28},{8,0},{12,4},{16,8},{20,12},{24,16},{28,20},{1,25},{... | collective-permute-start | bytes 294920 | tf_op jit(solution)/shard_map/ppermute | solution.py:21
  22.1 4.4 %collective-permute-start.2 = (bf16[96,512]{1,0:T(8,128)(2,1)S(1)}, bf16[96,512]{1,0:T(8,128)(2,1)S(1)}, u32[]{:S(2)}, u32[]{:S(2)}) collective-permute-start(bf16[96,512]{1,0:T(8,128)(2,1)S(1)} %get-tuple-element.35), channel_id=1, source_target_pairs={{0,16},{4,20},{8,24},{12,28},{16,0},{20,4},{24,8},{28,12},{1,17},{... | collective-permute-start | bytes 294920 | tf_op jit(solution)/shard_map/ppermute | solution.py:21
  26.5 1.5 collective-permute-done.1
  28.0 4.5 %collective-permute-done.2 = bf16[96,512]{1,0:T(8,128)(2,1)S(1)} collective-permute-done((bf16[96,512]{1,0:T(8,128)(2,1)S(1)}, bf16[96,512]{1,0:T(8,128)(2,1)S(1)}, u32[]{:S(2)}, u32[]{:S(2)}) %collective-permute-start.2) | collective-permute-done | bytes 98336 | tf_op jit(solution)/shard_map/ppermute | solution.py:21
  32.6 3.0 %collective-permute-start.4 = (bf16[4,96,896]{2,1,0:T(8,128)(2,1)S(1)}, bf16[4,96,896]{2,1,0:T(8,128)(2,1)S(1)}, u32[]{:S(2)}, u32[]{:S(2)}) collective-permute-start(bf16[4,96,896]{2,1,0:T(8,128)(2,1)S(1)} %all-to-all-done), channel_id=1, source_target_pairs={{0,4},{4,8},{8,12},{12,16},{16,20},{20,24},{24,28},{28,0},{1,5},{5... | collective-permute-start | bytes 2064392 | tf_op jit(solution)/shard_map/ppermute | solution.py:21
  35.6 1.5 collective-permute-start.3
  37.1 22.3 %collective-permute-done.3 = bf16[4,96,512]{2,1,0:T(8,128)(2,1)S(1)} collective-permute-done((bf16[4,96,512]{2,1,0:T(8,128)(2,1)S(1)}, bf16[4,96,512]{2,1,0:T(8,128)(2,1)S(1)}, u32[]{:S(2)}, u32[]{:S(2)}) %collective-permute-start.3) | collective-permute-done | bytes 393248 | tf_op jit(solution)/shard_map/ppermute | solution.py:357
  59.4 1.0 pad_maximum_fusion
  60.5 3.6 %collective-permute-start.7 = (bf16[4,96,896]{2,1,0:T(8,128)(2,1)S(1)}, bf16[4,96,896]{2,1,0:T(8,128)(2,1)S(1)}, u32[]{:S(2)}, u32[]{:S(2)}) collective-permute-start(bf16[4,96,896]{2,1,0:T(8,128)(2,1)S(1)} %collective-permute-done.5.refs_3_), channel_id=1, source_target_pairs={{0,24},{4,28},{8,0},{12,4},{16,8},{20,12},{24,16},{28,20},{1,25},{... | collective-permute-start | bytes 2064392 | tf_op jit(solution)/shard_map/ppermute | solution.py:21
  64.1 11.8 %all_to_all.25.refs_1_ = bf16[4,96,896]{2,1,0:T(8,128)(2,1)S(1)} all-to-all(bf16[4,96,896]{2,1,0:T(8,128)(2,1)S(1)} %get-tuple-element.40), channel_id=1, replica_groups=mesh['y'=4,'k'=2,'r'=4,'q'=2,'x'=4] {'x'}, dimensions={0} | all-to-all | bytes 1376256 | tf_op jit(solution)/shard_map/all_to_all | solution.py:76
  75.9 10.9 %collective-permute-done.6.refs_4_ = bf16[4,96,896]{2,1,0:T(8,128)(2,1)S(1)} collective-permute-done((bf16[4,96,896]{2,1,0:T(8,128)(2,1)S(1)}, bf16[4,96,896]{2,1,0:T(8,128)(2,1)S(1)}, u32[]{:S(2)}, u32[]{:S(2)}) %collective-permute-start.6) | collective-permute-done | bytes 688160 | tf_op jit(solution)/shard_map/ppermute | solution.py:21
  86.8 0.8 copy-done.4
  87.6 6.6 %collective-permute-done.7.refs_5_ = bf16[4,96,896]{2,1,0:T(8,128)(2,1)S(1)} collective-permute-done((bf16[4,96,896]{2,1,0:T(8,128)(2,1)S(1)}, bf16[4,96,896]{2,1,0:T(8,128)(2,1)S(1)}, u32[]{:S(2)}, u32[]{:S(2)}) %collective-permute-start.7) | collective-permute-done | bytes 688160 | tf_op jit(solution)/shard_map/ppermute | solution.py:21
  94.2 0.8 copy-done.6
  95.0 2.7 collective-permute-start.8
  97.8 0.8 collective-permute-start.9
  98.6 28.7 %collective-permute-done.8.refs_1_ = bf16[4,96,896]{2,1,0:T(8,128)(2,1)S(1)} collective-permute-done((bf16[4,96,896]{2,1,0:T(8,128)(2,1)S(1)}, bf16[4,96,896]{2,1,0:T(8,128)(2,1)S(1)}, u32[]{:S(2)}, u32[]{:S(2)}) %collective-permute-start.8) | collective-permute-done | bytes 688160 | tf_op jit(solution)/shard_map/ppermute | solution.py:21
  127.3 1.2 collective-permute-done.9.refs_2_
  128.5 0.8 slice.6
  129.3 2.6 collective-permute-start.10
  131.9 0.7 slice.7
  132.6 1.0 collective-permute-start.11
  133.6 1.1 copy-done.5
  134.7 1.1 copy-done.7
  135.8 7.1 %outer_first.1.refs_3_ = f32[512,896]{1,0:T(8,128)S(1)} custom-call(bf16[4,8,96,512]{3,2,1,0:T(8,128)(2,1)} %bitcast.26, bf16[4,96,896]{2,1,0:T(8,128)(2,1)S(1)} %all_to_all.25.refs_1_, bf16[4,96,896]{2,1,0:T(8,128)(2,1)S(1)} %collective-permute-done.4.refs_2_, bf16[4,96,896]{2,1,0:T(8,128)(2,1)S(1)} %collective-permute-done.5.refs_3_, ...), custom_call_target="tpu_custom_call" | custom-call | flops 1761607680 | bytes 7241728 | tf_op jit(solution)/shard_map/outer_first/pallas_call | solution.py:233
  142.9 3.6 %outer_next.1.refs_3_ = f32[512,896]{1,0:T(8,128)S(1)} custom-call(bf16[4,8,96,512]{3,2,1,0:T(8,128)(2,1)} %bitcast.27, bf16[4,96,896]{2,1,0:T(8,128)(2,1)S(1)} %collective-permute-done.8.refs_1_, bf16[4,96,896]{2,1,0:T(8,128)(2,1)S(1)} %collective-permute-done.9.refs_2_, f32[512,896]{1,0:T(8,128)S(1)} %outer_first.1.refs_3_), custom_call_target="tpu_custom_call", output_to_operand_aliasing={{}: (3, {})} | custom-call | flops 704643072 | bytes 3997696 | tf_op jit(solution)/shard_map/outer_next/pallas_call | solution.py:233
  146.6 2.7 outer_last.1
  149.4 28.9 %all_to_all.26.n_ref = f32[256,1,128]{2,1,0:T(1,128)S(1)} all-to-all(f32[256,1,128]{2,1,0:T(1,128)S(1)} %get-tuple-element.48), channel_id=1, replica_groups=mesh['y'=4,'k'=2,'r'=4,'q'=2,'x'=4] {'y','k','r','q','x'}, dimensions={0} | all-to-all | bytes 262144 | tf_op jit(solution)/shard_map/all_to_all | solution.py:76
  178.2 4.3 %update_of.1 = (f32[512,896]{1,0:T(8,128)S(1)}, bf16[512,896]{1,0:T(8,128)(2,1)}, bf16[512,896]{1,0:T(8,128)(2,1)}, f32[32,2,128]{2,1,0:T(2,128)S(1)}) custom-call(f32[256,1,128]{2,1,0:T(1,128)S(1)} %all_to_all.26.n_ref, f32[512,896]{1,0:T(8,128)S(1)} %get-tuple-element.49.g_ref, f32[512,896]{1,0:T(8,128)S(1)} %bitcast.16, bf16[512,896]{1,0:T(8,128)(2,1)S(1)} %bitcast.19, ...), custom_call_target="tpu_custom_call" | custom-call | tf_op jit(solution)/shard_map/update_of/pallas_call | solution.py:113
  182.6 13.1 %all_to_all.27.sums_ref = f32[32,2,128]{2,1,0:T(2,128)S(1)} all-to-all(f32[32,2,128]{2,1,0:T(2,128)S(1)} %get-tuple-element.50), channel_id=1, replica_groups=mesh['y'=4,'k'=2,'r'=4,'q'=2,'x'=4] {'r','q','x'}, dimensions={0} | all-to-all | bytes 65536 | tf_op jit(solution)/shard_map/all_to_all | solution.py:76
  195.7 2.1 weights_of.1
  198.1 3.2 %collective-permute-start.14 = (bf16[256,896]{1,0:T(8,128)(2,1)S(1)}, bf16[256,896]{1,0:T(8,128)(2,1)S(1)}, u32[]{:S(2)}, u32[]{:S(2)}) collective-permute-start(bf16[256,896]{1,0:T(8,128)(2,1)S(1)} %get-tuple-element.57.refs_2_), channel_id=1, source_target_pairs={{0,24},{4,28},{8,0},{12,4},{16,8},{20,12},{24,16},{28,20},{1,25},{... | collective-permute-start | bytes 1376264 | tf_op jit(solution)/shard_map/ppermute | solution.py:21
  201.3 3.6 %collective-permute-start.17 = (bf16[256,896]{1,0:T(8,128)(2,1)S(1)}, bf16[256,896]{1,0:T(8,128)(2,1)S(1)}, u32[]{:S(2)}, u32[]{:S(2)}) collective-permute-start(bf16[256,896]{1,0:T(8,128)(2,1)S(1)} %get-tuple-element.56.refs_1_), channel_id=1, source_target_pairs={{0,24},{4,28},{8,0},{12,4},{16,8},{20,12},{24,16},{28,20},{1,25},{... | collective-permute-start | bytes 1376264 | tf_op jit(solution)/shard_map/ppermute | solution.py:21
  204.9 10.6 %collective-permute-done.12.refs_1_ = bf16[256,896]{1,0:T(8,128)(2,1)S(1)} collective-permute-done((bf16[256,896]{1,0:T(8,128)(2,1)S(1)}, bf16[256,896]{1,0:T(8,128)(2,1)S(1)}, u32[]{:S(2)}, u32[]{:S(2)}) %collective-permute-start.12) | collective-permute-done | bytes 458784 | tf_op jit(solution)/shard_map/ppermute | solution.py:21
  215.5 14.6 %collective-permute-done.14.refs_4_ = bf16[256,896]{1,0:T(8,128)(2,1)S(1)} collective-permute-done((bf16[256,896]{1,0:T(8,128)(2,1)S(1)}, bf16[256,896]{1,0:T(8,128)(2,1)S(1)}, u32[]{:S(2)}, u32[]{:S(2)}) %collective-permute-start.14) | collective-permute-done | bytes 458784 | tf_op jit(solution)/shard_map/ppermute | solution.py:21
  230.1 3.8 %collective-permute-start.15 = (bf16[256,896]{1,0:T(8,128)(2,1)S(1)}, bf16[256,896]{1,0:T(8,128)(2,1)}, u32[]{:S(2)}, u32[]{:S(2)}) collective-permute-start(bf16[256,896]{1,0:T(8,128)(2,1)S(1)} %collective-permute-done.14.refs_4_), channel_id=1, source_target_pairs={{0,24},{4,28},{8,0},{12,4},{16,8},{20,12},{24,16},{28,20},{1,25},{... | collective-permute-start | bytes 1376264 | tf_op jit(solution)/shard_map/ppermute | solution.py:21
  234.0 3.2 %project_first.1.refs_5_ = f32[768,896]{1,0:T(8,128)S(1)} custom-call(bf16[8,96,2048]{2,1,0:T(8,128)(2,1)} %bitcast.23, bf16[256,896]{1,0:T(8,128)(2,1)S(1)} %get-tuple-element.56.refs_1_, bf16[256,896]{1,0:T(8,128)(2,1)S(1)} %get-tuple-element.57.refs_2_), custom_call_target="tpu_custom_call" | custom-call | flops 704643072 | bytes 1703936 | tf_op jit(solution)/shard_map/project_first/pallas_call | solution.py:306
  237.2 2.8 collective-permute-done.17.refs_3_
  240.0 5.0 %project_next.1.refs_3_ = f32[768,896]{1,0:T(8,128)S(1)} custom-call(bf16[8,96,2048]{2,1,0:T(8,128)(2,1)} %bitcast.24, bf16[256,896]{1,0:T(8,128)(2,1)S(1)} %collective-permute-done.12.refs_1_, bf16[256,896]{1,0:T(8,128)(2,1)S(1)} %collective-permute-done.16.refs_2_, bf16[256,896]{1,0:T(8,128)(2,1)S(1)} %collective-permute-done.17.refs_3_, ...), custom_call_target="tpu_custom_call" | custom-call | flops 1409286144 | bytes 3407872 | tf_op jit(solution)/shard_map/project_next/pallas_call | solution.py:306
  245.0 4.6 %collective-permute-done.13.refs_1_ = bf16[256,896]{1,0:T(8,128)(2,1)S(1)} collective-permute-done((bf16[256,896]{1,0:T(8,128)(2,1)S(1)}, bf16[256,896]{1,0:T(8,128)(2,1)S(1)}, u32[]{:S(2)}, u32[]{:S(2)}) %collective-permute-start.13) | collective-permute-done | bytes 458784 | tf_op jit(solution)/shard_map/ppermute | solution.py:21
  249.9 3.0 %project_last.1 = bf16[8,96,896]{2,1,0:T(8,128)(2,1)S(1)} custom-call(bf16[8,96,2048]{2,1,0:T(8,128)(2,1)} %bitcast.25, bf16[256,896]{1,0:T(8,128)(2,1)S(1)} %collective-permute-done.13.refs_1_, bf16[256,896]{1,0:T(8,128)(2,1)} %collective-permute-done.15.refs_2_, f32[768,896]{1,0:T(8,128)S(1)} %project_next.1.refs_3_), custom_call_target="tpu_custom_call" | custom-call | flops 704643072 | bytes 1703936 | tf_op jit(solution)/shard_map/project_last/pallas_call | solution.py:306
  253.0 32.1 %all_to_all.28.found_ref = bf16[8,96,896]{2,1,0:T(8,128)(2,1)S(1)} all-to-all(bf16[8,96,896]{2,1,0:T(8,128)(2,1)S(1)} %project_last.1), channel_id=1, replica_groups=mesh['y'=4,'k'=2,'r'=4,'q'=2,'x'=4] {'q','x'}, dimensions={0} | all-to-all | bytes 2752512 | tf_op jit(solution)/shard_map/all_to_all | solution.py:76
  285.1 1.2 assemble.1
  (32 shorter events, 0.9 us)
Async XLA Ops:
  7.8 1.3 copy-start.1
  9.2 1.0 copy-start.8
  11.2 21.4 %all-to-all-start = ((bf16[4,96,896]{2,1,0:T(8,128)(2,1)}), bf16[4,96,896]{2,1,0:T(8,128)(2,1)S(1)}, u32[]{:S(2)}, u32[]{:S(2)}) async-start(bf16[4,96,896]{2,1,0:T(8,128)(2,1)} %get-tuple-element.31), calls=%async_computation | async-start | bytes 1376256 | tf_op jit(solution)/shard_map/all_to_all | solution.py:76
  16.0 117.6 %all-gather.5.cloned.1.call-start = ((), (), s32[]{:S(2)}) async-start(), calls=%async_computation.5 | async-start | bytes 3932160 | tf_op jit(solution)/shard_map/all_gather | solution.py:371
  16.0 10.5 %collective-permute-start = (bf16[96,512]{1,0:T(8,128)(2,1)S(1)}, bf16[96,512]{1,0:T(8,128)(2,1)S(1)}, u32[]{:S(2)}, u32[]{:S(2)}) collective-permute-start(bf16[96,512]{1,0:T(8,128)(2,1)S(1)} %get-tuple-element.33), channel_id=1, source_target_pairs={{0,8},{4,12},{8,16},{12,20},{16,24},{20,28},{24,0},{28,4},{1,9},{5... | collective-permute-start | bytes 294920 | tf_op jit(solution)/shard_map/ppermute | solution.py:21
  19.0 9.0 %collective-permute-start.1 = (bf16[96,512]{1,0:T(8,128)(2,1)S(1)}, bf16[96,512]{1,0:T(8,128)(2,1)S(1)}, u32[]{:S(2)}, u32[]{:S(2)}) collective-permute-start(bf16[96,512]{1,0:T(8,128)(2,1)S(1)} %get-tuple-element.34), channel_id=1, source_target_pairs={{0,24},{4,28},{8,0},{12,4},{16,8},{20,12},{24,16},{28,20},{1,25},{... | collective-permute-start | bytes 294920 | tf_op jit(solution)/shard_map/ppermute | solution.py:21
  22.1 10.4 %collective-permute-start.2 = (bf16[96,512]{1,0:T(8,128)(2,1)S(1)}, bf16[96,512]{1,0:T(8,128)(2,1)S(1)}, u32[]{:S(2)}, u32[]{:S(2)}) collective-permute-start(bf16[96,512]{1,0:T(8,128)(2,1)S(1)} %get-tuple-element.35), channel_id=1, source_target_pairs={{0,16},{4,20},{8,24},{12,28},{16,0},{20,4},{24,8},{28,12},{1,17},{... | collective-permute-start | bytes 294920 | tf_op jit(solution)/shard_map/ppermute | solution.py:21
  32.6 26.8 %collective-permute-start.4 = (bf16[4,96,896]{2,1,0:T(8,128)(2,1)S(1)}, bf16[4,96,896]{2,1,0:T(8,128)(2,1)S(1)}, u32[]{:S(2)}, u32[]{:S(2)}) collective-permute-start(bf16[4,96,896]{2,1,0:T(8,128)(2,1)S(1)} %all-to-all-done), channel_id=1, source_target_pairs={{0,4},{4,8},{8,12},{12,16},{16,20},{20,24},{24,28},{28,0},{1,5},{5... | collective-permute-start | bytes 2064392 | tf_op jit(solution)/shard_map/ppermute | solution.py:21
  35.6 23.8 %collective-permute-start.5 = (bf16[4,96,896]{2,1,0:T(8,128)(2,1)S(1)}, bf16[4,96,896]{2,1,0:T(8,128)(2,1)S(1)}, u32[]{:S(2)}, u32[]{:S(2)}) collective-permute-start(bf16[4,96,896]{2,1,0:T(8,128)(2,1)S(1)} %all-to-all-done), channel_id=1, source_target_pairs={{0,28},{4,0},{8,4},{12,8},{16,12},{20,16},{24,20},{28,24},{1,29},{... | collective-permute-start | bytes 2064392 | tf_op jit(solution)/shard_map/ppermute | solution.py:21
  35.6 23.8 %collective-permute-start.3 = (bf16[4,96,512]{2,1,0:T(8,128)(2,1)S(1)}, bf16[4,96,512]{2,1,0:T(8,128)(2,1)S(1)}, u32[]{:S(2)}, u32[]{:S(2)}) collective-permute-start(bf16[4,96,512]{2,1,0:T(8,128)(2,1)S(1)} %pad_maximum_fusion.1), channel_id=1, source_target_pairs={{0,4},{4,0},{1,5},{5,1},{2,6},{6,2},{3,7},{7,3},{8,12},{12,8},{9,1... | collective-permute-start | bytes 1179656 | tf_op jit(solution)/shard_map/ppermute | solution.py:357
  60.4 173.6 %all-gather.7.cloned.1.call-start = ((), (), s32[]{:S(2)}) async-start(), calls=%async_computation.6 | async-start | bytes 3538944 | tf_op jit(solution)/shard_map/all_gather | solution.py:377
  60.4 26.3 %collective-permute-start.6 = (bf16[4,96,896]{2,1,0:T(8,128)(2,1)S(1)}, bf16[4,96,896]{2,1,0:T(8,128)(2,1)S(1)}, u32[]{:S(2)}, u32[]{:S(2)}) collective-permute-start(bf16[4,96,896]{2,1,0:T(8,128)(2,1)S(1)} %collective-permute-done.4.refs_2_), channel_id=1, source_target_pairs={{0,8},{4,12},{8,16},{12,20},{16,24},{20,28},{24,0},{28,4},{1,9},{5... | collective-permute-start | bytes 2064392 | tf_op jit(solution)/shard_map/ppermute | solution.py:21
  60.5 33.7 %collective-permute-start.7 = (bf16[4,96,896]{2,1,0:T(8,128)(2,1)S(1)}, bf16[4,96,896]{2,1,0:T(8,128)(2,1)S(1)}, u32[]{:S(2)}, u32[]{:S(2)}) collective-permute-start(bf16[4,96,896]{2,1,0:T(8,128)(2,1)S(1)} %collective-permute-done.5.refs_3_), channel_id=1, source_target_pairs={{0,24},{4,28},{8,0},{12,4},{16,8},{20,12},{24,16},{28,20},{1,25},{... | collective-permute-start | bytes 2064392 | tf_op jit(solution)/shard_map/ppermute | solution.py:21
  86.8 0.8 copy-start.4
  94.2 0.8 copy-start.6
  95.0 32.3 %collective-permute-start.8 = (bf16[4,96,896]{2,1,0:T(8,128)(2,1)S(1)}, bf16[4,96,896]{2,1,0:T(8,128)(2,1)S(1)}, u32[]{:S(2)}, u32[]{:S(2)}) collective-permute-start(bf16[4,96,896]{2,1,0:T(8,128)(2,1)S(1)} %all_to_all.25.refs_1_), channel_id=1, source_target_pairs={{0,8},{4,12},{8,16},{12,20},{16,24},{20,28},{24,0},{28,4},{1,9},{5... | collective-permute-start | bytes 2064392 | tf_op jit(solution)/shard_map/ppermute | solution.py:21
  97.8 30.7 %collective-permute-start.9 = (bf16[4,96,896]{2,1,0:T(8,128)(2,1)S(1)}, bf16[4,96,896]{2,1,0:T(8,128)(2,1)S(1)}, u32[]{:S(2)}, u32[]{:S(2)}) collective-permute-start(bf16[4,96,896]{2,1,0:T(8,128)(2,1)S(1)} %all_to_all.25.refs_1_), channel_id=1, source_target_pairs={{0,24},{4,28},{8,0},{12,4},{16,8},{20,12},{24,16},{28,20},{1,25},{... | collective-permute-start | bytes 2064392 | tf_op jit(solution)/shard_map/ppermute | solution.py:21
  129.3 17.3 %collective-permute-start.10 = (bf16[2,96,896]{2,1,0:T(8,128)(2,1)}, bf16[2,96,896]{2,1,0:T(8,128)(2,1)}, u32[]{:S(2)}, u32[]{:S(2)}) collective-permute-start(bf16[2,96,896]{2,1,0:T(8,128)(2,1)} %slice.6), channel_id=1, source_target_pairs={{0,8},{4,12},{8,16},{12,20},{16,24},{20,28},{24,0},{28,4},{1,9},{5... | collective-permute-start | bytes 1032200 | tf_op jit(solution)/shard_map/ppermute | solution.py:21
  132.6 14.0 %collective-permute-start.11 = (bf16[2,96,896]{2,1,0:T(8,128)(2,1)}, bf16[2,96,896]{2,1,0:T(8,128)(2,1)}, u32[]{:S(2)}, u32[]{:S(2)}) collective-permute-start(bf16[2,96,896]{2,1,0:T(8,128)(2,1)} %slice.7), channel_id=1, source_target_pairs={{0,24},{4,28},{8,0},{12,4},{16,8},{20,12},{24,16},{28,20},{1,25},{... | collective-permute-start | bytes 1032200 | tf_op jit(solution)/shard_map/ppermute | solution.py:21
  133.6 1.1 copy-start.5
  134.7 1.1 copy-start.7
  146.5 31.7 %copy-start = (f32[1,1,512,896]{3,2,1,0:T(8,128)S(1)}, f32[1,1,512,896]{3,2,1,0:T(8,128)}, u32[]{:S(2)}) copy-start(f32[1,1,512,896]{3,2,1,0:T(8,128)} %param.11) | copy-start | bytes 5505028
  146.6 31.7 %copy-start.2 = (bf16[1,1,512,896]{3,2,1,0:T(8,128)(2,1)S(1)}, bf16[1,1,512,896]{3,2,1,0:T(8,128)(2,1)}, u32[]{:S(2)}) copy-start(bf16[1,1,512,896]{3,2,1,0:T(8,128)(2,1)} %param.12) | copy-start | bytes 2752516
  146.6 31.7 %copy-start.3 = (bf16[1,1,512,896]{3,2,1,0:T(8,128)(2,1)S(1)}, bf16[1,1,512,896]{3,2,1,0:T(8,128)(2,1)}, u32[]{:S(2)}) copy-start(bf16[1,1,512,896]{3,2,1,0:T(8,128)(2,1)} %param.13) | copy-start | bytes 2752516
  197.8 17.8 %collective-permute-start.12 = (bf16[256,896]{1,0:T(8,128)(2,1)S(1)}, bf16[256,896]{1,0:T(8,128)(2,1)S(1)}, u32[]{:S(2)}, u32[]{:S(2)}) collective-permute-start(bf16[256,896]{1,0:T(8,128)(2,1)S(1)} %get-tuple-element.56.refs_1_), channel_id=1, source_target_pairs={{0,8},{4,12},{8,16},{12,20},{16,24},{20,28},{24,0},{28,4},{1,9},{5... | collective-permute-start | bytes 1376264 | tf_op jit(solution)/shard_map/ppermute | solution.py:21
  198.1 32.0 %collective-permute-start.14 = (bf16[256,896]{1,0:T(8,128)(2,1)S(1)}, bf16[256,896]{1,0:T(8,128)(2,1)S(1)}, u32[]{:S(2)}, u32[]{:S(2)}) collective-permute-start(bf16[256,896]{1,0:T(8,128)(2,1)S(1)} %get-tuple-element.57.refs_2_), channel_id=1, source_target_pairs={{0,24},{4,28},{8,0},{12,4},{16,8},{20,12},{24,16},{28,20},{1,25},{... | collective-permute-start | bytes 1376264 | tf_op jit(solution)/shard_map/ppermute | solution.py:21
  201.3 35.8 %collective-permute-start.16 = (bf16[256,896]{1,0:T(8,128)(2,1)S(1)}, bf16[256,896]{1,0:T(8,128)(2,1)S(1)}, u32[]{:S(2)}, u32[]{:S(2)}) collective-permute-start(bf16[256,896]{1,0:T(8,128)(2,1)S(1)} %get-tuple-element.57.refs_2_), channel_id=1, source_target_pairs={{0,8},{4,12},{8,16},{12,20},{16,24},{20,28},{24,0},{28,4},{1,9},{5... | collective-permute-start | bytes 1376264 | tf_op jit(solution)/shard_map/ppermute | solution.py:21
  201.3 38.6 %collective-permute-start.17 = (bf16[256,896]{1,0:T(8,128)(2,1)S(1)}, bf16[256,896]{1,0:T(8,128)(2,1)S(1)}, u32[]{:S(2)}, u32[]{:S(2)}) collective-permute-start(bf16[256,896]{1,0:T(8,128)(2,1)S(1)} %get-tuple-element.56.refs_1_), channel_id=1, source_target_pairs={{0,24},{4,28},{8,0},{12,4},{16,8},{20,12},{24,16},{28,20},{1,25},{... | collective-permute-start | bytes 1376264 | tf_op jit(solution)/shard_map/ppermute | solution.py:21
  215.5 34.1 %collective-permute-start.13 = (bf16[256,896]{1,0:T(8,128)(2,1)S(1)}, bf16[256,896]{1,0:T(8,128)(2,1)S(1)}, u32[]{:S(2)}, u32[]{:S(2)}) collective-permute-start(bf16[256,896]{1,0:T(8,128)(2,1)S(1)} %collective-permute-done.12.refs_1_), channel_id=1, source_target_pairs={{0,8},{4,12},{8,16},{12,20},{16,24},{20,28},{24,0},{28,4},{1,9},{5... | collective-permute-start | bytes 1376264 | tf_op jit(solution)/shard_map/ppermute | solution.py:21
  230.1 19.8 %collective-permute-start.15 = (bf16[256,896]{1,0:T(8,128)(2,1)S(1)}, bf16[256,896]{1,0:T(8,128)(2,1)}, u32[]{:S(2)}, u32[]{:S(2)}) collective-permute-start(bf16[256,896]{1,0:T(8,128)(2,1)S(1)} %collective-permute-done.14.refs_4_), channel_id=1, source_target_pairs={{0,24},{4,28},{8,0},{12,4},{16,8},{20,12},{24,16},{28,20},{1,25},{... | collective-permute-start | bytes 1376264 | tf_op jit(solution)/shard_map/ppermute | solution.py:21
Sparse Core Ops, SparseCore 0:
  60.5 44.6 all-gather.4
  128.7 49.9 all-gather.6

commit v5 on v4

--- a/solution.py
+++ b/solution.py
@@ -329,7 +329,8 @@
 
     def kernel(found_ref, out_ref):
         for i in range(blocks):
-            out_ref[:, i * f_blk : (i + 1) * f_blk] = found_ref[i]
+            start = (i % 2 * (blocks // 2) + i // 2) * f_blk
+            out_ref[:, start : start + f_blk] = found_ref[i]
 
     return pl.pallas_call(
         kernel,
@@ -353,7 +354,9 @@
 
     rows = [row0, shift(row_p1, 2), shift(row_m1, -2), shift(row_2, 4)]
     other = exchanged(other, "x")
-    other, rows = lax.optimization_barrier((other, jnp.stack(rows)))
+    mine = next_inputs[0, 0]
+    theirs = lax.ppermute(mine, "q", [(0, 1), (1, 0)])
+    other, rows, theirs = lax.optimization_barrier((other, jnp.stack(rows), theirs))
     beside = lax.ppermute(rows, "q", [(0, 1), (1, 0)])
     place_of = {
         0: lambda q: 0,
@@ -371,10 +374,11 @@
     rows = lax.all_gather(jnp.concatenate([rows, beside]), "x")
     own = exchanged(own, "x")
     other_m3, other_p3 = shift(other_m1, 2), shift(other_p1, -2)
-    own, other_m3, other_p3 = lax.optimization_barrier((own, other_m3, other_p3))
+    first = lax.axis_index("q") == 0
+    tokens = jnp.stack([jnp.where(first, mine, theirs), jnp.where(first, theirs, mine)])
+    own, other_m3, other_p3, tokens = lax.optimization_barrier((own, other_m3, other_p3, tokens))
+    tokens = lax.all_gather(tokens, "x").reshape(2 * size_x, cap, d)
     own_m2, own_p2 = shift(own, 2), shift(own, -2)
-    late_inputs, own_m2, own_p2 = lax.optimization_barrier((next_inputs[0, 0], own_m2, own_p2))
-    tokens = lax.all_gather(late_inputs, ("q", "x"))
     pieces = {0: [own], -1: [other_m1], 1: [other_p1], -3: [other_m3], 3: [other_p3]}
     pieces |= {-2: [own_m2], 2: [own_p2]}
     first_away = (0, -1, 1, -3, 3)
@@ -412,7 +416,7 @@
     part = project(tokens, [(0, [upper, lower])])
     part = project(tokens, [(3, [upper_m, lower_m]), (1, [upper_p, lower_p])], before=part)
     found = project(tokens, [(2, opposite)], before=part, last=True)
-    projected = assemble(exchanged(found, ("q", "x")))
+    projected = assemble(exchanged(found, ("x", "q")))
     return (
         weights_new[None, None],
         first_new[None, None],

time: 294 us -> 300 us (1.020)
  waiting for transfers between devices: 109 us -> 129 us
  blocking collectives: 85.9 us -> 66.1 us
    all_to_all x4 -> x3, blocking collectives: 85.9 us -> 66.1 us  [exchanged(): return lax.all_to_all(values, axes, 0, 0, tiled=True)]
    ppermute x17, waiting for transfers between devices: 86.3 us -> 103 us  [shift(): return lax.ppermute(value, Z, [(i, (i + by) % size) for i in range(size)])]
    all_to_all x1 -> x2, waiting for transfers between devices: 0.01 us -> 5.98 us  [exchanged(): return lax.all_to_all(values, axes, 0, 0, tiled=True)]
    all_to_all x1 -> x2, starting transfers between devices: 4.84 us -> 8.4 us  [exchanged(): return lax.all_to_all(values, axes, 0, 0, tiled=True)]
    unnamed x18 -> x22, local copies, waits for them, and re-layouts: 6.24 us -> 6.96 us
  transfers between devices with their start and end apart: 21 -> 23, of which waited for: 12 -> 12; matrix products, arithmetic and copies ran while one was open for 1% -> 1% of each run, Pallas kernels for 10% -> 9%
where the time goes in v5:
time: 300 us; the launch traced here: 299 us
  waiting for transfers between devices  129 us (43%)
  blocking collectives  66.1 us (22%)
  starting transfers between devices  44 us (15%)
  Pallas kernels  33.6 us (11%)
  between operations  14.8 us (5%)
  local copies, waits for them, and re-layouts  8.5 us (3%)
  other arithmetic  3.12 us (1%)
    ppermute x17, waiting for transfers between devices, shift(): return lax.ppermute(value, Z, [(i, (i + by) % size) for i in range(size)])  103 us
    all_to_all x3, blocking collectives, exchanged(): return lax.all_to_all(values, axes, 0, 0, tiled=True)  66.1 us
    ppermute x17, starting transfers between devices, shift(): return lax.ppermute(value, Z, [(i, (i + by) % size) for i in range(size)])  33.9 us
    ppermute x1, waiting for transfers between devices, body(): beside = lax.ppermute(rows, 'q', [(0, 1), (1, 0)])  20.3 us
    pallas_call x3, Pallas kernels, outer_sum(): pl.pallas_call(kernel, in_specs=in_specs, out_specs=[IN_VMEM] * len(out_s...  13.5 us
    pallas_call x3, Pallas kernels, project(): pl.pallas_call(kernel, in_specs=[ANYWHERE] * (1 + len(flat)) + [IN_VMEM]...  11.2 us
    all_to_all x2, starting transfers between devices, exchanged(): return lax.all_to_all(values, axes, 0, 0, tiled=True)  8.4 us
    unnamed x22, local copies, waits for them, and re-layouts  6.96 us
  transfers between devices with their start and end apart: 23, of which 12 were waited for; matrix products, arithmetic and copies ran while one was open for 1% of the time, Pallas kernels for 9%

profile of v5, /device:TPU:1, one launch (start us, length us, event | category | flops | bytes accessed | tf_op | source)
XLA Modules:
  0.0 299.1 jit_solution(6881105197455106944)
XLA Ops:
  7.8 1.3 copy-done.1
  9.2 1.0 copy-done.8
  10.2 1.3 split.1
  11.4 4.8 %all-to-all-start = ((bf16[4,96,896]{2,1,0:T(8,128)(2,1)}), bf16[4,96,896]{2,1,0:T(8,128)(2,1)S(1)}, u32[]{:S(2)}, u32[]{:S(2)}) async-start(bf16[4,96,896]{2,1,0:T(8,128)(2,1)} %get-tuple-element.30), calls=%async_computation | async-start | bytes 1376256 | tf_op jit(solution)/shard_map/all_to_all | solution.py:76
  16.3 1.7 collective-permute-start.3
  18.0 3.0 collective-permute-start
  21.0 2.1 collective-permute-start.1
  23.1 4.5 %collective-permute-start.2 = (bf16[96,512]{1,0:T(8,128)(2,1)S(1)}, bf16[96,512]{1,0:T(8,128)(2,1)S(1)}, u32[]{:S(2)}, u32[]{:S(2)}) collective-permute-start(bf16[96,512]{1,0:T(8,128)(2,1)S(1)} %get-tuple-element.34), channel_id=1, source_target_pairs={{0,16},{4,20},{8,24},{12,28},{16,0},{20,4},{24,8},{28,12},{1,17},{... | collective-permute-start | bytes 294920 | tf_op jit(solution)/shard_map/ppermute | solution.py:21
  27.6 7.7 %collective-permute-done = bf16[96,512]{1,0:T(8,128)(2,1)S(1)} collective-permute-done((bf16[96,512]{1,0:T(8,128)(2,1)S(1)}, bf16[96,512]{1,0:T(8,128)(2,1)S(1)}, u32[]{:S(2)}, u32[]{:S(2)}) %collective-permute-start) | collective-permute-done | bytes 98336 | tf_op jit(solution)/shard_map/ppermute | solution.py:21
  35.2 3.2 %collective-permute-done.2 = bf16[96,512]{1,0:T(8,128)(2,1)S(1)} collective-permute-done((bf16[96,512]{1,0:T(8,128)(2,1)S(1)}, bf16[96,512]{1,0:T(8,128)(2,1)S(1)}, u32[]{:S(2)}, u32[]{:S(2)}) %collective-permute-start.2) | collective-permute-done | bytes 98336 | tf_op jit(solution)/shard_map/ppermute | solution.py:21
  39.8 2.1 collective-permute-start.6
  41.9 20.3 %collective-permute-done.4 = bf16[4,96,512]{2,1,0:T(8,128)(2,1)S(1)} collective-permute-done((bf16[4,96,512]{2,1,0:T(8,128)(2,1)S(1)}, bf16[4,96,512]{2,1,0:T(8,128)(2,1)S(1)}, u32[]{:S(2)}, u32[]{:S(2)}) %collective-permute-start.4) | collective-permute-done | bytes 393248 | tf_op jit(solution)/shard_map/ppermute | solution.py:360
  62.2 1.0 pad_maximum_fusion
  63.2 3.8 %collective-permute-start.7 = (bf16[4,96,896]{2,1,0:T(8,128)(2,1)S(1)}, bf16[4,96,896]{2,1,0:T(8,128)(2,1)S(1)}, u32[]{:S(2)}, u32[]{:S(2)}) collective-permute-start(bf16[4,96,896]{2,1,0:T(8,128)(2,1)S(1)} %collective-permute-done.5.refs_2_), channel_id=1, source_target_pairs={{0,8},{4,12},{8,16},{12,20},{16,24},{20,28},{24,0},{28,4},{1,9},{5... | collective-permute-start | bytes 2064392 | tf_op jit(solution)/shard_map/ppermute | solution.py:21
  67.1 3.6 %all-to-all-start.1 = ((bf16[4,96,896]{2,1,0:T(8,128)(2,1)}), bf16[4,96,896]{2,1,0:T(8,128)(2,1)S(1)}, u32[]{:S(2)}, u32[]{:S(2)}) async-start(bf16[4,96,896]{2,1,0:T(8,128)(2,1)} %get-tuple-element.39), calls=%async_computation.1 | async-start | bytes 1376256 | tf_op jit(solution)/shard_map/all_to_all | solution.py:76
  70.6 1.2 select_bitcast_fusion.1
  71.8 0.9 pad_maximum_fusion.1
  72.7 6.0 %all-to-all-done.1.refs_1_ = bf16[4,96,896]{2,1,0:T(8,128)(2,1)S(1)} async-done(((bf16[4,96,896]{2,1,0:T(8,128)(2,1)}), bf16[4,96,896]{2,1,0:T(8,128)(2,1)S(1)}, u32[]{:S(2)}, u32[]{:S(2)}) %all-to-all-start.1) | async-done | bytes 688160 | tf_op jit(solution)/shard_map/all_to_all | solution.py:76
  78.7 11.0 %collective-permute-done.7.refs_4_ = bf16[4,96,896]{2,1,0:T(8,128)(2,1)S(1)} collective-permute-done((bf16[4,96,896]{2,1,0:T(8,128)(2,1)S(1)}, bf16[4,96,896]{2,1,0:T(8,128)(2,1)S(1)}, u32[]{:S(2)}, u32[]{:S(2)}) %collective-permute-start.7) | collective-permute-done | bytes 688160 | tf_op jit(solution)/shard_map/ppermute | solution.py:21
  89.8 0.8 copy-done.4
  90.6 9.6 %collective-permute-done.8.refs_5_ = bf16[4,96,896]{2,1,0:T(8,128)(2,1)S(1)} collective-permute-done((bf16[4,96,896]{2,1,0:T(8,128)(2,1)S(1)}, bf16[4,96,896]{2,1,0:T(8,128)(2,1)S(1)}, u32[]{:S(2)}, u32[]{:S(2)}) %collective-permute-start.8) | collective-permute-done | bytes 688160 | tf_op jit(solution)/shard_map/ppermute | solution.py:21
  100.2 0.8 copy-done.6
  101.0 1.4 collective-permute-start.9
  102.4 2.2 collective-permute-start.11
  104.6 28.2 %collective-permute-done.9.refs_1_ = bf16[4,96,896]{2,1,0:T(8,128)(2,1)S(1)} collective-permute-done((bf16[4,96,896]{2,1,0:T(8,128)(2,1)S(1)}, bf16[4,96,896]{2,1,0:T(8,128)(2,1)S(1)}, u32[]{:S(2)}, u32[]{:S(2)}) %collective-permute-start.9) | collective-permute-done | bytes 688160 | tf_op jit(solution)/shard_map/ppermute | solution.py:21
  133.5 0.8 collective-permute-start.10
  135.1 2.8 collective-permute-start.12
  137.9 1.1 copy-done.5
  139.0 1.1 copy-done.7
  140.1 7.1 %outer_first.1.refs_3_ = f32[512,896]{1,0:T(8,128)S(1)} custom-call(bf16[4,8,96,512]{3,2,1,0:T(8,128)(2,1)} %bitcast.28, bf16[4,96,896]{2,1,0:T(8,128)(2,1)S(1)} %all-to-all-done.1.refs_1_, bf16[4,96,896]{2,1,0:T(8,128)(2,1)S(1)} %collective-permute-done.5.refs_2_, bf16[4,96,896]{2,1,0:T(8,128)(2,1)S(1)} %collective-permute-done.6.refs_3_, ...), custom_call_target="tpu_custom_call" | custom-call | flops 1761607680 | bytes 7241728 | tf_op jit(solution)/shard_map/outer_first/pallas_call | solution.py:233
  147.2 3.6 %outer_next.1.refs_3_ = f32[512,896]{1,0:T(8,128)S(1)} custom-call(bf16[4,8,96,512]{3,2,1,0:T(8,128)(2,1)} %bitcast.29, bf16[4,96,896]{2,1,0:T(8,128)(2,1)S(1)} %collective-permute-done.9.refs_1_, bf16[4,96,896]{2,1,0:T(8,128)(2,1)S(1)} %collective-permute-done.11.refs_2_, f32[512,896]{1,0:T(8,128)S(1)} %outer_first.1.refs_3_), custom_call_target="tpu_custom_call", output_to_operand_aliasing={{}: (3, {})} | custom-call | flops 704643072 | bytes 3997696 | tf_op jit(solution)/shard_map/outer_next/pallas_call | solution.py:233
  150.9 2.7 outer_last.1
  153.7 30.7 %all_to_all.25.n_ref = f32[256,1,128]{2,1,0:T(1,128)S(1)} all-to-all(f32[256,1,128]{2,1,0:T(1,128)S(1)} %get-tuple-element.46), channel_id=1, replica_groups=mesh['y'=4,'k'=2,'r'=4,'q'=2,'x'=4] {'y','k','r','q','x'}, dimensions={0} | all-to-all | bytes 262144 | tf_op jit(solution)/shard_map/all_to_all | solution.py:76
  184.4 4.3 %update_of.1 = (f32[512,896]{1,0:T(8,128)S(1)}, bf16[512,896]{1,0:T(8,128)(2,1)}, bf16[512,896]{1,0:T(8,128)(2,1)}, f32[32,2,128]{2,1,0:T(2,128)S(1)}) custom-call(f32[256,1,128]{2,1,0:T(1,128)S(1)} %all_to_all.25.n_ref, f32[512,896]{1,0:T(8,128)S(1)} %get-tuple-element.47.g_ref, f32[512,896]{1,0:T(8,128)S(1)} %bitcast.21, bf16[512,896]{1,0:T(8,128)(2,1)S(1)} %bitcast.24, ...), custom_call_target="tpu_custom_call" | custom-call | tf_op jit(solution)/shard_map/update_of/pallas_call | solution.py:113
  188.7 12.0 %all_to_all.26.sums_ref = f32[32,2,128]{2,1,0:T(2,128)S(1)} all-to-all(f32[32,2,128]{2,1,0:T(2,128)S(1)} %get-tuple-element.48), channel_id=1, replica_groups=mesh['y'=4,'k'=2,'r'=4,'q'=2,'x'=4] {'r','q','x'}, dimensions={0} | all-to-all | bytes 65536 | tf_op jit(solution)/shard_map/all_to_all | solution.py:76
  200.7 2.1 weights_of.1
  203.3 3.1 %collective-permute-start.15 = (bf16[256,896]{1,0:T(8,128)(2,1)S(1)}, bf16[256,896]{1,0:T(8,128)(2,1)S(1)}, u32[]{:S(2)}, u32[]{:S(2)}) collective-permute-start(bf16[256,896]{1,0:T(8,128)(2,1)S(1)} %get-tuple-element.55.refs_2_), channel_id=1, source_target_pairs={{0,24},{4,28},{8,0},{12,4},{16,8},{20,12},{24,16},{28,20},{1,25},{... | collective-permute-start | bytes 1376264 | tf_op jit(solution)/shard_map/ppermute | solution.py:21
  206.4 3.6 %collective-permute-start.18 = (bf16[256,896]{1,0:T(8,128)(2,1)S(1)}, bf16[256,896]{1,0:T(8,128)(2,1)S(1)}, u32[]{:S(2)}, u32[]{:S(2)}) collective-permute-start(bf16[256,896]{1,0:T(8,128)(2,1)S(1)} %get-tuple-element.54.refs_1_), channel_id=1, source_target_pairs={{0,24},{4,28},{8,0},{12,4},{16,8},{20,12},{24,16},{28,20},{1,25},{... | collective-permute-start | bytes 1376264 | tf_op jit(solution)/shard_map/ppermute | solution.py:21
  210.0 10.8 %collective-permute-done.13.refs_1_ = bf16[256,896]{1,0:T(8,128)(2,1)S(1)} collective-permute-done((bf16[256,896]{1,0:T(8,128)(2,1)S(1)}, bf16[256,896]{1,0:T(8,128)(2,1)S(1)}, u32[]{:S(2)}, u32[]{:S(2)}) %collective-permute-start.13) | collective-permute-done | bytes 458784 | tf_op jit(solution)/shard_map/ppermute | solution.py:21
  220.7 15.8 %collective-permute-done.15.refs_4_ = bf16[256,896]{1,0:T(8,128)(2,1)S(1)} collective-permute-done((bf16[256,896]{1,0:T(8,128)(2,1)S(1)}, bf16[256,896]{1,0:T(8,128)(2,1)S(1)}, u32[]{:S(2)}, u32[]{:S(2)}) %collective-permute-start.15) | collective-permute-done | bytes 458784 | tf_op jit(solution)/shard_map/ppermute | solution.py:21
  236.5 3.5 %collective-permute-start.16 = (bf16[256,896]{1,0:T(8,128)(2,1)S(1)}, bf16[256,896]{1,0:T(8,128)(2,1)}, u32[]{:S(2)}, u32[]{:S(2)}) collective-permute-start(bf16[256,896]{1,0:T(8,128)(2,1)S(1)} %collective-permute-done.15.refs_4_), channel_id=1, source_target_pairs={{0,24},{4,28},{8,0},{12,4},{16,8},{20,12},{24,16},{28,20},{1,25},{... | collective-permute-start | bytes 1376264 | tf_op jit(solution)/shard_map/ppermute | solution.py:21
  240.0 3.2 %project_first.1.refs_5_ = f32[768,896]{1,0:T(8,128)S(1)} custom-call(bf16[8,96,2048]{2,1,0:T(8,128)(2,1)} %all-gather.7.cloned.1.call-done.refs_0_, bf16[256,896]{1,0:T(8,128)(2,1)S(1)} %get-tuple-element.54.refs_1_, bf16[256,896]{1,0:T(8,128)(2,1)S(1)} %get-tuple-element.55.refs_2_), custom_call_target="tpu_custom_call" | custom-call | flops 704643072 | bytes 1703936 | tf_op jit(solution)/shard_map/project_first/pallas_call | solution.py:306
  243.2 8.8 %collective-permute-done.18.refs_3_ = bf16[256,896]{1,0:T(8,128)(2,1)S(1)} collective-permute-done((bf16[256,896]{1,0:T(8,128)(2,1)S(1)}, bf16[256,896]{1,0:T(8,128)(2,1)S(1)}, u32[]{:S(2)}, u32[]{:S(2)}) %collective-permute-start.18) | collective-permute-done | bytes 458784 | tf_op jit(solution)/shard_map/ppermute | solution.py:21
  252.1 5.0 %project_next.1.refs_3_ = f32[768,896]{1,0:T(8,128)S(1)} custom-call(bf16[8,96,2048]{2,1,0:T(8,128)(2,1)} %all-gather.7.cloned.1.call-done.refs_0_, bf16[256,896]{1,0:T(8,128)(2,1)S(1)} %collective-permute-done.13.refs_1_, bf16[256,896]{1,0:T(8,128)(2,1)S(1)} %collective-permute-done.17.refs_2_, bf16[256,896]{1,0:T(8,128)(2,1)S(1)} %collective-permute-done.18.refs_3_, ...), custom_call_target="tpu_custom_call" | custom-call | flops 1409286144 | bytes 3407872 | tf_op jit(solution)/shard_map/project_next/pallas_call | solution.py:306
  257.6 7.1 %collective-permute-done.16.refs_2_ = bf16[256,896]{1,0:T(8,128)(2,1)} collective-permute-done((bf16[256,896]{1,0:T(8,128)(2,1)S(1)}, bf16[256,896]{1,0:T(8,128)(2,1)}, u32[]{:S(2)}, u32[]{:S(2)}) %collective-permute-start.16) | collective-permute-done | bytes 458784 | tf_op jit(solution)/shard_map/ppermute | solution.py:21
  264.7 3.0 %project_last.1 = bf16[8,96,896]{2,1,0:T(8,128)(2,1)S(1)} custom-call(bf16[8,96,2048]{2,1,0:T(8,128)(2,1)} %all-gather.7.cloned.1.call-done.refs_0_, bf16[256,896]{1,0:T(8,128)(2,1)S(1)} %collective-permute-done.14.refs_1_, bf16[256,896]{1,0:T(8,128)(2,1)} %collective-permute-done.16.refs_2_, f32[768,896]{1,0:T(8,128)S(1)} %project_next.1.refs_3_), custom_call_target="tpu_custom_call" | custom-call | flops 704643072 | bytes 1703936 | tf_op jit(solution)/shard_map/project_last/pallas_call | solution.py:306
  267.7 23.4 %all_to_all.27.found_ref = bf16[8,96,896]{2,1,0:T(8,128)(2,1)S(1)} all-to-all(bf16[8,96,896]{2,1,0:T(8,128)(2,1)S(1)} %project_last.1), channel_id=1, replica_groups=mesh['y'=4,'k'=2,'r'=4,'q'=2,'x'=4] {'x','q'}, dimensions={0} | all-to-all | bytes 2752512 | tf_op jit(solution)/shard_map/all_to_all | solution.py:76
  291.1 1.2 assemble.1
  (41 shorter events, 3.9 us)
Async XLA Ops:
  7.8 1.3 copy-start.1
  9.2 1.0 copy-start.8
  10.1 6.1 %copy-start.9 = (bf16[1,1,96,2048]{3,2,1,0:T(8,128)(2,1)S(1)}, bf16[1,1,96,2048]{3,2,1,0:T(8,128)(2,1)}, u32[]{:S(2)}) copy-start(bf16[1,1,96,2048]{3,2,1,0:T(8,128)(2,1)} %param.9) | copy-start | bytes 1179652
  11.4 27.1 %all-to-all-start = ((bf16[4,96,896]{2,1,0:T(8,128)(2,1)}), bf16[4,96,896]{2,1,0:T(8,128)(2,1)S(1)}, u32[]{:S(2)}, u32[]{:S(2)}) async-start(bf16[4,96,896]{2,1,0:T(8,128)(2,1)} %get-tuple-element.30), calls=%async_computation | async-start | bytes 1376256 | tf_op jit(solution)/shard_map/all_to_all | solution.py:76
  16.3 121.6 %all-gather.5.cloned.1.call-start = ((), (), s32[]{:S(2)}) async-start(), calls=%async_computation.5 | async-start | bytes 3932160 | tf_op jit(solution)/shard_map/all_gather | solution.py:374
  16.3 22.2 %collective-permute-start.3 = (bf16[96,2048]{1,0:T(8,128)(2,1)S(1)}, bf16[96,2048]{1,0:T(8,128)(2,1)S(1)}, u32[]{:S(2)}, u32[]{:S(2)}) collective-permute-start(bf16[96,2048]{1,0:T(8,128)(2,1)S(1)} %bitcast.32), channel_id=1, source_target_pairs={{0,4},{4,0},{1,5},{5,1},{2,6},{6,2},{3,7},{7,3},{8,12},{12,8},{9,1... | collective-permute-start | bytes 1179656 | tf_op jit(solution)/shard_map/ppermute | solution.py:358
  18.0 17.2 %collective-permute-start = (bf16[96,512]{1,0:T(8,128)(2,1)S(1)}, bf16[96,512]{1,0:T(8,128)(2,1)S(1)}, u32[]{:S(2)}, u32[]{:S(2)}) collective-permute-start(bf16[96,512]{1,0:T(8,128)(2,1)S(1)} %get-tuple-element.32), channel_id=1, source_target_pairs={{0,8},{4,12},{8,16},{12,20},{16,24},{20,28},{24,0},{28,4},{1,9},{5... | collective-permute-start | bytes 294920 | tf_op jit(solution)/shard_map/ppermute | solution.py:21
  21.0 14.3 %collective-permute-start.1 = (bf16[96,512]{1,0:T(8,128)(2,1)S(1)}, bf16[96,512]{1,0:T(8,128)(2,1)S(1)}, u32[]{:S(2)}, u32[]{:S(2)}) collective-permute-start(bf16[96,512]{1,0:T(8,128)(2,1)S(1)} %get-tuple-element.33), channel_id=1, source_target_pairs={{0,24},{4,28},{8,0},{12,4},{16,8},{20,12},{24,16},{28,20},{1,25},{... | collective-permute-start | bytes 294920 | tf_op jit(solution)/shard_map/ppermute | solution.py:21
  23.1 15.3 %collective-permute-start.2 = (bf16[96,512]{1,0:T(8,128)(2,1)S(1)}, bf16[96,512]{1,0:T(8,128)(2,1)S(1)}, u32[]{:S(2)}, u32[]{:S(2)}) collective-permute-start(bf16[96,512]{1,0:T(8,128)(2,1)S(1)} %get-tuple-element.34), channel_id=1, source_target_pairs={{0,16},{4,20},{8,24},{12,28},{16,0},{20,4},{24,8},{28,12},{1,17},{... | collective-permute-start | bytes 294920 | tf_op jit(solution)/shard_map/ppermute | solution.py:21
  38.5 0.7 copy-start.10
  39.2 23.0 %collective-permute-start.5 = (bf16[4,96,896]{2,1,0:T(8,128)(2,1)S(1)}, bf16[4,96,896]{2,1,0:T(8,128)(2,1)S(1)}, u32[]{:S(2)}, u32[]{:S(2)}) collective-permute-start(bf16[4,96,896]{2,1,0:T(8,128)(2,1)S(1)} %all-to-all-done), channel_id=1, source_target_pairs={{0,4},{4,8},{8,12},{12,16},{16,20},{20,24},{24,28},{28,0},{1,5},{5... | collective-permute-start | bytes 2064392 | tf_op jit(solution)/shard_map/ppermute | solution.py:21
  39.8 22.5 %collective-permute-start.6 = (bf16[4,96,896]{2,1,0:T(8,128)(2,1)S(1)}, bf16[4,96,896]{2,1,0:T(8,128)(2,1)S(1)}, u32[]{:S(2)}, u32[]{:S(2)}) collective-permute-start(bf16[4,96,896]{2,1,0:T(8,128)(2,1)S(1)} %all-to-all-done), channel_id=1, source_target_pairs={{0,28},{4,0},{8,4},{12,8},{16,12},{20,16},{24,20},{28,24},{1,29},{... | collective-permute-start | bytes 2064392 | tf_op jit(solution)/shard_map/ppermute | solution.py:21
  41.9 20.3 %collective-permute-start.4 = (bf16[4,96,512]{2,1,0:T(8,128)(2,1)S(1)}, bf16[4,96,512]{2,1,0:T(8,128)(2,1)S(1)}, u32[]{:S(2)}, u32[]{:S(2)}) collective-permute-start(bf16[4,96,512]{2,1,0:T(8,128)(2,1)S(1)} %pad_maximum_fusion.2), channel_id=1, source_target_pairs={{0,4},{4,0},{1,5},{5,1},{2,6},{6,2},{3,7},{7,3},{8,12},{12,8},{9,1... | collective-permute-start | bytes 1179656 | tf_op jit(solution)/shard_map/ppermute | solution.py:360
  63.2 26.5 %collective-permute-start.7 = (bf16[4,96,896]{2,1,0:T(8,128)(2,1)S(1)}, bf16[4,96,896]{2,1,0:T(8,128)(2,1)S(1)}, u32[]{:S(2)}, u32[]{:S(2)}) collective-permute-start(bf16[4,96,896]{2,1,0:T(8,128)(2,1)S(1)} %collective-permute-done.5.refs_2_), channel_id=1, source_target_pairs={{0,8},{4,12},{8,16},{12,20},{16,24},{20,28},{24,0},{28,4},{1,9},{5... | collective-permute-start | bytes 2064392 | tf_op jit(solution)/shard_map/ppermute | solution.py:21
  67.1 33.1 %collective-permute-start.8 = (bf16[4,96,896]{2,1,0:T(8,128)(2,1)S(1)}, bf16[4,96,896]{2,1,0:T(8,128)(2,1)S(1)}, u32[]{:S(2)}, u32[]{:S(2)}) collective-permute-start(bf16[4,96,896]{2,1,0:T(8,128)(2,1)S(1)} %collective-permute-done.6.refs_3_), channel_id=1, source_target_pairs={{0,24},{4,28},{8,0},{12,4},{16,8},{20,12},{24,16},{28,20},{1,25},{... | collective-permute-start | bytes 2064392 | tf_op jit(solution)/shard_map/ppermute | solution.py:21
  67.1 11.7 %all-to-all-start.1 = ((bf16[4,96,896]{2,1,0:T(8,128)(2,1)}), bf16[4,96,896]{2,1,0:T(8,128)(2,1)S(1)}, u32[]{:S(2)}, u32[]{:S(2)}) async-start(bf16[4,96,896]{2,1,0:T(8,128)(2,1)} %get-tuple-element.39), calls=%async_computation.1 | async-start | bytes 1376256 | tf_op jit(solution)/shard_map/all_to_all | solution.py:76
  70.6 169.4 %all-gather.7.cloned.1.call-start = ((), (), s32[]{:S(2)}) async-start(), calls=%async_computation.6 | async-start | bytes 3932160 | tf_op jit(solution)/shard_map/all_gather | solution.py:380
  89.8 0.8 copy-start.4
  100.2 0.8 copy-start.6
  101.0 31.8 %collective-permute-start.9 = (bf16[4,96,896]{2,1,0:T(8,128)(2,1)S(1)}, bf16[4,96,896]{2,1,0:T(8,128)(2,1)S(1)}, u32[]{:S(2)}, u32[]{:S(2)}) collective-permute-start(bf16[4,96,896]{2,1,0:T(8,128)(2,1)S(1)} %all-to-all-done.1.refs_1_), channel_id=1, source_target_pairs={{0,8},{4,12},{8,16},{12,20},{16,24},{20,28},{24,0},{28,4},{1,9},{5... | collective-permute-start | bytes 2064392 | tf_op jit(solution)/shard_map/ppermute | solution.py:21
  102.4 32.0 %collective-permute-start.11 = (bf16[4,96,896]{2,1,0:T(8,128)(2,1)S(1)}, bf16[4,96,896]{2,1,0:T(8,128)(2,1)S(1)}, u32[]{:S(2)}, u32[]{:S(2)}) collective-permute-start(bf16[4,96,896]{2,1,0:T(8,128)(2,1)S(1)} %all-to-all-done.1.refs_1_), channel_id=1, source_target_pairs={{0,24},{4,28},{8,0},{12,4},{16,8},{20,12},{24,16},{28,20},{1,25},{... | collective-permute-start | bytes 2064392 | tf_op jit(solution)/shard_map/ppermute | solution.py:21
  133.5 17.4 %collective-permute-start.10 = (bf16[2,96,896]{2,1,0:T(8,128)(2,1)}, bf16[2,96,896]{2,1,0:T(8,128)(2,1)}, u32[]{:S(2)}, u32[]{:S(2)}) collective-permute-start(bf16[2,96,896]{2,1,0:T(8,128)(2,1)} %slice.8), channel_id=1, source_target_pairs={{0,8},{4,12},{8,16},{12,20},{16,24},{20,28},{24,0},{28,4},{1,9},{5... | collective-permute-start | bytes 1032200 | tf_op jit(solution)/shard_map/ppermute | solution.py:21
  135.1 15.8 %collective-permute-start.12 = (bf16[2,96,896]{2,1,0:T(8,128)(2,1)}, bf16[2,96,896]{2,1,0:T(8,128)(2,1)}, u32[]{:S(2)}, u32[]{:S(2)}) collective-permute-start(bf16[2,96,896]{2,1,0:T(8,128)(2,1)} %slice.9), channel_id=1, source_target_pairs={{0,24},{4,28},{8,0},{12,4},{16,8},{20,12},{24,16},{28,20},{1,25},{... | collective-permute-start | bytes 1032200 | tf_op jit(solution)/shard_map/ppermute | solution.py:21
  137.9 1.1 copy-start.5
  139.0 1.1 copy-start.7
  150.9 33.5 %copy-start = (f32[1,1,512,896]{3,2,1,0:T(8,128)S(1)}, f32[1,1,512,896]{3,2,1,0:T(8,128)}, u32[]{:S(2)}) copy-start(f32[1,1,512,896]{3,2,1,0:T(8,128)} %param.11) | copy-start | bytes 5505028
  150.9 33.5 %copy-start.2 = (bf16[1,1,512,896]{3,2,1,0:T(8,128)(2,1)S(1)}, bf16[1,1,512,896]{3,2,1,0:T(8,128)(2,1)}, u32[]{:S(2)}) copy-start(bf16[1,1,512,896]{3,2,1,0:T(8,128)(2,1)} %param.12) | copy-start | bytes 2752516
  150.9 33.5 %copy-start.3 = (bf16[1,1,512,896]{3,2,1,0:T(8,128)(2,1)S(1)}, bf16[1,1,512,896]{3,2,1,0:T(8,128)(2,1)}, u32[]{:S(2)}) copy-start(bf16[1,1,512,896]{3,2,1,0:T(8,128)(2,1)} %param.13) | copy-start | bytes 2752516
  202.8 17.9 %collective-permute-start.13 = (bf16[256,896]{1,0:T(8,128)(2,1)S(1)}, bf16[256,896]{1,0:T(8,128)(2,1)S(1)}, u32[]{:S(2)}, u32[]{:S(2)}) collective-permute-start(bf16[256,896]{1,0:T(8,128)(2,1)S(1)} %get-tuple-element.54.refs_1_), channel_id=1, source_target_pairs={{0,8},{4,12},{8,16},{12,20},{16,24},{20,28},{24,0},{28,4},{1,9},{5... | collective-permute-start | bytes 1376264 | tf_op jit(solution)/shard_map/ppermute | solution.py:21
  203.3 33.2 %collective-permute-start.15 = (bf16[256,896]{1,0:T(8,128)(2,1)S(1)}, bf16[256,896]{1,0:T(8,128)(2,1)S(1)}, u32[]{:S(2)}, u32[]{:S(2)}) collective-permute-start(bf16[256,896]{1,0:T(8,128)(2,1)S(1)} %get-tuple-element.55.refs_2_), channel_id=1, source_target_pairs={{0,24},{4,28},{8,0},{12,4},{16,8},{20,12},{24,16},{28,20},{1,25},{... | collective-permute-start | bytes 1376264 | tf_op jit(solution)/shard_map/ppermute | solution.py:21
  206.4 36.8 %collective-permute-start.17 = (bf16[256,896]{1,0:T(8,128)(2,1)S(1)}, bf16[256,896]{1,0:T(8,128)(2,1)S(1)}, u32[]{:S(2)}, u32[]{:S(2)}) collective-permute-start(bf16[256,896]{1,0:T(8,128)(2,1)S(1)} %get-tuple-element.55.refs_2_), channel_id=1, source_target_pairs={{0,8},{4,12},{8,16},{12,20},{16,24},{20,28},{24,0},{28,4},{1,9},{5... | collective-permute-start | bytes 1376264 | tf_op jit(solution)/shard_map/ppermute | solution.py:21
  206.4 45.7 %collective-permute-start.18 = (bf16[256,896]{1,0:T(8,128)(2,1)S(1)}, bf16[256,896]{1,0:T(8,128)(2,1)S(1)}, u32[]{:S(2)}, u32[]{:S(2)}) collective-permute-start(bf16[256,896]{1,0:T(8,128)(2,1)S(1)} %get-tuple-element.54.refs_1_), channel_id=1, source_target_pairs={{0,24},{4,28},{8,0},{12,4},{16,8},{20,12},{24,16},{28,20},{1,25},{... | collective-permute-start | bytes 1376264 | tf_op jit(solution)/shard_map/ppermute | solution.py:21
  220.7 36.8 %collective-permute-start.14 = (bf16[256,896]{1,0:T(8,128)(2,1)S(1)}, bf16[256,896]{1,0:T(8,128)(2,1)S(1)}, u32[]{:S(2)}, u32[]{:S(2)}) collective-permute-start(bf16[256,896]{1,0:T(8,128)(2,1)S(1)} %collective-permute-done.13.refs_1_), channel_id=1, source_target_pairs={{0,8},{4,12},{8,16},{12,20},{16,24},{20,28},{24,0},{28,4},{1,9},{5... | collective-permute-start | bytes 1376264 | tf_op jit(solution)/shard_map/ppermute | solution.py:21
  236.5 28.1 %collective-permute-start.16 = (bf16[256,896]{1,0:T(8,128)(2,1)S(1)}, bf16[256,896]{1,0:T(8,128)(2,1)}, u32[]{:S(2)}, u32[]{:S(2)}) collective-permute-start(bf16[256,896]{1,0:T(8,128)(2,1)S(1)} %collective-permute-done.15.refs_4_), channel_id=1, source_target_pairs={{0,24},{4,28},{8,0},{12,4},{16,8},{20,12},{24,16},{28,20},{1,25},{... | collective-permute-start | bytes 1376264 | tf_op jit(solution)/shard_map/ppermute | solution.py:21
Sparse Core Ops, SparseCore 0:
  63.3 46.4 all-gather.4
  112.2 42.2 all-gather.6

commit v6 on v5

--- a/solution.py
+++ b/solution.py
@@ -252,7 +252,8 @@
 
 
 def project(tokens, tiles, before=None, last=False):
-    shards, cap, d = tokens.shape
+    size_x, cap, d = tokens[0].shape
+    shards = 2 * size_x
     d_blk = d // GRID_R
     f_blk = tiles[0][1][0].shape[-1]
     flat = [part for _, piece in tiles for part in piece]
@@ -261,7 +262,7 @@
 
     def kernel(*refs):
         refs = list(refs)
-        tokens_ref = refs.pop(0)
+        tokens_refs = [refs.pop(0), refs.pop(0)]
         flat_refs = [refs.pop(0) for _ in flat]
         before_ref = None if before is None else refs.pop(0)
         out_ref, left, right, total, sems = refs
@@ -276,7 +277,9 @@
                 at += 1
             block = lax.rem(lax.axis_index("r") + away, GRID_R)
             columns = pl.ds(pl.multiple_of(block * d_blk, 128), d_blk)
-            copies.append((tokens_ref.at[:, :, columns], left.at[i]))
+            for q, tokens_ref in zip((lax.axis_index("q"), 1 - lax.axis_index("q")), tokens_refs):
+                there = left.at[i, pl.ds(q * size_x, size_x)]
+                copies.append((tokens_ref.at[:, :, columns], there))
         fetch(copies, sems)
         total[...] = jnp.zeros_like(total) if before is None else before_ref[...]
         half = shards // 2
@@ -301,18 +304,18 @@
         out_shape = jax.ShapeDtypeStruct((shards, cap, f_blk), jnp.bfloat16)
     else:
         out_shape = jax.ShapeDtypeStruct((count, f_blk), jnp.float32)
-    operands = [pltpu.with_memory_space_constraint(tokens, pltpu.HBM), *flat]
+    operands = [pltpu.with_memory_space_constraint(t, pltpu.HBM) for t in tokens] + flat
     operands += [] if before is None else [before]
     return pl.pallas_call(
         kernel,
-        in_specs=[ANYWHERE] * (1 + len(flat)) + [IN_VMEM] * (len(operands) - 1 - len(flat)),
+        in_specs=[ANYWHERE] * (2 + len(flat)) + [IN_VMEM] * (len(operands) - 2 - len(flat)),
         out_specs=IN_VMEM,
         out_shape=out_shape,
         scratch_shapes=[
             pltpu.VMEM((n, shards, cap, d_blk), jnp.bfloat16),
             pltpu.VMEM((n, d_blk, f_blk), jnp.bfloat16),
             pltpu.VMEM((count, f_blk), jnp.float32),
-            pltpu.SemaphoreType.DMA((len(flat) + n,)),
+            pltpu.SemaphoreType.DMA((len(flat) + 2 * n,)),
         ],
         cost_estimate=pl.CostEstimate(
             flops=2 * n * count * d_blk * f_blk,
@@ -329,7 +332,7 @@
 
     def kernel(found_ref, out_ref):
         for i in range(blocks):
-            start = (i % 2 * (blocks // 2) + i // 2) * f_blk
+            start = i * f_blk
             out_ref[:, start : start + f_blk] = found_ref[i]
 
     return pl.pallas_call(
@@ -374,10 +377,8 @@
     rows = lax.all_gather(jnp.concatenate([rows, beside]), "x")
     own = exchanged(own, "x")
     other_m3, other_p3 = shift(other_m1, 2), shift(other_p1, -2)
-    first = lax.axis_index("q") == 0
-    tokens = jnp.stack([jnp.where(first, mine, theirs), jnp.where(first, theirs, mine)])
-    own, other_m3, other_p3, tokens = lax.optimization_barrier((own, other_m3, other_p3, tokens))
-    tokens = lax.all_gather(tokens, "x").reshape(2 * size_x, cap, d)
+    own, other_m3, other_p3, theirs = lax.optimization_barrier((own, other_m3, other_p3, theirs))
+    theirs = lax.all_gather(theirs, "x")
     own_m2, own_p2 = shift(own, 2), shift(own, -2)
     pieces = {0: [own], -1: [other_m1], 1: [other_p1], -3: [other_m3], 3: [other_p3]}
     pieces |= {-2: [own_m2], 2: [own_p2]}
@@ -387,6 +388,9 @@
     (gradient,) = outer_sum(
         rows, [place_of[a] for a in first_away], [pieces[a] for a in first_away]
     )
+    mine, gradient, own_m2, own_p2 = lax.optimization_barrier((mine, gradient, own_m2, own_p2))
+    pieces |= {-2: [own_m2], 2: [own_p2]}
+    tokens = (lax.all_gather(mine, "x"), theirs)
     half = size_x // 2
     up, down = own_m2[:half], own_p2[half:]
     pieces[4] = [shift(up, 2), shift(down, -2)]
@@ -416,7 +420,7 @@
     part = project(tokens, [(0, [upper, lower])])
     part = project(tokens, [(3, [upper_m, lower_m]), (1, [upper_p, lower_p])], before=part)
     found = project(tokens, [(2, opposite)], before=part, last=True)
-    projected = assemble(exchanged(found, ("x", "q")))
+    projected = assemble(exchanged(found, ("q", "x")))
     return (
         weights_new[None, None],
         first_new[None, None],

time: 300 us -> 296 us (0.987)
  blocking collectives: 66.1 us -> 78.5 us
  waiting for transfers between devices: 129 us -> 119 us
  starting transfers between devices: 44 us -> 39.9 us
    all_to_all x3 -> x4, blocking collectives: 66.1 us -> 78.5 us  [exchanged(): return lax.all_to_all(values, axes, 0, 0, tiled=True)]
    ppermute x17, waiting for transfers between devices: 103 us -> 92.4 us  [shift(): return lax.ppermute(value, Z, [(i, (i + by) % size) for i in range(size)])]
    all_gather x1, waiting for transfers between devices: 0.01 us -> 6.23 us  [body(): rows = lax.all_gather(jnp.concatenate([rows, beside]), 'x')]
    all_to_all x2 -> x1, waiting for transfers between devices: 5.98 us -> 0.01 us  [exchanged(): return lax.all_to_all(values, axes, 0, 0, tiled=True)]
    all_to_all x2 -> x1, starting transfers between devices: 8.4 us -> 4.84 us  [exchanged(): return lax.all_to_all(values, axes, 0, 0, tiled=True)]
    unnamed x22 -> x28, local copies, waits for them, and re-layouts: 6.96 us -> 8.48 us
  transfers between devices with their start and end apart: 23 -> 23, of which waited for: 12 -> 15; matrix products, arithmetic and copies ran while one was open for 1% -> 0% of each run, Pallas kernels for 9% -> 9%
where the time goes in v6:
time: 296 us
  waiting for transfers between devices  119 us (40%)
  blocking collectives  78.5 us (27%)
  starting transfers between devices  39.9 us (13%)
  Pallas kernels  33.1 us (11%)
  between operations  14.5 us (5%)
  local copies, waits for them, and re-layouts  9.53 us (3%)
    ppermute x17, waiting for transfers between devices, shift(): return lax.ppermute(value, Z, [(i, (i + by) % size) for i in range(size)])  92.4 us
    all_to_all x4, blocking collectives, exchanged(): return lax.all_to_all(values, axes, 0, 0, tiled=True)  78.5 us
    ppermute x17, starting transfers between devices, shift(): return lax.ppermute(value, Z, [(i, (i + by) % size) for i in range(size)])  33.3 us
    ppermute x1, waiting for transfers between devices, body(): beside = lax.ppermute(rows, 'q', [(0, 1), (1, 0)])  20.2 us
    pallas_call x3, Pallas kernels, outer_sum(): pl.pallas_call(kernel, in_specs=in_specs, out_specs=[IN_VMEM] * len(out_s...  13.2 us
    pallas_call x3, Pallas kernels, project(): pl.pallas_call(kernel, in_specs=[ANYWHERE] * (2 + len(flat)) + [IN_VMEM]...  11.2 us
    unnamed x28, local copies, waits for them, and re-layouts  8.48 us
    all_gather x1, waiting for transfers between devices, body(): rows = lax.all_gather(jnp.concatenate([rows, beside]), 'x')  6.23 us
  transfers between devices with their start and end apart: 23, of which 15 were waited for; matrix products, arithmetic and copies ran while one was open for 0% of the time, Pallas kernels for 9%

profile of v6, /device:TPU:1, one launch (start us, length us, event | category | flops | bytes accessed | tf_op | source)
XLA Modules:
  0.0 295.6 jit_solution(7929264827549582519)
XLA Ops:
  7.8 1.3 copy-done.1
  10.2 1.0 split.1
  11.2 4.8 %all-to-all-start = ((bf16[4,96,896]{2,1,0:T(8,128)(2,1)}), bf16[4,96,896]{2,1,0:T(8,128)(2,1)S(1)}, u32[]{:S(2)}, u32[]{:S(2)}) async-start(bf16[4,96,896]{2,1,0:T(8,128)(2,1)} %get-tuple-element.34), calls=%async_computation | async-start | bytes 1376256 | tf_op jit(solution)/shard_map/all_to_all | solution.py:76
  16.0 1.7 collective-permute-start.3
  17.7 3.0 %collective-permute-start = (bf16[96,512]{1,0:T(8,128)(2,1)S(1)}, bf16[96,512]{1,0:T(8,128)(2,1)S(1)}, u32[]{:S(2)}, u32[]{:S(2)}) collective-permute-start(bf16[96,512]{1,0:T(8,128)(2,1)S(1)} %get-tuple-element.36), channel_id=1, source_target_pairs={{0,8},{4,12},{8,16},{12,20},{16,24},{20,28},{24,0},{28,4},{1,9},{5... | collective-permute-start | bytes 294920 | tf_op jit(solution)/shard_map/ppermute | solution.py:21
  20.7 2.1 collective-permute-start.1
  22.9 4.5 %collective-permute-start.2 = (bf16[96,512]{1,0:T(8,128)(2,1)S(1)}, bf16[96,512]{1,0:T(8,128)(2,1)S(1)}, u32[]{:S(2)}, u32[]{:S(2)}) collective-permute-start(bf16[96,512]{1,0:T(8,128)(2,1)S(1)} %get-tuple-element.38), channel_id=1, source_target_pairs={{0,16},{4,20},{8,24},{12,28},{16,0},{20,4},{24,8},{28,12},{1,17},{... | collective-permute-start | bytes 294920 | tf_op jit(solution)/shard_map/ppermute | solution.py:21
  27.3 7.7 %collective-permute-done = bf16[96,512]{1,0:T(8,128)(2,1)S(1)} collective-permute-done((bf16[96,512]{1,0:T(8,128)(2,1)S(1)}, bf16[96,512]{1,0:T(8,128)(2,1)S(1)}, u32[]{:S(2)}, u32[]{:S(2)}) %collective-permute-start) | collective-permute-done | bytes 98336 | tf_op jit(solution)/shard_map/ppermute | solution.py:21
  35.0 3.2 %collective-permute-done.2 = bf16[96,512]{1,0:T(8,128)(2,1)S(1)} collective-permute-done((bf16[96,512]{1,0:T(8,128)(2,1)S(1)}, bf16[96,512]{1,0:T(8,128)(2,1)S(1)}, u32[]{:S(2)}, u32[]{:S(2)}) %collective-permute-start.2) | collective-permute-done | bytes 98336 | tf_op jit(solution)/shard_map/ppermute | solution.py:21
  38.9 2.1 collective-permute-start.6
  41.0 20.2 %collective-permute-done.4 = bf16[4,96,512]{2,1,0:T(8,128)(2,1)S(1)} collective-permute-done((bf16[4,96,512]{2,1,0:T(8,128)(2,1)S(1)}, bf16[4,96,512]{2,1,0:T(8,128)(2,1)S(1)}, u32[]{:S(2)}, u32[]{:S(2)}) %collective-permute-start.4) | collective-permute-done | bytes 393248 | tf_op jit(solution)/shard_map/ppermute | solution.py:363
  61.2 1.0 pad_maximum_fusion
  62.3 3.9 %collective-permute-start.7 = (bf16[4,96,896]{2,1,0:T(8,128)(2,1)S(1)}, bf16[4,96,896]{2,1,0:T(8,128)(2,1)S(1)}, u32[]{:S(2)}, u32[]{:S(2)}) collective-permute-start(bf16[4,96,896]{2,1,0:T(8,128)(2,1)S(1)} %collective-permute-done.5.refs_2_), channel_id=1, source_target_pairs={{0,8},{4,12},{8,16},{12,20},{16,24},{20,28},{24,0},{28,4},{1,9},{5... | collective-permute-start | bytes 2064392 | tf_op jit(solution)/shard_map/ppermute | solution.py:21
  66.3 11.5 %all_to_all.25.refs_1_ = bf16[4,96,896]{2,1,0:T(8,128)(2,1)S(1)} all-to-all(bf16[4,96,896]{2,1,0:T(8,128)(2,1)S(1)} %get-tuple-element.43), channel_id=1, replica_groups=mesh['y'=4,'k'=2,'r'=4,'q'=2,'x'=4] {'x'}, dimensions={0} | all-to-all | bytes 1376256 | tf_op jit(solution)/shard_map/all_to_all | solution.py:76
  77.7 11.3 %collective-permute-done.7.refs_4_ = bf16[4,96,896]{2,1,0:T(8,128)(2,1)S(1)} collective-permute-done((bf16[4,96,896]{2,1,0:T(8,128)(2,1)S(1)}, bf16[4,96,896]{2,1,0:T(8,128)(2,1)S(1)}, u32[]{:S(2)}, u32[]{:S(2)}) %collective-permute-start.7) | collective-permute-done | bytes 688160 | tf_op jit(solution)/shard_map/ppermute | solution.py:21
  89.9 9.1 %collective-permute-done.8.refs_5_ = bf16[4,96,896]{2,1,0:T(8,128)(2,1)S(1)} collective-permute-done((bf16[4,96,896]{2,1,0:T(8,128)(2,1)S(1)}, bf16[4,96,896]{2,1,0:T(8,128)(2,1)S(1)}, u32[]{:S(2)}, u32[]{:S(2)}) %collective-permute-start.8) | collective-permute-done | bytes 688160 | tf_op jit(solution)/shard_map/ppermute | solution.py:21
  100.0 1.1 collective-permute-start.10
  101.1 1.3 collective-permute-start.9
  102.4 6.2 %all-gather.7.cloned.1.call-done = bf16[32,96,512]{2,1,0:T(8,128)(2,1)} async-done(((bf16[8,96,512]{2,1,0:T(8,128)(2,1)}), bf16[32,96,512]{2,1,0:T(8,128)(2,1)}) %all-gather.7.cloned.1.call-update) | async-done | bytes 3145744 | tf_op jit(solution)/shard_map/all_gather | solution.py:377
  108.6 1.1 copy-done.5
  109.7 1.1 copy-done.7
  110.8 1.1 copy-done.9
  111.9 1.1 copy-done.11
  113.0 7.1 %outer_first.1.refs_3_ = f32[512,896]{1,0:T(8,128)S(1)} custom-call(bf16[4,8,96,512]{3,2,1,0:T(8,128)(2,1)} %bitcast.24, bf16[4,96,896]{2,1,0:T(8,128)(2,1)S(1)} %all_to_all.25.refs_1_, bf16[4,96,896]{2,1,0:T(8,128)(2,1)S(1)} %copy-done.5, bf16[4,96,896]{2,1,0:T(8,128)(2,1)S(1)} %copy-done.7, bf16[4,96,896]{2,1,0:T(8,128)(2,1)S(1)} %copy-done.9, ...), custom_call_target="tpu_custom_call" | custom-call | flops 1761607680 | bytes 7241728 | tf_op jit(solution)/shard_map/outer_first/pallas_call | solution.py:233
  120.1 11.0 %collective-permute-done.10.refs_2_ = bf16[4,96,896]{2,1,0:T(8,128)(2,1)S(1)} collective-permute-done((bf16[4,96,896]{2,1,0:T(8,128)(2,1)S(1)}, bf16[4,96,896]{2,1,0:T(8,128)(2,1)S(1)}, u32[]{:S(2)}, u32[]{:S(2)}) %collective-permute-start.10) | collective-permute-done | bytes 688160 | tf_op jit(solution)/shard_map/ppermute | solution.py:21
  131.1 1.2 collective-permute-done.9.refs_1_
  132.3 1.0 slice.6
  133.3 2.4 collective-permute-start.11
  135.7 1.5 collective-permute-start.12
  137.3 3.5 %outer_next.1.refs_3_ = f32[512,896]{1,0:T(8,128)S(1)} custom-call(bf16[4,8,96,512]{3,2,1,0:T(8,128)(2,1)} %bitcast.25, bf16[4,96,896]{2,1,0:T(8,128)(2,1)} %collective-permute-done.9.refs_1_, bf16[4,96,896]{2,1,0:T(8,128)(2,1)S(1)} %collective-permute-done.10.refs_2_, f32[512,896]{1,0:T(8,128)S(1)} %outer_first.1.refs_3_), custom_call_target="tpu_custom_call", output_to_operand_aliasing={{}: (3, {})} | custom-call | flops 704643072 | bytes 3997696 | tf_op jit(solution)/shard_map/outer_next/pallas_call | solution.py:233
  140.8 5.6 %collective-permute-done.11.refs_1_ = bf16[2,96,896]{2,1,0:T(8,128)(2,1)S(1)} collective-permute-done((bf16[2,96,896]{2,1,0:T(8,128)(2,1)S(1)}, bf16[2,96,896]{2,1,0:T(8,128)(2,1)S(1)}, u32[]{:S(2)}, u32[]{:S(2)}) %collective-permute-start.11) | collective-permute-done | bytes 344096 | tf_op jit(solution)/shard_map/ppermute | solution.py:21
  146.8 2.6 outer_last.1
  149.5 32.1 %all_to_all.26.n_ref = f32[256,1,128]{2,1,0:T(1,128)S(1)} all-to-all(f32[256,1,128]{2,1,0:T(1,128)S(1)} %get-tuple-element.53), channel_id=1, replica_groups=mesh['y'=4,'k'=2,'r'=4,'q'=2,'x'=4] {'y','k','r','q','x'}, dimensions={0} | all-to-all | bytes 262144 | tf_op jit(solution)/shard_map/all_to_all | solution.py:76
  181.6 4.3 %update_of.1 = (f32[512,896]{1,0:T(8,128)S(1)}, bf16[512,896]{1,0:T(8,128)(2,1)}, bf16[512,896]{1,0:T(8,128)(2,1)}, f32[32,2,128]{2,1,0:T(2,128)S(1)}) custom-call(f32[256,1,128]{2,1,0:T(1,128)S(1)} %all_to_all.26.n_ref, f32[512,896]{1,0:T(8,128)S(1)} %get-tuple-element.54.g_ref, f32[512,896]{1,0:T(8,128)S(1)} %bitcast.17, bf16[512,896]{1,0:T(8,128)(2,1)S(1)} %bitcast.20, ...), custom_call_target="tpu_custom_call" | custom-call | tf_op jit(solution)/shard_map/update_of/pallas_call | solution.py:113
  185.9 12.0 %all_to_all.27.sums_ref = f32[32,2,128]{2,1,0:T(2,128)S(1)} all-to-all(f32[32,2,128]{2,1,0:T(2,128)S(1)} %get-tuple-element.55), channel_id=1, replica_groups=mesh['y'=4,'k'=2,'r'=4,'q'=2,'x'=4] {'r','q','x'}, dimensions={0} | all-to-all | bytes 65536 | tf_op jit(solution)/shard_map/all_to_all | solution.py:76
  197.9 2.1 weights_of.1
  200.5 3.1 %collective-permute-start.15 = (bf16[256,896]{1,0:T(8,128)(2,1)S(1)}, bf16[256,896]{1,0:T(8,128)(2,1)S(1)}, u32[]{:S(2)}, u32[]{:S(2)}) collective-permute-start(bf16[256,896]{1,0:T(8,128)(2,1)S(1)} %get-tuple-element.63.refs_3_), channel_id=1, source_target_pairs={{0,24},{4,28},{8,0},{12,4},{16,8},{20,12},{24,16},{28,20},{1,25},{... | collective-permute-start | bytes 1376264 | tf_op jit(solution)/shard_map/ppermute | solution.py:21
  203.6 3.6 %collective-permute-start.18 = (bf16[256,896]{1,0:T(8,128)(2,1)S(1)}, bf16[256,896]{1,0:T(8,128)(2,1)S(1)}, u32[]{:S(2)}, u32[]{:S(2)}) collective-permute-start(bf16[256,896]{1,0:T(8,128)(2,1)S(1)} %get-tuple-element.62.refs_2_), channel_id=1, source_target_pairs={{0,24},{4,28},{8,0},{12,4},{16,8},{20,12},{24,16},{28,20},{1,25},{... | collective-permute-start | bytes 1376264 | tf_op jit(solution)/shard_map/ppermute | solution.py:21
  207.1 10.8 %collective-permute-done.13.refs_2_ = bf16[256,896]{1,0:T(8,128)(2,1)S(1)} collective-permute-done((bf16[256,896]{1,0:T(8,128)(2,1)S(1)}, bf16[256,896]{1,0:T(8,128)(2,1)S(1)}, u32[]{:S(2)}, u32[]{:S(2)}) %collective-permute-start.13) | collective-permute-done | bytes 458784 | tf_op jit(solution)/shard_map/ppermute | solution.py:21
  217.9 15.8 %collective-permute-done.15.refs_5_ = bf16[256,896]{1,0:T(8,128)(2,1)S(1)} collective-permute-done((bf16[256,896]{1,0:T(8,128)(2,1)S(1)}, bf16[256,896]{1,0:T(8,128)(2,1)S(1)}, u32[]{:S(2)}, u32[]{:S(2)}) %collective-permute-start.15) | collective-permute-done | bytes 458784 | tf_op jit(solution)/shard_map/ppermute | solution.py:21
  233.7 3.5 %collective-permute-start.16 = (bf16[256,896]{1,0:T(8,128)(2,1)S(1)}, bf16[256,896]{1,0:T(8,128)(2,1)}, u32[]{:S(2)}, u32[]{:S(2)}) collective-permute-start(bf16[256,896]{1,0:T(8,128)(2,1)S(1)} %collective-permute-done.15.refs_5_), channel_id=1, source_target_pairs={{0,24},{4,28},{8,0},{12,4},{16,8},{20,12},{24,16},{28,20},{1,25},{... | collective-permute-start | bytes 1376264 | tf_op jit(solution)/shard_map/ppermute | solution.py:21
  237.2 3.2 %project_first.1.refs_6_ = f32[768,896]{1,0:T(8,128)S(1)} custom-call(bf16[4,96,2048]{2,1,0:T(8,128)(2,1)} %bitcast.30, bf16[4,96,2048]{2,1,0:T(8,128)(2,1)} %bitcast.27, bf16[256,896]{1,0:T(8,128)(2,1)S(1)} %get-tuple-element.62.refs_2_, bf16[256,896]{1,0:T(8,128)(2,1)S(1)} %get-tuple-element.63.refs_3_), custom_call_target="tpu_custom_call" | custom-call | flops 704643072 | bytes 1703936 | tf_op jit(solution)/shard_map/project_first/pallas_call | solution.py:309
  240.4 8.8 %collective-permute-done.18.refs_4_ = bf16[256,896]{1,0:T(8,128)(2,1)S(1)} collective-permute-done((bf16[256,896]{1,0:T(8,128)(2,1)S(1)}, bf16[256,896]{1,0:T(8,128)(2,1)S(1)}, u32[]{:S(2)}, u32[]{:S(2)}) %collective-permute-start.18) | collective-permute-done | bytes 458784 | tf_op jit(solution)/shard_map/ppermute | solution.py:21
  249.2 5.0 %project_next.1.refs_4_ = f32[768,896]{1,0:T(8,128)S(1)} custom-call(bf16[4,96,2048]{2,1,0:T(8,128)(2,1)} %bitcast.31, bf16[4,96,2048]{2,1,0:T(8,128)(2,1)} %bitcast.28, bf16[256,896]{1,0:T(8,128)(2,1)S(1)} %collective-permute-done.13.refs_2_, bf16[256,896]{1,0:T(8,128)(2,1)S(1)} %collective-permute-done.17.refs_3_, ...), custom_call_target="tpu_custom_call" | custom-call | flops 1409286144 | bytes 3407872 | tf_op jit(solution)/shard_map/project_next/pallas_call | solution.py:309
  254.7 7.1 %collective-permute-done.16.refs_3_ = bf16[256,896]{1,0:T(8,128)(2,1)} collective-permute-done((bf16[256,896]{1,0:T(8,128)(2,1)S(1)}, bf16[256,896]{1,0:T(8,128)(2,1)}, u32[]{:S(2)}, u32[]{:S(2)}) %collective-permute-start.16) | collective-permute-done | bytes 458784 | tf_op jit(solution)/shard_map/ppermute | solution.py:21
  261.8 3.0 %project_last.1 = bf16[8,96,896]{2,1,0:T(8,128)(2,1)S(1)} custom-call(bf16[4,96,2048]{2,1,0:T(8,128)(2,1)} %bitcast.32, bf16[4,96,2048]{2,1,0:T(8,128)(2,1)} %bitcast.29, bf16[256,896]{1,0:T(8,128)(2,1)S(1)} %collective-permute-done.14.refs_2_, bf16[256,896]{1,0:T(8,128)(2,1)} %collective-permute-done.16.refs_3_, f32[768,896]{1,0:T(8,128)S(1)} %project_next.1.refs_4_), custom_call_target="tpu_custom_call" | custom-call | flops 704643072 | bytes 1703936 | tf_op jit(solution)/shard_map/project_last/pallas_call | solution.py:309
  264.9 23.0 %all_to_all.28.found_ref = bf16[8,96,896]{2,1,0:T(8,128)(2,1)S(1)} all-to-all(bf16[8,96,896]{2,1,0:T(8,128)(2,1)S(1)} %project_last.1), channel_id=1, replica_groups=mesh['y'=4,'k'=2,'r'=4,'q'=2,'x'=4] {'q','x'}, dimensions={0} | all-to-all | bytes 2752512 | tf_op jit(solution)/shard_map/all_to_all | solution.py:76
  287.9 1.2 assemble.1
  (47 shorter events, 5.1 us)
Async XLA Ops:
  7.8 1.3 copy-start.1
  9.2 1.0 copy-start.12
  10.1 5.9 %copy-start.13 = (bf16[1,1,96,2048]{3,2,1,0:T(8,128)(2,1)S(1)}, bf16[1,1,96,2048]{3,2,1,0:T(8,128)(2,1)}, u32[]{:S(2)}) copy-start(bf16[1,1,96,2048]{3,2,1,0:T(8,128)(2,1)} %param.9) | copy-start | bytes 1179652
  11.2 27.0 %all-to-all-start = ((bf16[4,96,896]{2,1,0:T(8,128)(2,1)}), bf16[4,96,896]{2,1,0:T(8,128)(2,1)S(1)}, u32[]{:S(2)}, u32[]{:S(2)}) async-start(bf16[4,96,896]{2,1,0:T(8,128)(2,1)} %get-tuple-element.34), calls=%async_computation | async-start | bytes 1376256 | tf_op jit(solution)/shard_map/all_to_all | solution.py:76
  16.0 92.6 %all-gather.7.cloned.1.call-start = ((), (), s32[]{:S(2)}) async-start(), calls=%async_computation.5 | async-start | bytes 3932160 | tf_op jit(solution)/shard_map/all_gather | solution.py:377
  16.0 22.2 %collective-permute-start.3 = (bf16[96,2048]{1,0:T(8,128)(2,1)S(1)}, bf16[96,2048]{1,0:T(8,128)(2,1)}, u32[]{:S(2)}, u32[]{:S(2)}) collective-permute-start(bf16[96,2048]{1,0:T(8,128)(2,1)S(1)} %bitcast.35), channel_id=1, source_target_pairs={{0,4},{4,0},{1,5},{5,1},{2,6},{6,2},{3,7},{7,3},{8,12},{12,8},{9,1... | collective-permute-start | bytes 1179656 | tf_op jit(solution)/shard_map/ppermute | solution.py:361
  17.7 17.2 %collective-permute-start = (bf16[96,512]{1,0:T(8,128)(2,1)S(1)}, bf16[96,512]{1,0:T(8,128)(2,1)S(1)}, u32[]{:S(2)}, u32[]{:S(2)}) collective-permute-start(bf16[96,512]{1,0:T(8,128)(2,1)S(1)} %get-tuple-element.36), channel_id=1, source_target_pairs={{0,8},{4,12},{8,16},{12,20},{16,24},{20,28},{24,0},{28,4},{1,9},{5... | collective-permute-start | bytes 294920 | tf_op jit(solution)/shard_map/ppermute | solution.py:21
  20.7 14.3 %collective-permute-start.1 = (bf16[96,512]{1,0:T(8,128)(2,1)S(1)}, bf16[96,512]{1,0:T(8,128)(2,1)S(1)}, u32[]{:S(2)}, u32[]{:S(2)}) collective-permute-start(bf16[96,512]{1,0:T(8,128)(2,1)S(1)} %get-tuple-element.37), channel_id=1, source_target_pairs={{0,24},{4,28},{8,0},{12,4},{16,8},{20,12},{24,16},{28,20},{1,25},{... | collective-permute-start | bytes 294920 | tf_op jit(solution)/shard_map/ppermute | solution.py:21
  22.9 15.3 %collective-permute-start.2 = (bf16[96,512]{1,0:T(8,128)(2,1)S(1)}, bf16[96,512]{1,0:T(8,128)(2,1)S(1)}, u32[]{:S(2)}, u32[]{:S(2)}) collective-permute-start(bf16[96,512]{1,0:T(8,128)(2,1)S(1)} %get-tuple-element.38), channel_id=1, source_target_pairs={{0,16},{4,20},{8,24},{12,28},{16,0},{20,4},{24,8},{28,12},{1,17},{... | collective-permute-start | bytes 294920 | tf_op jit(solution)/shard_map/ppermute | solution.py:21
  38.2 23.0 %collective-permute-start.5 = (bf16[4,96,896]{2,1,0:T(8,128)(2,1)S(1)}, bf16[4,96,896]{2,1,0:T(8,128)(2,1)S(1)}, u32[]{:S(2)}, u32[]{:S(2)}) collective-permute-start(bf16[4,96,896]{2,1,0:T(8,128)(2,1)S(1)} %all-to-all-done), channel_id=1, source_target_pairs={{0,4},{4,8},{8,12},{12,16},{16,20},{20,24},{24,28},{28,0},{1,5},{5... | collective-permute-start | bytes 2064392 | tf_op jit(solution)/shard_map/ppermute | solution.py:21
  38.9 22.4 %collective-permute-start.6 = (bf16[4,96,896]{2,1,0:T(8,128)(2,1)S(1)}, bf16[4,96,896]{2,1,0:T(8,128)(2,1)S(1)}, u32[]{:S(2)}, u32[]{:S(2)}) collective-permute-start(bf16[4,96,896]{2,1,0:T(8,128)(2,1)S(1)} %all-to-all-done), channel_id=1, source_target_pairs={{0,28},{4,0},{8,4},{12,8},{16,12},{20,16},{24,20},{28,24},{1,29},{... | collective-permute-start | bytes 2064392 | tf_op jit(solution)/shard_map/ppermute | solution.py:21
  41.0 20.2 %collective-permute-start.4 = (bf16[4,96,512]{2,1,0:T(8,128)(2,1)S(1)}, bf16[4,96,512]{2,1,0:T(8,128)(2,1)S(1)}, u32[]{:S(2)}, u32[]{:S(2)}) collective-permute-start(bf16[4,96,512]{2,1,0:T(8,128)(2,1)S(1)} %pad_maximum_fusion.1), channel_id=1, source_target_pairs={{0,4},{4,0},{1,5},{5,1},{2,6},{6,2},{3,7},{7,3},{8,12},{12,8},{9,1... | collective-permute-start | bytes 1179656 | tf_op jit(solution)/shard_map/ppermute | solution.py:363
  61.2 16.5 %copy-start.4 = (bf16[4,96,896]{2,1,0:T(8,128)(2,1)}, bf16[4,96,896]{2,1,0:T(8,128)(2,1)S(1)}, u32[]{:S(2)}) copy-start(bf16[4,96,896]{2,1,0:T(8,128)(2,1)S(1)} %collective-permute-done.5.refs_2_) | copy-start | bytes 2064388
  61.2 16.5 %copy-start.6 = (bf16[4,96,896]{2,1,0:T(8,128)(2,1)}, bf16[4,96,896]{2,1,0:T(8,128)(2,1)S(1)}, u32[]{:S(2)}) copy-start(bf16[4,96,896]{2,1,0:T(8,128)(2,1)S(1)} %collective-permute-done.6.refs_3_) | copy-start | bytes 2064388
  62.3 174.9 %all-gather.11.cloned.1.call-start = ((), (), s32[]{:S(2)}) async-start(), calls=%async_computation.7 | async-start | bytes 1966080 | tf_op jit(solution)/shard_map/all_gather | solution.py:381
  62.3 26.7 %collective-permute-start.7 = (bf16[4,96,896]{2,1,0:T(8,128)(2,1)S(1)}, bf16[4,96,896]{2,1,0:T(8,128)(2,1)S(1)}, u32[]{:S(2)}, u32[]{:S(2)}) collective-permute-start(bf16[4,96,896]{2,1,0:T(8,128)(2,1)S(1)} %collective-permute-done.5.refs_2_), channel_id=1, source_target_pairs={{0,8},{4,12},{8,16},{12,20},{16,24},{20,28},{24,0},{28,4},{1,9},{5... | collective-permute-start | bytes 2064392 | tf_op jit(solution)/shard_map/ppermute | solution.py:21
  66.3 32.7 %collective-permute-start.8 = (bf16[4,96,896]{2,1,0:T(8,128)(2,1)S(1)}, bf16[4,96,896]{2,1,0:T(8,128)(2,1)S(1)}, u32[]{:S(2)}, u32[]{:S(2)}) collective-permute-start(bf16[4,96,896]{2,1,0:T(8,128)(2,1)S(1)} %collective-permute-done.6.refs_3_), channel_id=1, source_target_pairs={{0,24},{4,28},{8,0},{12,4},{16,8},{20,12},{24,16},{28,20},{1,25},{... | collective-permute-start | bytes 2064392 | tf_op jit(solution)/shard_map/ppermute | solution.py:21
  89.0 0.8 copy-start.8
  99.0 0.9 copy-start.10
  99.9 137.2 %all-gather.9.cloned.1.call-start = ((), (), s32[]{:S(2)}) async-start(), calls=%async_computation.6 | async-start | bytes 1966080 | tf_op jit(solution)/shard_map/all_gather | solution.py:393
  100.0 31.1 %collective-permute-start.10 = (bf16[4,96,896]{2,1,0:T(8,128)(2,1)S(1)}, bf16[4,96,896]{2,1,0:T(8,128)(2,1)S(1)}, u32[]{:S(2)}, u32[]{:S(2)}) collective-permute-start(bf16[4,96,896]{2,1,0:T(8,128)(2,1)S(1)} %all_to_all.25.refs_1_), channel_id=1, source_target_pairs={{0,24},{4,28},{8,0},{12,4},{16,8},{20,12},{24,16},{28,20},{1,25},{... | collective-permute-start | bytes 2064392 | tf_op jit(solution)/shard_map/ppermute | solution.py:21
  101.1 31.2 %collective-permute-start.9 = (bf16[4,96,896]{2,1,0:T(8,128)(2,1)S(1)}, bf16[4,96,896]{2,1,0:T(8,128)(2,1)}, u32[]{:S(2)}, u32[]{:S(2)}) collective-permute-start(bf16[4,96,896]{2,1,0:T(8,128)(2,1)S(1)} %all_to_all.25.refs_1_), channel_id=1, source_target_pairs={{0,8},{4,12},{8,16},{12,20},{16,24},{20,28},{24,0},{28,4},{1,9},{5... | collective-permute-start | bytes 2064392 | tf_op jit(solution)/shard_map/ppermute | solution.py:21
  108.6 1.1 copy-start.5
  109.7 1.1 copy-start.7
  110.8 1.1 copy-start.9
  111.9 1.1 copy-start.11
  133.3 13.0 %collective-permute-start.11 = (bf16[2,96,896]{2,1,0:T(8,128)(2,1)S(1)}, bf16[2,96,896]{2,1,0:T(8,128)(2,1)S(1)}, u32[]{:S(2)}, u32[]{:S(2)}) collective-permute-start(bf16[2,96,896]{2,1,0:T(8,128)(2,1)S(1)} %slice.6), channel_id=1, source_target_pairs={{0,8},{4,12},{8,16},{12,20},{16,24},{20,28},{24,0},{28,4},{1,9},{5... | collective-permute-start | bytes 1032200 | tf_op jit(solution)/shard_map/ppermute | solution.py:21
  135.7 11.1 %collective-permute-start.12 = (bf16[2,96,896]{2,1,0:T(8,128)(2,1)S(1)}, bf16[2,96,896]{2,1,0:T(8,128)(2,1)S(1)}, u32[]{:S(2)}, u32[]{:S(2)}) collective-permute-start(bf16[2,96,896]{2,1,0:T(8,128)(2,1)S(1)} %slice.7), channel_id=1, source_target_pairs={{0,24},{4,28},{8,0},{12,4},{16,8},{20,12},{24,16},{28,20},{1,25},{... | collective-permute-start | bytes 1032200 | tf_op jit(solution)/shard_map/ppermute | solution.py:21
  140.8 40.8 %copy-start = (f32[1,1,512,896]{3,2,1,0:T(8,128)S(1)}, f32[1,1,512,896]{3,2,1,0:T(8,128)}, u32[]{:S(2)}) copy-start(f32[1,1,512,896]{3,2,1,0:T(8,128)} %param.11) | copy-start | bytes 5505028
  140.8 40.8 %copy-start.2 = (bf16[1,1,512,896]{3,2,1,0:T(8,128)(2,1)S(1)}, bf16[1,1,512,896]{3,2,1,0:T(8,128)(2,1)}, u32[]{:S(2)}) copy-start(bf16[1,1,512,896]{3,2,1,0:T(8,128)(2,1)} %param.12) | copy-start | bytes 2752516
  140.8 40.8 %copy-start.3 = (bf16[1,1,512,896]{3,2,1,0:T(8,128)(2,1)S(1)}, bf16[1,1,512,896]{3,2,1,0:T(8,128)(2,1)}, u32[]{:S(2)}) copy-start(bf16[1,1,512,896]{3,2,1,0:T(8,128)(2,1)} %param.13) | copy-start | bytes 2752516
  200.0 17.9 %collective-permute-start.13 = (bf16[256,896]{1,0:T(8,128)(2,1)S(1)}, bf16[256,896]{1,0:T(8,128)(2,1)S(1)}, u32[]{:S(2)}, u32[]{:S(2)}) collective-permute-start(bf16[256,896]{1,0:T(8,128)(2,1)S(1)} %get-tuple-element.62.refs_2_), channel_id=1, source_target_pairs={{0,8},{4,12},{8,16},{12,20},{16,24},{20,28},{24,0},{28,4},{1,9},{5... | collective-permute-start | bytes 1376264 | tf_op jit(solution)/shard_map/ppermute | solution.py:21
  200.5 33.2 %collective-permute-start.15 = (bf16[256,896]{1,0:T(8,128)(2,1)S(1)}, bf16[256,896]{1,0:T(8,128)(2,1)S(1)}, u32[]{:S(2)}, u32[]{:S(2)}) collective-permute-start(bf16[256,896]{1,0:T(8,128)(2,1)S(1)} %get-tuple-element.63.refs_3_), channel_id=1, source_target_pairs={{0,24},{4,28},{8,0},{12,4},{16,8},{20,12},{24,16},{28,20},{1,25},{... | collective-permute-start | bytes 1376264 | tf_op jit(solution)/shard_map/ppermute | solution.py:21
  203.6 36.8 %collective-permute-start.17 = (bf16[256,896]{1,0:T(8,128)(2,1)S(1)}, bf16[256,896]{1,0:T(8,128)(2,1)S(1)}, u32[]{:S(2)}, u32[]{:S(2)}) collective-permute-start(bf16[256,896]{1,0:T(8,128)(2,1)S(1)} %get-tuple-element.63.refs_3_), channel_id=1, source_target_pairs={{0,8},{4,12},{8,16},{12,20},{16,24},{20,28},{24,0},{28,4},{1,9},{5... | collective-permute-start | bytes 1376264 | tf_op jit(solution)/shard_map/ppermute | solution.py:21
  203.6 45.7 %collective-permute-start.18 = (bf16[256,896]{1,0:T(8,128)(2,1)S(1)}, bf16[256,896]{1,0:T(8,128)(2,1)S(1)}, u32[]{:S(2)}, u32[]{:S(2)}) collective-permute-start(bf16[256,896]{1,0:T(8,128)(2,1)S(1)} %get-tuple-element.62.refs_2_), channel_id=1, source_target_pairs={{0,24},{4,28},{8,0},{12,4},{16,8},{20,12},{24,16},{28,20},{1,25},{... | collective-permute-start | bytes 1376264 | tf_op jit(solution)/shard_map/ppermute | solution.py:21
  217.9 36.8 %collective-permute-start.14 = (bf16[256,896]{1,0:T(8,128)(2,1)S(1)}, bf16[256,896]{1,0:T(8,128)(2,1)S(1)}, u32[]{:S(2)}, u32[]{:S(2)}) collective-permute-start(bf16[256,896]{1,0:T(8,128)(2,1)S(1)} %collective-permute-done.13.refs_2_), channel_id=1, source_target_pairs={{0,8},{4,12},{8,16},{12,20},{16,24},{20,28},{24,0},{28,4},{1,9},{5... | collective-permute-start | bytes 1376264 | tf_op jit(solution)/shard_map/ppermute | solution.py:21
  233.7 28.1 %collective-permute-start.16 = (bf16[256,896]{1,0:T(8,128)(2,1)S(1)}, bf16[256,896]{1,0:T(8,128)(2,1)}, u32[]{:S(2)}, u32[]{:S(2)}) collective-permute-start(bf16[256,896]{1,0:T(8,128)(2,1)S(1)} %collective-permute-done.15.refs_5_), channel_id=1, source_target_pairs={{0,24},{4,28},{8,0},{12,4},{16,8},{20,12},{24,16},{28,20},{1,25},{... | collective-permute-start | bytes 1376264 | tf_op jit(solution)/shard_map/ppermute | solution.py:21
Sparse Core Ops, SparseCore 0:
  62.4 46.1 all-gather.6
  110.4 31.0 all-gather.10
  143.4 29.2 all-gather.8
